TPU v7x, 256 devices: a whole 4x4x8 slice. The times are simulated.
256 devices in a mesh: samp: 64 (over z, x, core), snp: 4 (over y).
Axes of the slice: x: 4, y: 4, z: 8, core: 2. Of those that a mesh axis runs over, the one named last changes fastest.
Arguments:
- genotype: int32 [40960, 4096], P('samp', 'snp'), may hold values from 0 to 2
- freqs: float32 [4096], P('snp'), may hold values from 0.35 to 0.65
- left_factors: float32 [40960, 20], P('samp'), may hold values from -6 to 6
- singular: float32 [20], replicated, may hold values from 0.5 to 2
- right_factors: float32 [4096, 20], P(('snp', 'samp')), may hold values from -1.25 to 1.25
- sketch: bfloat16 [4096, 64], P('snp'), may hold values from -6 to 6
- batch_sizes: int32 [12], replicated, may hold values from 1 to 6826, 40960 in all
- missing_batch: int32 [48], replicated, may hold values from 0 to 11, as said below
- missing_block: int32 [48], replicated, may hold values from 0 to 15, as said below
Outputs:
- basis: float32 [40960, 64], P('samp')
- projection: float32 [4096, 64], P('snp')
- snp_basis: float32 [4096, 64], P('snp')
Inputs may be any that keep to these rules, and one draw needn't show every extreme that they name: The pairs (missing_batch, missing_block) are distinct; every block id appears exactly 3 times and every batch id exactly 48 // 12 times. `missing_block`: paired entry by entry with missing_batch.
All inputs are finite; a program needn't handle non-finite values.
Results may differ from a plain program's by a relative error of at most 0.012.
Values may be sent and summed in bfloat16 or wider, within the bound.
No kernel may reach another device: no remote copies, remote signals or barrier semaphores. Data moves between devices by JAX's collectives and lax.ppermute only.
A program may use at most 64 MiB of HBM per device.

v0:
```python
import math

import jax
import jax.numpy as jnp
from jax import lax
from jax.experimental import pallas as pl
from jax.experimental.pallas import tpu as pltpu
from jax.sharding import Mesh, PartitionSpec as P

BATCHES = 12
BLOCK = 256
ITERS = 2
BLOCKS = 16
LANES = 128
SUB = 8
GROUP = 32
F32 = jnp.float32
BF16 = jnp.bfloat16
HIGH = lax.Precision.HIGHEST


def exact_dot(a, b, a_dim, b_dim):
    return lax.dot_general(
        a, b, (((a_dim,), (b_dim,)), ((), ())), precision=HIGH, preferred_element_type=F32
    )


def split_dot(values, matrix, dim):
    high = values.astype(BF16)
    low = (values - high.astype(F32)).astype(BF16)
    both = jnp.concatenate([high, low], axis=0)
    out = lax.dot_general(
        both, matrix, (((1,), (dim,)), ((), ())), preferred_element_type=F32
    )
    rows = values.shape[0]
    return out[:rows] + out[rows:]


def inverse_factor(gram, lower):
    size = gram.shape[0]
    across = lax.broadcasted_iota(jnp.int32, (size, size), 1)
    down = lax.broadcasted_iota(jnp.int32, (size, size), 0)
    wide = jnp.concatenate([gram, (across == down).astype(F32)], axis=1)
    count = size // SUB
    shape = (SUB, 2 * size)
    tiles = [wide[SUB * t : SUB * (t + 1)] for t in range(count)]
    sub = lax.broadcasted_iota(jnp.int32, shape, 0)
    step = 1 if lower else -1
    for a in range(count)[::step]:
        active = range(a, count) if lower else range(a + 1)
        cols = {
            t: [
                jnp.broadcast_to(tiles[t][:, SUB * a + k : SUB * a + k + 1], shape)
                for k in range(SUB)
            ]
            for t in active
        }
        scale = jnp.zeros(shape, F32)
        for k in range(SUB)[::step]:
            pivot = jnp.broadcast_to(cols[a][k][k : k + 1], shape)
            inverse = 1.0 / pivot
            scale = jnp.where(sub == k, pivot, scale)
            keep = (sub > k) if lower else (sub < k)
            rest = range(k + 1, SUB) if lower else range(k)
            row = jnp.broadcast_to(tiles[a][k : k + 1], shape) * inverse
            heads = {j: jnp.broadcast_to(cols[a][j][k : k + 1], shape) * inverse for j in rest}
            for t in active:
                column = cols[t][k]
                if t == a:
                    column = jnp.where(keep, column, 0.0)
                tiles[t] = tiles[t] - column * row
                for j in rest:
                    cols[t][j] = cols[t][j] - column * heads[j]
        tiles[a] = tiles[a] * lax.rsqrt(scale)
    return jnp.concatenate(tiles, axis=0)[:, size:]


def kernel_call(body, out_shapes, *operands):
    return pl.pallas_call(
        body,
        out_shape=out_shapes,
        compiler_params=pltpu.CompilerParams(vmem_limit_bytes=48 * 1024 * 1024),
    )(*operands)


def shape_of(shape, dtype=F32):
    return jax.ShapeDtypeStruct(shape, dtype)


def write_send(columns, gram, core, mine, other):
    rows = columns.shape[0]
    blank = jnp.zeros((rows, LANES - gram.shape[1]), F32)
    value = jnp.concatenate([columns, gram, blank], axis=1)
    top, bottom = value[: rows // 2], value[rows // 2 :]
    mine[...] = jnp.where(core == 0, top, bottom)
    other[...] = jnp.where(core == 0, bottom, top)


def three_parts(value):
    high = value.astype(BF16)
    rest = value - high.astype(F32)
    middle = rest.astype(BF16)
    return [high, middle, (rest - middle.astype(F32)).astype(BF16)]


def solution(mesh):
    samp, snp = mesh.shape["samp"], mesh.shape["snp"]
    chips, ring = samp // 2, 4
    depth = chips // ring
    fine = Mesh(mesh.devices.reshape(depth, ring, 2, snp), ("z", "x", "core", "snp"))
    samp_axes = ("z", "x", "core")

    def swap(value):
        return lax.ppermute(value, "core", [(0, 1), (1, 0)])

    def snp_others(value):
        return [
            lax.ppermute(value, "snp", [(i, (i + k) % snp) for i in range(snp)])
            for k in range(1, snp)
        ]

    def x_shift(value, k):
        return lax.ppermute(value, "x", [(i, (i + k) % ring) for i in range(ring)])

    def on_device(
        genotype,
        freqs,
        left_factors,
        singular,
        right_factors,
        sketch,
        batch_sizes,
        missing_batch,
        missing_block,
    ):
        row_count, col_width = genotype.shape
        rank = left_factors.shape[1]
        width = sketch.shape[1]
        sample_count = row_count * samp
        snp_count = col_width * snp
        place = lax.axis_index((*samp_axes, "snp")).reshape(1).astype(jnp.int32)
        local_blocks = col_width // BLOCK
        omega = sketch.T

        def core_of(place):
            return place[0] // snp % 2

        def x_of(place):
            return place[0] // (snp * 2) % ring

        def call_with_place(body, outs, *operands, scalars=(), scratch=()):
            smem = pl.BlockSpec(memory_space=pltpu.SMEM)
            specs = [smem] * (1 + len(scalars)) + [
                pl.BlockSpec(memory_space=pltpu.VMEM) for _ in operands
            ]
            return pl.pallas_call(
                body,
                out_shape=outs,
                in_specs=specs,
                scratch_shapes=scratch,
                compiler_params=pltpu.CompilerParams(vmem_limit_bytes=48 * 1024 * 1024),
            )(place, *scalars, *operands)

        def batch_ids(place, sizes, shape, axis):
            ids = lax.broadcasted_iota(jnp.int32, shape, axis) + place[0] // snp * row_count
            batch = jnp.zeros(shape, jnp.int32)
            end = jnp.int32(0)
            for b in range(BATCHES - 1):
                end = end + sizes[b]
                batch = batch + (ids >= end).astype(jnp.int32)
            return batch

        def gone_in(bits, batch):
            return ((jnp.broadcast_to(bits, batch.shape) >> batch) & 1) == 1

        chunk = LANES

        def observe_kernel(
            place, sizes_in, batch_in, block_in, geno_in, freq_in, om_in,
            obs, start, bits,
            sizes, tile_batch, tile_block, geno, freq, om, sems,
        ):
            copies = [
                pltpu.make_async_copy(source, target, sems.at[i])
                for i, (source, target) in enumerate(
                    [
                        (batch_in, tile_batch),
                        (block_in, tile_block),
                        (sizes_in, sizes),
                        (freq_in, freq),
                    ]
                    + [
                        (geno_in.at[pl.ds(low, chunk)], geno.at[pl.ds(low, chunk)])
                        for low in range(0, row_count, chunk)
                    ]
                    + [(om_in, om)]
                )
            ]
            for copy in copies:
                copy.start()
            for block in range(BLOCKS):
                bits[block] = 0
            copies[0].wait()
            copies[1].wait()
            for i in range(tile_batch.shape[0]):
                block = tile_block[i]
                bits[block] = bits[block] | (1 << tile_batch[i])
            copies[2].wait()
            copies[3].wait()
            batch = batch_ids(place, sizes, (row_count, LANES), 0)
            own_bits = [bits[place[0] % snp * local_blocks + j] for j in range(local_blocks)]
            for n, top in enumerate(range(0, row_count, chunk)):
                copies[4 + n].wait()
                rows = slice(top, top + chunk)
                for j in range(local_blocks):
                    gone = gone_in(own_bits[j], batch[rows])
                    for low in range(BLOCK * j, BLOCK * (j + 1), LANES):
                        at = slice(low, low + LANES)
                        values = geno[rows, at].astype(F32) - 2.0 * freq[:, at]
                        obs[rows, at] = jnp.where(gone, 0.0, values).astype(BF16)
            copies[-1].wait()
            start[...] = lax.dot_general(
                om[...], obs[...], (((1,), (1,)), ((), ())), preferred_element_type=F32
            )

        vmem = pl.BlockSpec(memory_space=pltpu.VMEM)
        smem = pl.BlockSpec(memory_space=pltpu.SMEM)
        tiles = missing_batch.shape
        observed, start, bits = pl.pallas_call(
            observe_kernel,
            out_shape=(
                shape_of((row_count, col_width), BF16),
                shape_of((width, row_count)),
                shape_of((BLOCKS,), jnp.int32),
            ),
            in_specs=[smem] + [pl.BlockSpec(memory_space=pltpu.HBM)] * 6,
            out_specs=(vmem, vmem, smem),
            scratch_shapes=[
                pltpu.SMEM(batch_sizes.shape, jnp.int32),
                pltpu.SMEM(tiles, jnp.int32),
                pltpu.SMEM(tiles, jnp.int32),
                pltpu.VMEM((row_count, col_width), jnp.int32),
                pltpu.VMEM((1, col_width), F32),
                pltpu.VMEM((width, col_width), BF16),
                pltpu.SemaphoreType.DMA((5 + row_count // chunk,)),
            ],
            compiler_params=pltpu.CompilerParams(vmem_limit_bytes=63 * 1024 * 1024),
        )(
            place,
            batch_sizes,
            missing_batch,
            missing_block,
            genotype,
            freqs.reshape(1, col_width),
            omega,
        )

        def pack_kernel(place, bits, mine, other, spread):
            del bits
            first = core_of(place) == 0
            low = jnp.where(first, mine[...], other[...])
            high = jnp.where(first, other[...], mine[...])
            fill = jnp.zeros((SUB, GROUP - rank), F32)
            pieces = []
            for part in (low, high):
                for top in range(0, part.shape[0], SUB):
                    pieces += [part[top : top + SUB], fill]
            tile = jnp.concatenate(pieces, axis=1)
            spread[...] = jnp.broadcast_to(tile[None], spread.shape)

        right_tiles = lax.all_to_all(
            call_with_place(
                pack_kernel,
                shape_of((chips, SUB, LANES)),
                right_factors,
                swap(right_factors),
                scalars=(bits,),
            ),
            ("z", "x"),
            0,
            0,
        )
        start_others = snp_others(start)

        def right_rows(tiles):
            value = tiles[...]
            parts = [value[:, :, g : g + GROUP] for g in range(0, LANES, GROUP)]
            return jnp.stack(parts, axis=1).reshape(col_width, GROUP)

        def weight_rows(scale, left):
            rows = [left[r : r + 1, :] * scale[r] for r in range(rank)]
            return jnp.concatenate(
                [*rows, jnp.zeros((GROUP - rank, row_count), F32)], axis=0
            )

        def mix_kernel(place, tiles, om, mixed):
            right = right_rows(tiles)
            pieces = [
                exact_dot(
                    om[:, BLOCK * j : BLOCK * (j + 1)].astype(F32),
                    right[BLOCK * j : BLOCK * (j + 1)],
                    1,
                    0,
                )
                for j in range(local_blocks)
            ]
            mixed[...] = jnp.concatenate(pieces, axis=1)

        def build_kernel(place, sizes, bits, scale, obs, left, tiles, x_out):
            right = right_rows(tiles)
            weight = weight_rows(scale, left).T
            batch = batch_ids(place, sizes, (row_count, BLOCK), 0)
            for j in range(local_blocks):
                at = slice(BLOCK * j, BLOCK * (j + 1))
                lowrank = exact_dot(weight, right[at], 1, 1)
                gone = gone_in(bits[place[0] % snp * local_blocks + j], batch)
                x_out[:, at] = jnp.where(gone, lowrank, obs[:, at].astype(F32)).astype(BF16)

        mixed = call_with_place(
            mix_kernel,
            shape_of((width, local_blocks * GROUP)),
            right_tiles,
            omega,
        )
        mixed_others = snp_others(mixed)
        left_rows = left_factors.T
        matrix = call_with_place(
            build_kernel,
            shape_of((row_count, col_width), BF16),
            observed,
            left_rows,
            right_tiles,
            scalars=(batch_sizes, bits, singular),
        )

        packed = row_count + 3 * width
        sum_width = col_width + LANES
        part_shape = shape_of((width // 2, sum_width))
        tile_shape = shape_of((SUB, sum_width))

        def split_kernel(place, mine, got, own, *sends):
            for k, ref in enumerate((own, *sends)):
                rows = pl.ds(pl.multiple_of((x_of(place) + k) % ring * SUB, SUB), SUB)
                ref[...] = mine[rows, :] + got[rows, :]

        def spread_kernel(place, own, a, b, c, out):
            total = own[...] + a[...] + b[...] + c[...]
            if out.dtype == BF16:
                columns, gram = total[:, :col_width], total[:, col_width : col_width + width]
                total = jnp.concatenate(
                    [
                        columns.astype(BF16),
                        *three_parts(gram),
                        jnp.zeros((SUB, out.shape[2] - col_width - 3 * width), BF16),
                    ],
                    axis=1,
                )
            out[...] = jnp.broadcast_to(total[None], out.shape)

        def gather_kernel(place, parts, out):
            total = jnp.sum(parts[...].astype(F32), axis=0)
            if parts.dtype == BF16:
                grams = [
                    total[:, col_width + width * i : col_width + width * (i + 1)]
                    for i in range(3)
                ]
                total = jnp.concatenate(
                    [
                        total[:, :col_width],
                        grams[0] + (grams[1] + grams[2]),
                        jnp.zeros((SUB, LANES - width), F32),
                    ],
                    axis=1,
                )
            out[...] = jnp.broadcast_to(total[None], out.shape)

        def samp_sum(mine, other, dtype):
            own, *sends = call_with_place(
                split_kernel, (tile_shape,) * ring, mine, swap(other)
            )
            gots = [x_shift(send, k) for k, send in enumerate(sends, 1)]
            wide = sum_width if dtype == F32 else col_width + 2 * LANES
            spread = call_with_place(
                spread_kernel, shape_of((depth, SUB, wide), dtype), own, *gots
            )
            tiles = call_with_place(
                gather_kernel,
                shape_of((ring, *tile_shape.shape)),
                lax.all_to_all(spread, "z", 0, 0),
            )
            near = lax.all_to_all(tiles, "x", 0, 0)
            return [near, swap(near)]

        def read_sum(place, tiles, whole):
            half = width // 2
            for side, ref in zip((core_of(place), 1 - core_of(place)), tiles):
                whole[pl.ds(pl.multiple_of(side * half, half), half), :] = ref[...].reshape(
                    half, sum_width
                )
            return whole[:, :col_width], whole[:, col_width : col_width + width]

        whole_scratch = [pltpu.VMEM((width, sum_width), F32)]

        def first_kernel(
            place, sizes, bits, scale, own, a, b, c, q0, q1, q2, q3, left, x,
            samples_out, mine, other,
        ):
            samples = own[...] + a[...] + b[...] + c[...]
            batch = batch_ids(place, sizes, (1, row_count), 1)
            weight = weight_rows(scale, left)
            for k, q in enumerate((q0, q1, q2, q3)):
                source = (place[0] + (snp - k)) % snp
                masked = [
                    jnp.where(gone_in(bits[source * local_blocks + j], batch), weight, 0.0)
                    for j in range(local_blocks)
                ]
                samples = samples + exact_dot(q[...], jnp.concatenate(masked, axis=0), 1, 0)
            samples_out[...] = samples
            write_send(
                split_dot(samples, x[...], 0),
                exact_dot(samples, samples, 1, 1),
                core_of(place),
                mine,
                other,
            )

        def forward_kernel(place, *refs):
            tiles, (x, raw_out, product_out, gram_out, wire, whole) = refs[:2], refs[2:]
            columns, gram = read_sum(place, tiles, whole)
            raw = exact_dot(inverse_factor(gram / sample_count, True), columns, 1, 0)
            raw_out[...] = raw
            product = split_dot(raw, x[...], 1)
            own = exact_dot(raw, raw, 1, 1)
            product_out[...] = product
            gram_out[...] = own
            wire[...] = jnp.concatenate([product.astype(BF16), *three_parts(own)], axis=1)

        def backward_kernel(
            place, product, gram, a, b, c, raw, x, samples_out, columns_out, mine, other
        ):
            total, own = product[...], gram[...]
            for ref in (a, b, c):
                total = total + ref[:, :row_count].astype(F32)
                parts = [
                    ref[:, row_count + width * i : row_count + width * (i + 1)].astype(F32)
                    for i in range(3)
                ]
                own = own + (parts[0] + (parts[1] + parts[2]))
            factor = inverse_factor(own / snp_count, False)
            samples = exact_dot(factor, total, 1, 0)
            samples_out[...] = samples
            columns_out[...] = exact_dot(factor, raw[...], 1, 0)
            write_send(
                split_dot(samples, x[...], 0),
                exact_dot(samples, samples, 1, 1),
                core_of(place),
                mine,
                other,
            )

        def last_kernel(place, *refs):
            tiles, (samples, basis, projection, whole) = refs[:2], refs[2:]
            columns, gram = read_sum(place, tiles, whole)
            factor = inverse_factor(gram / sample_count, True)
            basis[...] = exact_dot(factor, samples[...], 1, 0)
            projection[...] = exact_dot(factor / math.sqrt(sample_count), columns, 1, 0)

        samples_shape = shape_of((width, row_count))
        columns_shape = shape_of((width, col_width))
        samples, mine, other = call_with_place(
            first_kernel,
            (samples_shape, part_shape, part_shape),
            start,
            *start_others,
            mixed,
            *mixed_others,
            left_rows,
            matrix,
            scalars=(batch_sizes, bits, singular),
        )
        columns, dtype = None, F32
        for _ in range(ITERS):
            raw, product, gram, wire = call_with_place(
                forward_kernel,
                (
                    columns_shape,
                    samples_shape,
                    shape_of((width, width)),
                    shape_of((width, packed), BF16),
                ),
                *samp_sum(mine, other, dtype),
                matrix,
                scratch=whole_scratch,
            )
            dtype = BF16
            samples, columns, mine, other = call_with_place(
                backward_kernel,
                (samples_shape, columns_shape, part_shape, part_shape),
                product,
                gram,
                *snp_others(wire),
                raw,
                matrix,
            )
        basis, projection = call_with_place(
            last_kernel,
            (samples_shape, columns_shape),
            *samp_sum(mine, other, dtype),
            samples,
            scratch=whole_scratch,
        )
        return (basis.T, projection.T, columns.T)

    in_specs = (
        P(samp_axes, "snp"),
        P("snp"),
        P(samp_axes, None),
        P(),
        P(("snp", *samp_axes), None),
        P("snp", None),
        P(),
        P(),
        P(),
    )
    out_specs = (P(samp_axes, None), P("snp", None), P("snp", None))
    return jax.shard_map(
        on_device, mesh=fine, in_specs=in_specs, out_specs=out_specs, check_vma=False
    )
```

profile of v0, /device:TPU:1, one launch (start us, length us, event | category | flops | bytes accessed | tf_op | source)
XLA Modules:
  0.0 176.3 jit_solution(6472302301501364273)
XLA Ops:
  0.6 3.3 %collective-permute-start.3 = (f32[16,20]{1,0:T(8,128)}, f32[16,20]{1,0:T(8,128)S(1)}, u32[]{:S(2)}, u32[]{:S(2)}) collective-permute-start(f32[16,20]{1,0:T(8,128)} %mine.1), channel_id=1, source_target_pairs={{0,4},{4,0},{1,5},{5,1},{2,6},{6,2},{3,7},{7,3},{8,12},{12,8},{9,1... | collective-permute-start | bytes 3848 | tf_op jit(solution)/shard_map/ppermute | solution.py:114
  4.0 3.2 %shard_map.112 = (bf16[640,1024]{1,0:T(8,128)(2,1)}, f32[64,640]{1,0:T(8,128)}, s32[16]{0:T(128)}) custom-call(s32[1]{0:T(128)} %bitcast.place, s32[12]{0:T(128)} %sizes.3, s32[48]{0:T(128)} %batch_in.1, s32[48]{0:T(128)} %block_in.1, s32[640,1024]{1,0:T(8,128)} %geno_in.1, f32[1,1024]{1,0:T(1,128)} %bitcast.11, bf16[64,1024]{1,0:T(8,128)(2,1)} %bitcast.7), custom_call_target="tpu_custom_call" | custom-call | tf_op jit(solution)/shard_map/pallas_call | solution.py:229
  7.2 0.6 copy-done.6
  7.9 1.3 shard_map.113
  9.2 9.3 %all-to-all-start = ((f32[32,8,128]{2,1,0:T(8,128)}), f32[32,8,128]{2,1,0:T(8,128)S(1)}, u32[]{:S(2)}, u32[]{:S(2)}) async-start(f32[32,8,128]{2,1,0:T(8,128)} %shard_map.113), calls=%async_computation | async-start | bytes 262144 | tf_op jit(solution)/shard_map/all_to_all | solution.py:271
  18.5 2.8 %collective-permute-start.2 = (f32[64,640]{1,0:T(8,128)}, f32[64,640]{1,0:T(8,128)S(1)}, u32[]{:S(2)}, u32[]{:S(2)}) collective-permute-start(f32[64,640]{1,0:T(8,128)} %get-tuple-element.37.own), channel_id=1, source_target_pairs={{0,3},{1,0},{2,1},{3,2},{4,7},{5,4},{6,5},{7,6},{8,11},{9,8},{10,9... | collective-permute-start | bytes 491528 | tf_op jit(solution)/shard_map/ppermute | solution.py:118
  21.6 0.7 collective-permute-start
  22.3 6.1 %all-to-all-done.tiles = f32[32,8,128]{2,1,0:T(8,128)S(1)} async-done(((f32[32,8,128]{2,1,0:T(8,128)}), f32[32,8,128]{2,1,0:T(8,128)S(1)}, u32[]{:S(2)}, u32[]{:S(2)}) %all-to-all-start) | async-done | bytes 131104 | tf_op jit(solution)/shard_map/all_to_all | solution.py:271
  28.4 0.5 shard_map.114.q0
  28.9 2.8 %collective-permute-start.6 = (f32[64,128]{1,0:T(8,128)S(1)}, f32[64,128]{1,0:T(8,128)S(1)}, u32[]{:S(2)}, u32[]{:S(2)}) collective-permute-start(f32[64,128]{1,0:T(8,128)S(1)} %shard_map.114.q0), channel_id=1, source_target_pairs={{0,3},{1,0},{2,1},{3,2},{4,7},{5,4},{6,5},{7,6},{8,11},{9,8},{10,9... | collective-permute-start | bytes 98312 | tf_op jit(solution)/shard_map/ppermute | solution.py:118
  32.1 0.7 collective-permute-start.4
  32.8 1.3 copy-done
  34.1 0.7 copy-done.7
  34.8 2.9 %shard_map.115.x.refs_2_ = bf16[640,1024]{1,0:T(8,128)(2,1)S(1)} custom-call(s32[1]{0:T(128)} %bitcast.place, s32[12]{0:T(128)S(1)} %copy-done.5, s32[16]{0:T(128)S(1)} %copy-done.7, f32[20]{0:T(128)S(1)} %copy-done.8, bf16[640,1024]{1,0:T(8,128)(2,1)S(1)} %copy-done, f32[20,640]{1,0:T(8,128)S(1)} %bitcast.9, f32[32,8,128]{2,1,0:T(8,128)S(1)} %all-to-all-done.tiles), custom_call_target="tpu_custom_call" | custom-call | tf_op jit(solution)/shard_map/pallas_call | solution.py:156
  37.7 2.2 %shard_map.116 = (f32[64,640]{1,0:T(8,128)}, f32[32,1152]{1,0:T(8,128)S(1)}, f32[32,1152]{1,0:T(8,128)S(1)}) custom-call(s32[1]{0:T(128)} %bitcast.place, s32[12]{0:T(128)S(1)} %copy-done.5, s32[16]{0:T(128)S(1)} %copy-done.7, f32[20]{0:T(128)S(1)} %copy-done.8, f32[64,640]{1,0:T(8,128)S(1)} %copy-done.3, f32[64,640]{1,0:T(8,128)S(1)} %collective-permute-done.a, ...), custom_call_target="tpu_custom_call" | custom-call | tf_op jit(solution)/shard_map/pallas_call | solution.py:156
  40.0 2.3 %collective-permute-start.7 = (f32[32,1152]{1,0:T(8,128)S(1)}, f32[32,1152]{1,0:T(8,128)S(1)}, u32[]{:S(2)}, u32[]{:S(2)}) collective-permute-start(f32[32,1152]{1,0:T(8,128)S(1)} %get-tuple-element.40), channel_id=1, source_target_pairs={{0,4},{4,0},{1,5},{5,1},{2,6},{6,2},{3,7},{7,3},{8,12},{12,8},{9,1... | collective-permute-start | bytes 442376 | tf_op jit(solution)/shard_map/ppermute | solution.py:114
  42.2 1.0 collective-permute-done.7.got
  43.4 2.3 %collective-permute-start.9 = (f32[8,1152]{1,0:T(8,128)S(1)}, f32[8,1152]{1,0:T(8,128)S(1)}, u32[]{:S(2)}, u32[]{:S(2)}) collective-permute-start(f32[8,1152]{1,0:T(8,128)S(1)} %get-tuple-element.43), channel_id=1, source_target_pairs={{0,16},{8,24},{16,0},{24,8},{1,17},{9,25},{17,1},{25,9},{2,18},{10... | collective-permute-start | bytes 110600 | tf_op jit(solution)/shard_map/ppermute | solution.py:123
  45.7 0.8 collective-permute-start.10
  46.4 0.9 collective-permute-done.8.a
  47.4 1.0 collective-permute-done.9.b
  48.3 0.4 collective-permute-done.10.c
  48.8 12.8 %all_to_all.35.parts = f32[8,8,1152]{2,1,0:T(8,128)S(1)} all-to-all(f32[8,8,1152]{2,1,0:T(8,128)S(1)} %shard_map.118), channel_id=1, replica_groups=mesh['z'=8,'x'=4,'core'=2,'snp'=4] {'z'}, dimensions={0} | all-to-all | bytes 589824 | tf_op jit(solution)/shard_map/all_to_all | solution.py:389
  61.6 8.6 %all_to_all.36.refs_0_ = f32[4,8,1152]{2,1,0:T(8,128)S(1)} all-to-all(f32[4,8,1152]{2,1,0:T(8,128)S(1)} %shard_map.119), channel_id=1, replica_groups=mesh['z'=8,'x'=4,'core'=2,'snp'=4] {'x'}, dimensions={0} | all-to-all | bytes 294912 | tf_op jit(solution)/shard_map/all_to_all | solution.py:391
  70.2 5.2 %collective-permute-start.11 = (f32[4,8,1152]{2,1,0:T(8,128)S(1)}, f32[4,8,1152]{2,1,0:T(8,128)S(1)}, u32[]{:S(2)}, u32[]{:S(2)}) collective-permute-start(f32[4,8,1152]{2,1,0:T(8,128)S(1)} %all_to_all.36.refs_0_), channel_id=1, source_target_pairs={{0,4},{4,0},{1,5},{5,1},{2,6},{6,2},{3,7},{7,3},{8,12},{12,8},{9,1... | collective-permute-start | bytes 442376 | tf_op jit(solution)/shard_map/ppermute | solution.py:114
  75.4 1.0 collective-permute-done.11.refs_1_
  76.4 3.1 %shard_map.120 = (f32[64,1024]{1,0:T(8,128)S(1)}, f32[64,640]{1,0:T(8,128)S(1)}, f32[64,64]{1,0:T(8,128)S(1)}, bf16[64,832]{1,0:T(8,128)(2,1)S(1)}) custom-call(s32[1]{0:T(128)} %bitcast.place, f32[4,8,1152]{2,1,0:T(8,128)S(1)} %all_to_all.36.refs_0_, f32[4,8,1152]{2,1,0:T(8,128)S(1)} %collective-permute-done.11.refs_1_, ...), custom_call_target="tpu_custom_call" | custom-call | tf_op jit(solution)/shard_map/pallas_call | solution.py:156
  79.5 2.9 %collective-permute-start.14 = (bf16[64,832]{1,0:T(8,128)(2,1)S(1)}, bf16[64,832]{1,0:T(8,128)(2,1)S(1)}, u32[]{:S(2)}, u32[]{:S(2)}) collective-permute-start(bf16[64,832]{1,0:T(8,128)(2,1)S(1)} %get-tuple-element.47), channel_id=1, source_target_pairs={{0,3},{1,0},{2,1},{3,2},{4,7},{5,4},{6,5},{7,6},{8,11},{9,8},{10,9... | collective-permute-start | bytes 319496 | tf_op jit(solution)/shard_map/ppermute | solution.py:118
  82.3 1.6 collective-permute-start.13
  83.9 0.8 collective-permute-start.12
  84.6 3.2 %collective-permute-done.13.b = bf16[64,832]{1,0:T(8,128)(2,1)S(1)} collective-permute-done((bf16[64,832]{1,0:T(8,128)(2,1)S(1)}, bf16[64,832]{1,0:T(8,128)(2,1)S(1)}, u32[]{:S(2)}, u32[]{:S(2)}) %collective-permute-start.13) | collective-permute-done | bytes 106528 | tf_op jit(solution)/shard_map/ppermute | solution.py:118
  87.9 3.0 %collective-permute-done.12.a = bf16[64,832]{1,0:T(8,128)(2,1)S(1)} collective-permute-done((bf16[64,832]{1,0:T(8,128)(2,1)S(1)}, bf16[64,832]{1,0:T(8,128)(2,1)S(1)}, u32[]{:S(2)}, u32[]{:S(2)}) %collective-permute-start.12) | collective-permute-done | bytes 106528 | tf_op jit(solution)/shard_map/ppermute | solution.py:118
  90.9 3.5 %shard_map.121 = (f32[64,640]{1,0:T(8,128)}, f32[64,1024]{1,0:T(8,128)}, f32[32,1152]{1,0:T(8,128)S(1)}, f32[32,1152]{1,0:T(8,128)S(1)}) custom-call(s32[1]{0:T(128)} %bitcast.place, f32[64,640]{1,0:T(8,128)S(1)} %get-tuple-element.45.product, f32[64,64]{1,0:T(8,128)S(1)} %get-tuple-element.46.gram, bf16[64,832]{1,0:T(8,128)(2,1)S(1)} %collective-permute-done.12.a, ...), custom_call_target="tpu_custom_call" | custom-call | tf_op jit(solution)/shard_map/pallas_call | solution.py:156
  94.4 0.9 collective-permute-start.15
  95.3 1.0 collective-permute-done.15.got
  96.7 1.8 %collective-permute-start.17 = (f32[8,1152]{1,0:T(8,128)S(1)}, f32[8,1152]{1,0:T(8,128)S(1)}, u32[]{:S(2)}, u32[]{:S(2)}) collective-permute-start(f32[8,1152]{1,0:T(8,128)S(1)} %get-tuple-element.53), channel_id=1, source_target_pairs={{0,16},{8,24},{16,0},{24,8},{1,17},{9,25},{17,1},{25,9},{2,18},{10... | collective-permute-start | bytes 110600 | tf_op jit(solution)/shard_map/ppermute | solution.py:123
  98.5 0.8 collective-permute-start.18
  99.3 1.1 collective-permute-done.16.a
  100.5 0.6 collective-permute-done.17.b
  101.1 0.6 collective-permute-done.18.c
  101.8 10.8 %all_to_all.37.parts = bf16[8,8,1280]{2,1,0:T(8,128)(2,1)S(1)} all-to-all(bf16[8,8,1280]{2,1,0:T(8,128)(2,1)S(1)} %shard_map.123), channel_id=1, replica_groups=mesh['z'=8,'x'=4,'core'=2,'snp'=4] {'z'}, dimensions={0} | all-to-all | bytes 327680 | tf_op jit(solution)/shard_map/all_to_all | solution.py:389
  112.7 7.9 %all_to_all.38.refs_0_ = f32[4,8,1152]{2,1,0:T(8,128)S(1)} all-to-all(f32[4,8,1152]{2,1,0:T(8,128)S(1)} %shard_map.124), channel_id=1, replica_groups=mesh['z'=8,'x'=4,'core'=2,'snp'=4] {'x'}, dimensions={0} | all-to-all | bytes 294912 | tf_op jit(solution)/shard_map/all_to_all | solution.py:391
  120.6 4.4 %collective-permute-start.19 = (f32[4,8,1152]{2,1,0:T(8,128)S(1)}, f32[4,8,1152]{2,1,0:T(8,128)S(1)}, u32[]{:S(2)}, u32[]{:S(2)}) collective-permute-start(f32[4,8,1152]{2,1,0:T(8,128)S(1)} %all_to_all.38.refs_0_), channel_id=1, source_target_pairs={{0,4},{4,0},{1,5},{5,1},{2,6},{6,2},{3,7},{7,3},{8,12},{12,8},{9,1... | collective-permute-start | bytes 442376 | tf_op jit(solution)/shard_map/ppermute | solution.py:114
  125.1 1.0 collective-permute-done.19.refs_1_
  126.1 3.1 %shard_map.125 = (f32[64,1024]{1,0:T(8,128)S(1)}, f32[64,640]{1,0:T(8,128)S(1)}, f32[64,64]{1,0:T(8,128)S(1)}, bf16[64,832]{1,0:T(8,128)(2,1)S(1)}) custom-call(s32[1]{0:T(128)} %bitcast.place, f32[4,8,1152]{2,1,0:T(8,128)S(1)} %all_to_all.38.refs_0_, f32[4,8,1152]{2,1,0:T(8,128)S(1)} %collective-permute-done.19.refs_1_, ...), custom_call_target="tpu_custom_call" | custom-call | tf_op jit(solution)/shard_map/pallas_call | solution.py:156
  129.5 1.6 collective-permute-start.21
  131.1 0.4 collective-permute-start.20
  131.5 2.0 %collective-permute-done.22.c = bf16[64,832]{1,0:T(8,128)(2,1)S(1)} collective-permute-done((bf16[64,832]{1,0:T(8,128)(2,1)S(1)}, bf16[64,832]{1,0:T(8,128)(2,1)S(1)}, u32[]{:S(2)}, u32[]{:S(2)}) %collective-permute-start.22) | collective-permute-done | bytes 106528 | tf_op jit(solution)/shard_map/ppermute | solution.py:118
  133.5 1.5 collective-permute-done.21.b
  135.0 3.0 %collective-permute-done.20.a = bf16[64,832]{1,0:T(8,128)(2,1)S(1)} collective-permute-done((bf16[64,832]{1,0:T(8,128)(2,1)S(1)}, bf16[64,832]{1,0:T(8,128)(2,1)S(1)}, u32[]{:S(2)}, u32[]{:S(2)}) %collective-permute-start.20) | collective-permute-done | bytes 106528 | tf_op jit(solution)/shard_map/ppermute | solution.py:118
  138.1 3.4 %shard_map.126 = (f32[64,640]{1,0:T(8,128)S(1)}, f32[64,1024]{1,0:T(8,128)}, f32[32,1152]{1,0:T(8,128)S(1)}, f32[32,1152]{1,0:T(8,128)S(1)}) custom-call(s32[1]{0:T(128)} %bitcast.place, f32[64,640]{1,0:T(8,128)S(1)} %get-tuple-element.55.product, f32[64,64]{1,0:T(8,128)S(1)} %get-tuple-element.56.gram, bf16[64,832]{1,0:T(8,128)(2,1)S(1)} %collective-permute-done.20.a, ...), custom_call_target="tpu_custom_call" | custom-call | tf_op jit(solution)/shard_map/pallas_call | solution.py:156
  141.5 0.9 collective-permute-start.23
  142.4 1.0 collective-permute-done.23.got
  143.4 0.4 collective-permute-start.24
  143.8 1.8 %collective-permute-start.25 = (f32[8,1152]{1,0:T(8,128)S(1)}, f32[8,1152]{1,0:T(8,128)S(1)}, u32[]{:S(2)}, u32[]{:S(2)}) collective-permute-start(f32[8,1152]{1,0:T(8,128)S(1)} %get-tuple-element.63), channel_id=1, source_target_pairs={{0,16},{8,24},{16,0},{24,8},{1,17},{9,25},{17,1},{25,9},{2,18},{10... | collective-permute-start | bytes 110600 | tf_op jit(solution)/shard_map/ppermute | solution.py:123
  145.6 0.8 collective-permute-start.26
  146.4 1.1 collective-permute-done.24.a
  147.5 0.6 collective-permute-done.25.b
  148.2 0.6 collective-permute-done.26.c
  148.9 10.8 %all_to_all.39.parts = bf16[8,8,1280]{2,1,0:T(8,128)(2,1)S(1)} all-to-all(bf16[8,8,1280]{2,1,0:T(8,128)(2,1)S(1)} %shard_map.128), channel_id=1, replica_groups=mesh['z'=8,'x'=4,'core'=2,'snp'=4] {'z'}, dimensions={0} | all-to-all | bytes 327680 | tf_op jit(solution)/shard_map/all_to_all | solution.py:389
  159.8 7.9 %all_to_all.40.refs_0_ = f32[4,8,1152]{2,1,0:T(8,128)S(1)} all-to-all(f32[4,8,1152]{2,1,0:T(8,128)S(1)} %shard_map.129), channel_id=1, replica_groups=mesh['z'=8,'x'=4,'core'=2,'snp'=4] {'x'}, dimensions={0} | all-to-all | bytes 294912 | tf_op jit(solution)/shard_map/all_to_all | solution.py:391
  167.7 4.4 %collective-permute-start.27 = (f32[4,8,1152]{2,1,0:T(8,128)S(1)}, f32[4,8,1152]{2,1,0:T(8,128)S(1)}, u32[]{:S(2)}, u32[]{:S(2)}) collective-permute-start(f32[4,8,1152]{2,1,0:T(8,128)S(1)} %all_to_all.40.refs_0_), channel_id=1, source_target_pairs={{0,4},{4,0},{1,5},{5,1},{2,6},{6,2},{3,7},{7,3},{8,12},{12,8},{9,1... | collective-permute-start | bytes 442376 | tf_op jit(solution)/shard_map/ppermute | solution.py:114
  172.1 1.0 collective-permute-done.27.refs_1_
  173.1 3.2 %shard_map.130 = (f32[64,640]{1,0:T(8,128)}, f32[64,1024]{1,0:T(8,128)}) custom-call(s32[1]{0:T(128)} %bitcast.place, f32[4,8,1152]{2,1,0:T(8,128)S(1)} %all_to_all.40.refs_0_, f32[4,8,1152]{2,1,0:T(8,128)S(1)} %collective-permute-done.27.refs_1_, f32[64,640]{1,0:T(8,128)S(1)} %get-tuple-element.65.refs_2_), custom_call_target="tpu_custom_call" | custom-call | tf_op jit(solution)/shard_map/pallas_call | solution.py:156
  (37 shorter events, 2.1 us)
Async XLA Ops:
  0.6 6.6 %collective-permute-start.3 = (f32[16,20]{1,0:T(8,128)}, f32[16,20]{1,0:T(8,128)S(1)}, u32[]{:S(2)}, u32[]{:S(2)}) collective-permute-start(f32[16,20]{1,0:T(8,128)} %mine.1), channel_id=1, source_target_pairs={{0,4},{4,0},{1,5},{5,1},{2,6},{6,2},{3,7},{7,3},{8,12},{12,8},{9,1... | collective-permute-start | bytes 3848 | tf_op jit(solution)/shard_map/ppermute | solution.py:114
  4.0 3.2 %copy-start.4 = (f32[16,20]{1,0:T(8,128)S(1)}, f32[16,20]{1,0:T(8,128)}, u32[]{:S(2)}) copy-start(f32[16,20]{1,0:T(8,128)} %mine.1) | copy-start | bytes 3844
  4.0 24.4 %copy-start.1 = (bf16[1024,64]{0,1:T(8,128)(2,1)S(1)}, bf16[1024,64]{0,1:T(8,128)(2,1)}, u32[]{:S(2)}) copy-start(bf16[1024,64]{0,1:T(8,128)(2,1)} %param.14) | copy-start | bytes 393220
  4.0 28.8 %copy-start.2 = (f32[640,20]{0,1:T(8,128)S(1)}, f32[640,20]{0,1:T(8,128)}, u32[]{:S(2)}) copy-start(f32[640,20]{0,1:T(8,128)} %param.11) | copy-start | bytes 153604
  4.0 28.8 %copy-start.5 = (s32[12]{0:T(128)S(1)}, s32[12]{0:T(128)}, u32[]{:S(2)}) copy-start(s32[12]{0:T(128)} %sizes.3) | copy-start | bytes 148
  4.0 28.8 %copy-start.8 = (f32[20]{0:T(128)S(1)}, f32[20]{0:T(128)}, u32[]{:S(2)}) copy-start(f32[20]{0:T(128)} %scale.3) | copy-start | bytes 244
  7.2 0.7 copy-start.6
  9.2 19.2 %all-to-all-start = ((f32[32,8,128]{2,1,0:T(8,128)}), f32[32,8,128]{2,1,0:T(8,128)S(1)}, u32[]{:S(2)}, u32[]{:S(2)}) async-start(f32[32,8,128]{2,1,0:T(8,128)} %shard_map.113), calls=%async_computation | async-start | bytes 262144 | tf_op jit(solution)/shard_map/all_to_all | solution.py:271
  18.5 13.6 %collective-permute-start.2 = (f32[64,640]{1,0:T(8,128)}, f32[64,640]{1,0:T(8,128)S(1)}, u32[]{:S(2)}, u32[]{:S(2)}) collective-permute-start(f32[64,640]{1,0:T(8,128)} %get-tuple-element.37.own), channel_id=1, source_target_pairs={{0,3},{1,0},{2,1},{3,2},{4,7},{5,4},{6,5},{7,6},{8,11},{9,8},{10,9... | collective-permute-start | bytes 491528 | tf_op jit(solution)/shard_map/ppermute | solution.py:118
  21.3 16.4 %collective-permute-start.1 = (f32[64,640]{1,0:T(8,128)}, f32[64,640]{1,0:T(8,128)S(1)}, u32[]{:S(2)}, u32[]{:S(2)}) collective-permute-start(f32[64,640]{1,0:T(8,128)} %get-tuple-element.37.own), channel_id=1, source_target_pairs={{0,2},{1,3},{2,0},{3,1},{4,6},{5,7},{6,4},{7,5},{8,10},{9,11},{10,... | collective-permute-start | bytes 491528 | tf_op jit(solution)/shard_map/ppermute | solution.py:118
  21.6 16.1 %collective-permute-start = (f32[64,640]{1,0:T(8,128)}, f32[64,640]{1,0:T(8,128)S(1)}, u32[]{:S(2)}, u32[]{:S(2)}) collective-permute-start(f32[64,640]{1,0:T(8,128)} %get-tuple-element.37.own), channel_id=1, source_target_pairs={{0,1},{1,2},{2,3},{3,0},{4,5},{5,6},{6,7},{7,4},{8,9},{9,10},{10,1... | collective-permute-start | bytes 491528 | tf_op jit(solution)/shard_map/ppermute | solution.py:118
  28.9 8.8 %collective-permute-start.6 = (f32[64,128]{1,0:T(8,128)S(1)}, f32[64,128]{1,0:T(8,128)S(1)}, u32[]{:S(2)}, u32[]{:S(2)}) collective-permute-start(f32[64,128]{1,0:T(8,128)S(1)} %shard_map.114.q0), channel_id=1, source_target_pairs={{0,3},{1,0},{2,1},{3,2},{4,7},{5,4},{6,5},{7,6},{8,11},{9,8},{10,9... | collective-permute-start | bytes 98312 | tf_op jit(solution)/shard_map/ppermute | solution.py:118
  31.7 6.0 %collective-permute-start.5 = (f32[64,128]{1,0:T(8,128)S(1)}, f32[64,128]{1,0:T(8,128)S(1)}, u32[]{:S(2)}, u32[]{:S(2)}) collective-permute-start(f32[64,128]{1,0:T(8,128)S(1)} %shard_map.114.q0), channel_id=1, source_target_pairs={{0,2},{1,3},{2,0},{3,1},{4,6},{5,7},{6,4},{7,5},{8,10},{9,11},{10,... | collective-permute-start | bytes 98312 | tf_op jit(solution)/shard_map/ppermute | solution.py:118
  32.1 5.6 %collective-permute-start.4 = (f32[64,128]{1,0:T(8,128)S(1)}, f32[64,128]{1,0:T(8,128)S(1)}, u32[]{:S(2)}, u32[]{:S(2)}) collective-permute-start(f32[64,128]{1,0:T(8,128)S(1)} %shard_map.114.q0), channel_id=1, source_target_pairs={{0,1},{1,2},{2,3},{3,0},{4,5},{5,6},{6,7},{7,4},{8,9},{9,10},{10,1... | collective-permute-start | bytes 98312 | tf_op jit(solution)/shard_map/ppermute | solution.py:118
  32.8 1.3 copy-start
  34.1 0.7 copy-start.7
  34.8 3.0 %copy-start.3 = (f32[64,640]{1,0:T(8,128)S(1)}, f32[64,640]{1,0:T(8,128)}, u32[]{:S(2)}) copy-start(f32[64,640]{1,0:T(8,128)} %get-tuple-element.37.own) | copy-start | bytes 491524
  40.0 3.3 %collective-permute-start.7 = (f32[32,1152]{1,0:T(8,128)S(1)}, f32[32,1152]{1,0:T(8,128)S(1)}, u32[]{:S(2)}, u32[]{:S(2)}) collective-permute-start(f32[32,1152]{1,0:T(8,128)S(1)} %get-tuple-element.40), channel_id=1, source_target_pairs={{0,4},{4,0},{1,5},{5,1},{2,6},{6,2},{3,7},{7,3},{8,12},{12,8},{9,1... | collective-permute-start | bytes 442376 | tf_op jit(solution)/shard_map/ppermute | solution.py:114
  43.3 4.1 %collective-permute-start.8 = (f32[8,1152]{1,0:T(8,128)S(1)}, f32[8,1152]{1,0:T(8,128)S(1)}, u32[]{:S(2)}, u32[]{:S(2)}) collective-permute-start(f32[8,1152]{1,0:T(8,128)S(1)} %get-tuple-element.42), channel_id=1, source_target_pairs={{0,8},{8,16},{16,24},{24,0},{1,9},{9,17},{17,25},{25,1},{2,10},{10... | collective-permute-start | bytes 110600 | tf_op jit(solution)/shard_map/ppermute | solution.py:123
  43.4 5.0 %collective-permute-start.9 = (f32[8,1152]{1,0:T(8,128)S(1)}, f32[8,1152]{1,0:T(8,128)S(1)}, u32[]{:S(2)}, u32[]{:S(2)}) collective-permute-start(f32[8,1152]{1,0:T(8,128)S(1)} %get-tuple-element.43), channel_id=1, source_target_pairs={{0,16},{8,24},{16,0},{24,8},{1,17},{9,25},{17,1},{25,9},{2,18},{10... | collective-permute-start | bytes 110600 | tf_op jit(solution)/shard_map/ppermute | solution.py:123
  45.7 3.1 %collective-permute-start.10 = (f32[8,1152]{1,0:T(8,128)S(1)}, f32[8,1152]{1,0:T(8,128)S(1)}, u32[]{:S(2)}, u32[]{:S(2)}) collective-permute-start(f32[8,1152]{1,0:T(8,128)S(1)} %get-tuple-element.44), channel_id=1, source_target_pairs={{0,24},{8,0},{16,8},{24,16},{1,25},{9,1},{17,9},{25,17},{2,26},{10... | collective-permute-start | bytes 110600 | tf_op jit(solution)/shard_map/ppermute | solution.py:123
  70.2 6.2 %collective-permute-start.11 = (f32[4,8,1152]{2,1,0:T(8,128)S(1)}, f32[4,8,1152]{2,1,0:T(8,128)S(1)}, u32[]{:S(2)}, u32[]{:S(2)}) collective-permute-start(f32[4,8,1152]{2,1,0:T(8,128)S(1)} %all_to_all.36.refs_0_), channel_id=1, source_target_pairs={{0,4},{4,0},{1,5},{5,1},{2,6},{6,2},{3,7},{7,3},{8,12},{12,8},{9,1... | collective-permute-start | bytes 442376 | tf_op jit(solution)/shard_map/ppermute | solution.py:114
  79.5 5.2 %collective-permute-start.14 = (bf16[64,832]{1,0:T(8,128)(2,1)S(1)}, bf16[64,832]{1,0:T(8,128)(2,1)S(1)}, u32[]{:S(2)}, u32[]{:S(2)}) collective-permute-start(bf16[64,832]{1,0:T(8,128)(2,1)S(1)} %get-tuple-element.47), channel_id=1, source_target_pairs={{0,3},{1,0},{2,1},{3,2},{4,7},{5,4},{6,5},{7,6},{8,11},{9,8},{10,9... | collective-permute-start | bytes 319496 | tf_op jit(solution)/shard_map/ppermute | solution.py:118
  82.3 5.6 %collective-permute-start.13 = (bf16[64,832]{1,0:T(8,128)(2,1)S(1)}, bf16[64,832]{1,0:T(8,128)(2,1)S(1)}, u32[]{:S(2)}, u32[]{:S(2)}) collective-permute-start(bf16[64,832]{1,0:T(8,128)(2,1)S(1)} %get-tuple-element.47), channel_id=1, source_target_pairs={{0,2},{1,3},{2,0},{3,1},{4,6},{5,7},{6,4},{7,5},{8,10},{9,11},{10,... | collective-permute-start | bytes 319496 | tf_op jit(solution)/shard_map/ppermute | solution.py:118
  83.9 7.1 %collective-permute-start.12 = (bf16[64,832]{1,0:T(8,128)(2,1)S(1)}, bf16[64,832]{1,0:T(8,128)(2,1)S(1)}, u32[]{:S(2)}, u32[]{:S(2)}) collective-permute-start(bf16[64,832]{1,0:T(8,128)(2,1)S(1)} %get-tuple-element.47), channel_id=1, source_target_pairs={{0,1},{1,2},{2,3},{3,0},{4,5},{5,6},{6,7},{7,4},{8,9},{9,10},{10,1... | collective-permute-start | bytes 319496 | tf_op jit(solution)/shard_map/ppermute | solution.py:118
  94.4 1.9 %collective-permute-start.15 = (f32[32,1152]{1,0:T(8,128)S(1)}, f32[32,1152]{1,0:T(8,128)S(1)}, u32[]{:S(2)}, u32[]{:S(2)}) collective-permute-start(f32[32,1152]{1,0:T(8,128)S(1)} %get-tuple-element.50), channel_id=1, source_target_pairs={{0,4},{4,0},{1,5},{5,1},{2,6},{6,2},{3,7},{7,3},{8,12},{12,8},{9,1... | collective-permute-start | bytes 442376 | tf_op jit(solution)/shard_map/ppermute | solution.py:114
  96.4 4.1 %collective-permute-start.16 = (f32[8,1152]{1,0:T(8,128)S(1)}, f32[8,1152]{1,0:T(8,128)S(1)}, u32[]{:S(2)}, u32[]{:S(2)}) collective-permute-start(f32[8,1152]{1,0:T(8,128)S(1)} %get-tuple-element.52), channel_id=1, source_target_pairs={{0,8},{8,16},{16,24},{24,0},{1,9},{9,17},{17,25},{25,1},{2,10},{10... | collective-permute-start | bytes 110600 | tf_op jit(solution)/shard_map/ppermute | solution.py:123
  96.7 4.4 %collective-permute-start.17 = (f32[8,1152]{1,0:T(8,128)S(1)}, f32[8,1152]{1,0:T(8,128)S(1)}, u32[]{:S(2)}, u32[]{:S(2)}) collective-permute-start(f32[8,1152]{1,0:T(8,128)S(1)} %get-tuple-element.53), channel_id=1, source_target_pairs={{0,16},{8,24},{16,0},{24,8},{1,17},{9,25},{17,1},{25,9},{2,18},{10... | collective-permute-start | bytes 110600 | tf_op jit(solution)/shard_map/ppermute | solution.py:123
  98.5 3.2 %collective-permute-start.18 = (f32[8,1152]{1,0:T(8,128)S(1)}, f32[8,1152]{1,0:T(8,128)S(1)}, u32[]{:S(2)}, u32[]{:S(2)}) collective-permute-start(f32[8,1152]{1,0:T(8,128)S(1)} %get-tuple-element.54), channel_id=1, source_target_pairs={{0,24},{8,0},{16,8},{24,16},{1,25},{9,1},{17,9},{25,17},{2,26},{10... | collective-permute-start | bytes 110600 | tf_op jit(solution)/shard_map/ppermute | solution.py:123
  120.6 5.4 %collective-permute-start.19 = (f32[4,8,1152]{2,1,0:T(8,128)S(1)}, f32[4,8,1152]{2,1,0:T(8,128)S(1)}, u32[]{:S(2)}, u32[]{:S(2)}) collective-permute-start(f32[4,8,1152]{2,1,0:T(8,128)S(1)} %all_to_all.38.refs_0_), channel_id=1, source_target_pairs={{0,4},{4,0},{1,5},{5,1},{2,6},{6,2},{3,7},{7,3},{8,12},{12,8},{9,1... | collective-permute-start | bytes 442376 | tf_op jit(solution)/shard_map/ppermute | solution.py:114
  129.1 4.4 %collective-permute-start.22 = (bf16[64,832]{1,0:T(8,128)(2,1)S(1)}, bf16[64,832]{1,0:T(8,128)(2,1)S(1)}, u32[]{:S(2)}, u32[]{:S(2)}) collective-permute-start(bf16[64,832]{1,0:T(8,128)(2,1)S(1)} %get-tuple-element.57), channel_id=1, source_target_pairs={{0,3},{1,0},{2,1},{3,2},{4,7},{5,4},{6,5},{7,6},{8,11},{9,8},{10,9... | collective-permute-start | bytes 319496 | tf_op jit(solution)/shard_map/ppermute | solution.py:118
  129.5 5.6 %collective-permute-start.21 = (bf16[64,832]{1,0:T(8,128)(2,1)S(1)}, bf16[64,832]{1,0:T(8,128)(2,1)S(1)}, u32[]{:S(2)}, u32[]{:S(2)}) collective-permute-start(bf16[64,832]{1,0:T(8,128)(2,1)S(1)} %get-tuple-element.57), channel_id=1, source_target_pairs={{0,2},{1,3},{2,0},{3,1},{4,6},{5,7},{6,4},{7,5},{8,10},{9,11},{10,... | collective-permute-start | bytes 319496 | tf_op jit(solution)/shard_map/ppermute | solution.py:118
  131.1 7.0 %collective-permute-start.20 = (bf16[64,832]{1,0:T(8,128)(2,1)S(1)}, bf16[64,832]{1,0:T(8,128)(2,1)S(1)}, u32[]{:S(2)}, u32[]{:S(2)}) collective-permute-start(bf16[64,832]{1,0:T(8,128)(2,1)S(1)} %get-tuple-element.57), channel_id=1, source_target_pairs={{0,1},{1,2},{2,3},{3,0},{4,5},{5,6},{6,7},{7,4},{8,9},{9,10},{10,1... | collective-permute-start | bytes 319496 | tf_op jit(solution)/shard_map/ppermute | solution.py:118
  141.5 1.9 %collective-permute-start.23 = (f32[32,1152]{1,0:T(8,128)S(1)}, f32[32,1152]{1,0:T(8,128)S(1)}, u32[]{:S(2)}, u32[]{:S(2)}) collective-permute-start(f32[32,1152]{1,0:T(8,128)S(1)} %get-tuple-element.60), channel_id=1, source_target_pairs={{0,4},{4,0},{1,5},{5,1},{2,6},{6,2},{3,7},{7,3},{8,12},{12,8},{9,1... | collective-permute-start | bytes 442376 | tf_op jit(solution)/shard_map/ppermute | solution.py:114
  143.4 4.1 %collective-permute-start.24 = (f32[8,1152]{1,0:T(8,128)S(1)}, f32[8,1152]{1,0:T(8,128)S(1)}, u32[]{:S(2)}, u32[]{:S(2)}) collective-permute-start(f32[8,1152]{1,0:T(8,128)S(1)} %get-tuple-element.62), channel_id=1, source_target_pairs={{0,8},{8,16},{16,24},{24,0},{1,9},{9,17},{17,25},{25,1},{2,10},{10... | collective-permute-start | bytes 110600 | tf_op jit(solution)/shard_map/ppermute | solution.py:123
  143.8 4.4 %collective-permute-start.25 = (f32[8,1152]{1,0:T(8,128)S(1)}, f32[8,1152]{1,0:T(8,128)S(1)}, u32[]{:S(2)}, u32[]{:S(2)}) collective-permute-start(f32[8,1152]{1,0:T(8,128)S(1)} %get-tuple-element.63), channel_id=1, source_target_pairs={{0,16},{8,24},{16,0},{24,8},{1,17},{9,25},{17,1},{25,9},{2,18},{10... | collective-permute-start | bytes 110600 | tf_op jit(solution)/shard_map/ppermute | solution.py:123
  145.6 3.2 %collective-permute-start.26 = (f32[8,1152]{1,0:T(8,128)S(1)}, f32[8,1152]{1,0:T(8,128)S(1)}, u32[]{:S(2)}, u32[]{:S(2)}) collective-permute-start(f32[8,1152]{1,0:T(8,128)S(1)} %get-tuple-element.64), channel_id=1, source_target_pairs={{0,24},{8,0},{16,8},{24,16},{1,25},{9,1},{17,9},{25,17},{2,26},{10... | collective-permute-start | bytes 110600 | tf_op jit(solution)/shard_map/ppermute | solution.py:123
  167.7 5.4 %collective-permute-start.27 = (f32[4,8,1152]{2,1,0:T(8,128)S(1)}, f32[4,8,1152]{2,1,0:T(8,128)S(1)}, u32[]{:S(2)}, u32[]{:S(2)}) collective-permute-start(f32[4,8,1152]{2,1,0:T(8,128)S(1)} %all_to_all.40.refs_0_), channel_id=1, source_target_pairs={{0,4},{4,0},{1,5},{5,1},{2,6},{6,2},{3,7},{7,3},{8,12},{12,8},{9,1... | collective-permute-start | bytes 442376 | tf_op jit(solution)/shard_map/ppermute | solution.py:114
where the time goes:
time: 177 us; the launch traced here: 176 us
  blocking collectives  58.8 us (33%)
  starting transfers between devices  55.1 us (31%)
  waiting for transfers between devices  32.1 us (18%)
  Pallas kernels  26.9 us (15%)
  local copies, waits for them, and re-layouts  2.64 us (1%)
    all_to_all x3, blocking collectives, samp_sum(): lax.all_to_all(spread, 'z', 0, 0)  34.3 us
    all_to_all x3, blocking collectives, samp_sum(): near = lax.all_to_all(tiles, 'x', 0, 0)  24.5 us
    pallas_call x18, Pallas kernels, call_with_place(): pl.pallas_call(body, out_shape=outs, in_specs=specs, scratch_shapes=scrat...  23.7 us
    ppermute x7, starting transfers between devices, swap(): return lax.ppermute(value, 'core', [(0, 1), (1, 0)])  21.4 us
    ppermute x12, starting transfers between devices, snp_others(): lax.ppermute(value, 'snp', [(i, (i + k) % snp) for i in range(snp)])  15.2 us
    ppermute x12, waiting for transfers between devices, snp_others(): lax.ppermute(value, 'snp', [(i, (i + k) % snp) for i in range(snp)])  12.9 us
    all_to_all x1, starting transfers between devices, on_device(): lax.all_to_all(call_with_place(pack_kernel, shape_of((chips, SUB, LANES))...  9.3 us
    ppermute x9, starting transfers between devices, x_shift(): return lax.ppermute(value, 'x', [(i, (i + k) % ring) for i in range(ring)])  9.13 us
  transfers between devices with their start and end apart: 29, of which 21 were waited for; matrix products, arithmetic and copies ran while one was open for 0% of the time, Pallas kernels for 4%

commit v1 on v0

--- a/solution.py
+++ b/solution.py
@@ -46,6 +46,10 @@
     tiles = [wide[SUB * t : SUB * (t + 1)] for t in range(count)]
     sub = lax.broadcasted_iota(jnp.int32, shape, 0)
     step = 1 if lower else -1
+
+    def spread_row(value, k):
+        return jnp.broadcast_to(value[k : k + 1], shape)
+
     for a in range(count)[::step]:
         active = range(a, count) if lower else range(a + 1)
         cols = {
@@ -56,31 +60,36 @@
             for t in active
         }
         scale = jnp.zeros(shape, F32)
-        for k in range(SUB)[::step]:
-            pivot = jnp.broadcast_to(cols[a][k][k : k + 1], shape)
-            inverse = 1.0 / pivot
-            scale = jnp.where(sub == k, pivot, scale)
-            keep = (sub > k) if lower else (sub < k)
-            rest = range(k + 1, SUB) if lower else range(k)
-            row = jnp.broadcast_to(tiles[a][k : k + 1], shape) * inverse
-            heads = {j: jnp.broadcast_to(cols[a][j][k : k + 1], shape) * inverse for j in rest}
+        order = range(SUB)[::step]
+        for p, q in zip(order[::2], order[1::2]):
+            aa, bb = spread_row(cols[a][p], p), spread_row(cols[a][p], q)
+            cc = spread_row(cols[a][q], q)
+            det = aa * cc - bb * bb
+            inverse, first = 1.0 / det, 1.0 / aa
+            ia, ib, ic = cc * inverse, bb * inverse, aa * inverse
+            scale = jnp.where(sub == p, aa, jnp.where(sub == q, det * first, scale))
+            keep = (sub > q) if lower else (sub < q)
+            rest = [j for j in order if (j > q if lower else j < q)]
+
+            def solved(value):
+                vp, vq = spread_row(value, p), spread_row(value, q)
+                return ia * vp - ib * vq, ic * vq - ib * vp
+
+            row_p = spread_row(tiles[a], p)
+            up, uq = solved(tiles[a])
+            heads = {j: solved(cols[a][j]) for j in rest}
             for t in active:
-                column = cols[t][k]
+                cp, cq = cols[t][p], cols[t][q]
+                for j in rest:
+                    cols[t][j] = cols[t][j] - (cp * heads[j][0] + cq * heads[j][1])
                 if t == a:
-                    column = jnp.where(keep, column, 0.0)
-                tiles[t] = tiles[t] - column * row
-                for j in rest:
-                    cols[t][j] = cols[t][j] - column * heads[j]
+                    inner = jnp.where(sub == q, bb * first, 0.0) * row_p
+                    cp, cq = jnp.where(keep, cp, 0.0), jnp.where(keep, cq, 0.0)
+                    tiles[t] = tiles[t] - (cp * up + cq * uq) - inner
+                else:
+                    tiles[t] = tiles[t] - (cp * up + cq * uq)
         tiles[a] = tiles[a] * lax.rsqrt(scale)
     return jnp.concatenate(tiles, axis=0)[:, size:]
-
-
-def kernel_call(body, out_shapes, *operands):
-    return pl.pallas_call(
-        body,
-        out_shape=out_shapes,
-        compiler_params=pltpu.CompilerParams(vmem_limit_bytes=48 * 1024 * 1024),
-    )(*operands)
 
 
 def shape_of(shape, dtype=F32):
@@ -255,8 +264,7 @@
             omega,
         )
 
-        def pack_kernel(place, bits, mine, other, spread):
-            del bits
+        def pack_kernel(place, mine, other, spread):
             first = core_of(place) == 0
             low = jnp.where(first, mine[...], other[...])
             high = jnp.where(first, other[...], mine[...])
@@ -274,7 +282,6 @@
                 shape_of((chips, SUB, LANES)),
                 right_factors,
                 swap(right_factors),
-                scalars=(bits,),
             ),
             ("z", "x"),
             0,

time: 177 us -> 175 us (0.989)
  waiting for transfers between devices: 32.1 us -> 26.1 us
  starting transfers between devices: 55.1 us -> 59.1 us
    all_to_all x1, waiting for transfers between devices: 6.07 us -> 1.02 us  [on_device(): lax.all_to_all(call_with_place(pack_kernel, shape_of((chips, SUB, LANES))...]
    ppermute x12, starting transfers between devices: 15.2 us -> 18.6 us  [snp_others(): lax.ppermute(value, 'snp', [(i, (i + k) % snp) for i in range(snp)])]
    ppermute x12, waiting for transfers between devices: 12.9 us -> 9.9 us  [snp_others(): lax.ppermute(value, 'snp', [(i, (i + k) % snp) for i in range(snp)])]
where the time goes in v1:
time: 175 us; the launch traced here: 174 us
  blocking collectives  59.7 us (34%)
  starting transfers between devices  59.1 us (34%)
  waiting for transfers between devices  26.1 us (15%)
  Pallas kernels  25.6 us (15%)
  local copies, waits for them, and re-layouts  2.69 us (2%)
    all_to_all x3, blocking collectives, samp_sum(): lax.all_to_all(spread, 'z', 0, 0)  35.6 us
    all_to_all x3, blocking collectives, samp_sum(): near = lax.all_to_all(tiles, 'x', 0, 0)  24.2 us
    ppermute x7, starting transfers between devices, swap(): return lax.ppermute(value, 'core', [(0, 1), (1, 0)])  22.8 us
    pallas_call x18, Pallas kernels, call_with_place(): pl.pallas_call(body, out_shape=outs, in_specs=specs, scratch_shapes=scrat...  22.4 us
    ppermute x12, starting transfers between devices, snp_others(): lax.ppermute(value, 'snp', [(i, (i + k) % snp) for i in range(snp)])  18.6 us
    ppermute x12, waiting for transfers between devices, snp_others(): lax.ppermute(value, 'snp', [(i, (i + k) % snp) for i in range(snp)])  9.9 us
    all_to_all x1, starting transfers between devices, on_device(): lax.all_to_all(call_with_place(pack_kernel, shape_of((chips, SUB, LANES))...  9.3 us
    ppermute x9, starting transfers between devices, x_shift(): return lax.ppermute(value, 'x', [(i, (i + k) % ring) for i in range(ring)])  8.49 us
  transfers between devices with their start and end apart: 29, of which 21 were waited for; matrix products, arithmetic and copies ran while one was open for 0% of the time, Pallas kernels for 4%

profile of v1, /device:TPU:1, one launch (start us, length us, event | category | flops | bytes accessed | tf_op | source)
XLA Modules:
  0.0 174.1 jit_solution(18431073304816344598)
XLA Ops:
  0.6 3.3 %collective-permute-start.3 = (f32[16,20]{1,0:T(8,128)}, f32[16,20]{1,0:T(8,128)S(1)}, u32[]{:S(2)}, u32[]{:S(2)}) collective-permute-start(f32[16,20]{1,0:T(8,128)} %mine.1), channel_id=1, source_target_pairs={{0,4},{4,0},{1,5},{5,1},{2,6},{6,2},{3,7},{7,3},{8,12},{12,8},{9,1... | collective-permute-start | bytes 3848 | tf_op jit(solution)/shard_map/ppermute | solution.py:123
  4.0 1.0 collective-permute-done.3.other
  5.0 0.7 copy-done.4
  5.7 0.7 shard_map.113
  6.4 9.3 %all-to-all-start = ((f32[32,8,128]{2,1,0:T(8,128)}), f32[32,8,128]{2,1,0:T(8,128)S(1)}, u32[]{:S(2)}, u32[]{:S(2)}) async-start(f32[32,8,128]{2,1,0:T(8,128)} %shard_map.113), calls=%async_computation | async-start | bytes 262144 | tf_op jit(solution)/shard_map/all_to_all | solution.py:279
  15.8 3.2 %shard_map.112 = (bf16[640,1024]{1,0:T(8,128)(2,1)}, f32[64,640]{1,0:T(8,128)}, s32[16]{0:T(128)}) custom-call(s32[1]{0:T(128)} %bitcast.place, s32[12]{0:T(128)} %sizes.3, s32[48]{0:T(128)} %batch_in.1, s32[48]{0:T(128)} %block_in.1, s32[640,1024]{1,0:T(8,128)} %geno_in.1, f32[1,1024]{1,0:T(1,128)} %bitcast.11, bf16[64,1024]{1,0:T(8,128)(2,1)} %bitcast.7), custom_call_target="tpu_custom_call" | custom-call | tf_op jit(solution)/shard_map/pallas_call | solution.py:238
  19.0 1.4 collective-permute-start
  20.4 2.6 %collective-permute-start.1 = (f32[64,640]{1,0:T(8,128)}, f32[64,640]{1,0:T(8,128)S(1)}, u32[]{:S(2)}, u32[]{:S(2)}) collective-permute-start(f32[64,640]{1,0:T(8,128)} %get-tuple-element.37.own), channel_id=1, source_target_pairs={{0,2},{1,3},{2,0},{3,1},{4,6},{5,7},{6,4},{7,5},{8,10},{9,11},{10,... | collective-permute-start | bytes 491528 | tf_op jit(solution)/shard_map/ppermute | solution.py:127
  23.0 1.1 collective-permute-start.2
  24.1 1.0 all-to-all-done.tiles
  25.1 0.5 shard_map.114.q0
  25.6 1.4 collective-permute-start.4
  27.0 2.6 %collective-permute-start.5 = (f32[64,128]{1,0:T(8,128)S(1)}, f32[64,128]{1,0:T(8,128)S(1)}, u32[]{:S(2)}, u32[]{:S(2)}) collective-permute-start(f32[64,128]{1,0:T(8,128)S(1)} %shard_map.114.q0), channel_id=1, source_target_pairs={{0,2},{1,3},{2,0},{3,1},{4,6},{5,7},{6,4},{7,5},{8,10},{9,11},{10,... | collective-permute-start | bytes 98312 | tf_op jit(solution)/shard_map/ppermute | solution.py:127
  29.6 1.1 collective-permute-start.6
  30.7 1.3 copy-done
  32.0 0.7 copy-done.7
  32.7 2.9 %shard_map.115.x.refs_2_ = bf16[640,1024]{1,0:T(8,128)(2,1)S(1)} custom-call(s32[1]{0:T(128)} %bitcast.place, s32[12]{0:T(128)S(1)} %copy-done.5, s32[16]{0:T(128)S(1)} %copy-done.7, f32[20]{0:T(128)S(1)} %copy-done.6, bf16[640,1024]{1,0:T(8,128)(2,1)S(1)} %copy-done, f32[20,640]{1,0:T(8,128)S(1)} %bitcast.9, f32[32,8,128]{2,1,0:T(8,128)S(1)} %all-to-all-done.tiles), custom_call_target="tpu_custom_call" | custom-call | tf_op jit(solution)/shard_map/pallas_call | solution.py:165
  35.6 2.2 %shard_map.116 = (f32[64,640]{1,0:T(8,128)}, f32[32,1152]{1,0:T(8,128)S(1)}, f32[32,1152]{1,0:T(8,128)S(1)}) custom-call(s32[1]{0:T(128)} %bitcast.place, s32[12]{0:T(128)S(1)} %copy-done.5, s32[16]{0:T(128)S(1)} %copy-done.7, f32[20]{0:T(128)S(1)} %copy-done.6, f32[64,640]{1,0:T(8,128)S(1)} %copy-done.3, f32[64,640]{1,0:T(8,128)S(1)} %collective-permute-done.a, ...), custom_call_target="tpu_custom_call" | custom-call | tf_op jit(solution)/shard_map/pallas_call | solution.py:165
  37.9 2.9 %collective-permute-start.7 = (f32[32,1152]{1,0:T(8,128)S(1)}, f32[32,1152]{1,0:T(8,128)S(1)}, u32[]{:S(2)}, u32[]{:S(2)}) collective-permute-start(f32[32,1152]{1,0:T(8,128)S(1)} %get-tuple-element.40), channel_id=1, source_target_pairs={{0,4},{4,0},{1,5},{5,1},{2,6},{6,2},{3,7},{7,3},{8,12},{12,8},{9,1... | collective-permute-start | bytes 442376 | tf_op jit(solution)/shard_map/ppermute | solution.py:123
  40.8 1.0 collective-permute-done.7.got
  41.8 1.0 collective-permute-start.10
  42.9 0.5 collective-permute-start.8
  43.4 1.0 collective-permute-start.9
  44.7 2.2 %collective-permute-done.8.a = f32[8,1152]{1,0:T(8,128)S(1)} collective-permute-done((f32[8,1152]{1,0:T(8,128)S(1)}, f32[8,1152]{1,0:T(8,128)S(1)}, u32[]{:S(2)}, u32[]{:S(2)}) %collective-permute-start.8) | collective-permute-done | bytes 36896 | tf_op jit(solution)/shard_map/ppermute | solution.py:132
  46.9 0.8 collective-permute-done.9.b
  47.7 14.1 %all_to_all.35.parts = f32[8,8,1152]{2,1,0:T(8,128)S(1)} all-to-all(f32[8,8,1152]{2,1,0:T(8,128)S(1)} %shard_map.118), channel_id=1, replica_groups=mesh['z'=8,'x'=4,'core'=2,'snp'=4] {'z'}, dimensions={0} | all-to-all | bytes 589824 | tf_op jit(solution)/shard_map/all_to_all | solution.py:396
  61.8 8.3 %all_to_all.36.refs_0_ = f32[4,8,1152]{2,1,0:T(8,128)S(1)} all-to-all(f32[4,8,1152]{2,1,0:T(8,128)S(1)} %shard_map.119), channel_id=1, replica_groups=mesh['z'=8,'x'=4,'core'=2,'snp'=4] {'x'}, dimensions={0} | all-to-all | bytes 294912 | tf_op jit(solution)/shard_map/all_to_all | solution.py:398
  70.1 5.2 %collective-permute-start.11 = (f32[4,8,1152]{2,1,0:T(8,128)S(1)}, f32[4,8,1152]{2,1,0:T(8,128)S(1)}, u32[]{:S(2)}, u32[]{:S(2)}) collective-permute-start(f32[4,8,1152]{2,1,0:T(8,128)S(1)} %all_to_all.36.refs_0_), channel_id=1, source_target_pairs={{0,4},{4,0},{1,5},{5,1},{2,6},{6,2},{3,7},{7,3},{8,12},{12,8},{9,1... | collective-permute-start | bytes 442376 | tf_op jit(solution)/shard_map/ppermute | solution.py:123
  75.2 1.0 collective-permute-done.11.refs_1_
  76.2 2.9 %shard_map.120 = (f32[64,1024]{1,0:T(8,128)S(1)}, f32[64,640]{1,0:T(8,128)S(1)}, f32[64,64]{1,0:T(8,128)S(1)}, bf16[64,832]{1,0:T(8,128)(2,1)S(1)}) custom-call(s32[1]{0:T(128)} %bitcast.place, f32[4,8,1152]{2,1,0:T(8,128)S(1)} %all_to_all.36.refs_0_, f32[4,8,1152]{2,1,0:T(8,128)S(1)} %collective-permute-done.11.refs_1_, ...), custom_call_target="tpu_custom_call" | custom-call | tf_op jit(solution)/shard_map/pallas_call | solution.py:165
  79.2 4.4 %collective-permute-start.13 = (bf16[64,832]{1,0:T(8,128)(2,1)S(1)}, bf16[64,832]{1,0:T(8,128)(2,1)S(1)}, u32[]{:S(2)}, u32[]{:S(2)}) collective-permute-start(bf16[64,832]{1,0:T(8,128)(2,1)S(1)} %get-tuple-element.47), channel_id=1, source_target_pairs={{0,2},{1,3},{2,0},{3,1},{4,6},{5,7},{6,4},{7,5},{8,10},{9,11},{10,... | collective-permute-start | bytes 319496 | tf_op jit(solution)/shard_map/ppermute | solution.py:127
  83.9 1.7 collective-permute-done.12.a
  85.7 3.3 %collective-permute-done.13.b = bf16[64,832]{1,0:T(8,128)(2,1)S(1)} collective-permute-done((bf16[64,832]{1,0:T(8,128)(2,1)S(1)}, bf16[64,832]{1,0:T(8,128)(2,1)S(1)}, u32[]{:S(2)}, u32[]{:S(2)}) %collective-permute-start.13) | collective-permute-done | bytes 106528 | tf_op jit(solution)/shard_map/ppermute | solution.py:127
  89.0 3.4 %shard_map.121 = (f32[64,640]{1,0:T(8,128)}, f32[64,1024]{1,0:T(8,128)}, f32[32,1152]{1,0:T(8,128)S(1)}, f32[32,1152]{1,0:T(8,128)S(1)}) custom-call(s32[1]{0:T(128)} %bitcast.place, f32[64,640]{1,0:T(8,128)S(1)} %get-tuple-element.45.product, f32[64,64]{1,0:T(8,128)S(1)} %get-tuple-element.46.gram, bf16[64,832]{1,0:T(8,128)(2,1)S(1)} %collective-permute-done.12.a, ...), custom_call_target="tpu_custom_call" | custom-call | tf_op jit(solution)/shard_map/pallas_call | solution.py:165
  92.4 1.2 collective-permute-start.15
  93.5 1.0 collective-permute-done.15.got
  94.9 1.8 %collective-permute-start.17 = (f32[8,1152]{1,0:T(8,128)S(1)}, f32[8,1152]{1,0:T(8,128)S(1)}, u32[]{:S(2)}, u32[]{:S(2)}) collective-permute-start(f32[8,1152]{1,0:T(8,128)S(1)} %get-tuple-element.53), channel_id=1, source_target_pairs={{0,16},{8,24},{16,0},{24,8},{1,17},{9,25},{17,1},{25,9},{2,18},{10... | collective-permute-start | bytes 110600 | tf_op jit(solution)/shard_map/ppermute | solution.py:132
  96.7 0.8 collective-permute-start.18
  97.6 1.1 collective-permute-done.16.a
  98.7 0.6 collective-permute-done.17.b
  99.3 0.6 collective-permute-done.18.c
  100.0 10.8 %all_to_all.37.parts = bf16[8,8,1280]{2,1,0:T(8,128)(2,1)S(1)} all-to-all(bf16[8,8,1280]{2,1,0:T(8,128)(2,1)S(1)} %shard_map.123), channel_id=1, replica_groups=mesh['z'=8,'x'=4,'core'=2,'snp'=4] {'z'}, dimensions={0} | all-to-all | bytes 327680 | tf_op jit(solution)/shard_map/all_to_all | solution.py:396
  110.9 7.9 %all_to_all.38.refs_0_ = f32[4,8,1152]{2,1,0:T(8,128)S(1)} all-to-all(f32[4,8,1152]{2,1,0:T(8,128)S(1)} %shard_map.124), channel_id=1, replica_groups=mesh['z'=8,'x'=4,'core'=2,'snp'=4] {'x'}, dimensions={0} | all-to-all | bytes 294912 | tf_op jit(solution)/shard_map/all_to_all | solution.py:398
  118.9 4.4 %collective-permute-start.19 = (f32[4,8,1152]{2,1,0:T(8,128)S(1)}, f32[4,8,1152]{2,1,0:T(8,128)S(1)}, u32[]{:S(2)}, u32[]{:S(2)}) collective-permute-start(f32[4,8,1152]{2,1,0:T(8,128)S(1)} %all_to_all.38.refs_0_), channel_id=1, source_target_pairs={{0,4},{4,0},{1,5},{5,1},{2,6},{6,2},{3,7},{7,3},{8,12},{12,8},{9,1... | collective-permute-start | bytes 442376 | tf_op jit(solution)/shard_map/ppermute | solution.py:123
  123.3 1.0 collective-permute-done.19.refs_1_
  124.3 2.9 %shard_map.125 = (f32[64,1024]{1,0:T(8,128)S(1)}, f32[64,640]{1,0:T(8,128)S(1)}, f32[64,64]{1,0:T(8,128)S(1)}, bf16[64,832]{1,0:T(8,128)(2,1)S(1)}) custom-call(s32[1]{0:T(128)} %bitcast.place, f32[4,8,1152]{2,1,0:T(8,128)S(1)} %all_to_all.38.refs_0_, f32[4,8,1152]{2,1,0:T(8,128)S(1)} %collective-permute-done.19.refs_1_, ...), custom_call_target="tpu_custom_call" | custom-call | tf_op jit(solution)/shard_map/pallas_call | solution.py:165
  127.1 1.0 collective-permute-start.20
  128.1 2.2 %collective-permute-start.21 = (bf16[64,832]{1,0:T(8,128)(2,1)S(1)}, bf16[64,832]{1,0:T(8,128)(2,1)S(1)}, u32[]{:S(2)}, u32[]{:S(2)}) collective-permute-start(bf16[64,832]{1,0:T(8,128)(2,1)S(1)} %get-tuple-element.57), channel_id=1, source_target_pairs={{0,2},{1,3},{2,0},{3,1},{4,6},{5,7},{6,4},{7,5},{8,10},{9,11},{10,... | collective-permute-start | bytes 319496 | tf_op jit(solution)/shard_map/ppermute | solution.py:127
  130.3 0.5 collective-permute-start.22
  130.8 2.0 %collective-permute-done.20.a = bf16[64,832]{1,0:T(8,128)(2,1)S(1)} collective-permute-done((bf16[64,832]{1,0:T(8,128)(2,1)S(1)}, bf16[64,832]{1,0:T(8,128)(2,1)S(1)}, u32[]{:S(2)}, u32[]{:S(2)}) %collective-permute-start.20) | collective-permute-done | bytes 106528 | tf_op jit(solution)/shard_map/ppermute | solution.py:127
  132.8 2.9 %collective-permute-done.21.b = bf16[64,832]{1,0:T(8,128)(2,1)S(1)} collective-permute-done((bf16[64,832]{1,0:T(8,128)(2,1)S(1)}, bf16[64,832]{1,0:T(8,128)(2,1)S(1)}, u32[]{:S(2)}, u32[]{:S(2)}) %collective-permute-start.21) | collective-permute-done | bytes 106528 | tf_op jit(solution)/shard_map/ppermute | solution.py:127
  135.7 3.3 %shard_map.126 = (f32[64,640]{1,0:T(8,128)S(1)}, f32[64,1024]{1,0:T(8,128)}, f32[32,1152]{1,0:T(8,128)S(1)}, f32[32,1152]{1,0:T(8,128)S(1)}) custom-call(s32[1]{0:T(128)} %bitcast.place, f32[64,640]{1,0:T(8,128)S(1)} %get-tuple-element.55.product, f32[64,64]{1,0:T(8,128)S(1)} %get-tuple-element.56.gram, bf16[64,832]{1,0:T(8,128)(2,1)S(1)} %collective-permute-done.20.a, ...), custom_call_target="tpu_custom_call" | custom-call | tf_op jit(solution)/shard_map/pallas_call | solution.py:165
  139.0 1.4 collective-permute-start.23
  140.3 1.0 collective-permute-done.23.got
  141.7 1.8 %collective-permute-start.25 = (f32[8,1152]{1,0:T(8,128)S(1)}, f32[8,1152]{1,0:T(8,128)S(1)}, u32[]{:S(2)}, u32[]{:S(2)}) collective-permute-start(f32[8,1152]{1,0:T(8,128)S(1)} %get-tuple-element.63), channel_id=1, source_target_pairs={{0,16},{8,24},{16,0},{24,8},{1,17},{9,25},{17,1},{25,9},{2,18},{10... | collective-permute-start | bytes 110600 | tf_op jit(solution)/shard_map/ppermute | solution.py:132
  143.5 0.8 collective-permute-start.26
  144.4 1.1 collective-permute-done.24.a
  145.5 0.6 collective-permute-done.25.b
  146.1 0.6 collective-permute-done.26.c
  146.8 10.8 %all_to_all.39.parts = bf16[8,8,1280]{2,1,0:T(8,128)(2,1)S(1)} all-to-all(bf16[8,8,1280]{2,1,0:T(8,128)(2,1)S(1)} %shard_map.128), channel_id=1, replica_groups=mesh['z'=8,'x'=4,'core'=2,'snp'=4] {'z'}, dimensions={0} | all-to-all | bytes 327680 | tf_op jit(solution)/shard_map/all_to_all | solution.py:396
  157.7 7.9 %all_to_all.40.refs_0_ = f32[4,8,1152]{2,1,0:T(8,128)S(1)} all-to-all(f32[4,8,1152]{2,1,0:T(8,128)S(1)} %shard_map.129), channel_id=1, replica_groups=mesh['z'=8,'x'=4,'core'=2,'snp'=4] {'x'}, dimensions={0} | all-to-all | bytes 294912 | tf_op jit(solution)/shard_map/all_to_all | solution.py:398
  165.7 4.4 %collective-permute-start.27 = (f32[4,8,1152]{2,1,0:T(8,128)S(1)}, f32[4,8,1152]{2,1,0:T(8,128)S(1)}, u32[]{:S(2)}, u32[]{:S(2)}) collective-permute-start(f32[4,8,1152]{2,1,0:T(8,128)S(1)} %all_to_all.40.refs_0_), channel_id=1, source_target_pairs={{0,4},{4,0},{1,5},{5,1},{2,6},{6,2},{3,7},{7,3},{8,12},{12,8},{9,1... | collective-permute-start | bytes 442376 | tf_op jit(solution)/shard_map/ppermute | solution.py:123
  170.1 1.0 collective-permute-done.27.refs_1_
  171.1 3.0 %shard_map.130 = (f32[64,640]{1,0:T(8,128)}, f32[64,1024]{1,0:T(8,128)}) custom-call(s32[1]{0:T(128)} %bitcast.place, f32[4,8,1152]{2,1,0:T(8,128)S(1)} %all_to_all.40.refs_0_, f32[4,8,1152]{2,1,0:T(8,128)S(1)} %collective-permute-done.27.refs_1_, f32[64,640]{1,0:T(8,128)S(1)} %get-tuple-element.65.refs_2_), custom_call_target="tpu_custom_call" | custom-call | tf_op jit(solution)/shard_map/pallas_call | solution.py:165
  (35 shorter events, 2.1 us)
Async XLA Ops:
  0.6 4.4 %collective-permute-start.3 = (f32[16,20]{1,0:T(8,128)}, f32[16,20]{1,0:T(8,128)S(1)}, u32[]{:S(2)}, u32[]{:S(2)}) collective-permute-start(f32[16,20]{1,0:T(8,128)} %mine.1), channel_id=1, source_target_pairs={{0,4},{4,0},{1,5},{5,1},{2,6},{6,2},{3,7},{7,3},{8,12},{12,8},{9,1... | collective-permute-start | bytes 3848 | tf_op jit(solution)/shard_map/ppermute | solution.py:123
  5.0 0.7 copy-start.4
  6.4 18.7 %all-to-all-start = ((f32[32,8,128]{2,1,0:T(8,128)}), f32[32,8,128]{2,1,0:T(8,128)S(1)}, u32[]{:S(2)}, u32[]{:S(2)}) async-start(f32[32,8,128]{2,1,0:T(8,128)} %shard_map.113), calls=%async_computation | async-start | bytes 262144 | tf_op jit(solution)/shard_map/all_to_all | solution.py:279
  15.7 9.3 %copy-start.1 = (bf16[1024,64]{0,1:T(8,128)(2,1)S(1)}, bf16[1024,64]{0,1:T(8,128)(2,1)}, u32[]{:S(2)}) copy-start(bf16[1024,64]{0,1:T(8,128)(2,1)} %param.14) | copy-start | bytes 393220
  15.8 14.9 %copy-start.2 = (f32[640,20]{0,1:T(8,128)S(1)}, f32[640,20]{0,1:T(8,128)}, u32[]{:S(2)}) copy-start(f32[640,20]{0,1:T(8,128)} %param.11) | copy-start | bytes 153604
  15.8 14.9 %copy-start.5 = (s32[12]{0:T(128)S(1)}, s32[12]{0:T(128)}, u32[]{:S(2)}) copy-start(s32[12]{0:T(128)} %sizes.3) | copy-start | bytes 148
  15.8 14.9 %copy-start.6 = (f32[20]{0:T(128)S(1)}, f32[20]{0:T(128)}, u32[]{:S(2)}) copy-start(f32[20]{0:T(128)} %scale.3) | copy-start | bytes 244
  19.0 10.6 %collective-permute-start = (f32[64,640]{1,0:T(8,128)}, f32[64,640]{1,0:T(8,128)S(1)}, u32[]{:S(2)}, u32[]{:S(2)}) collective-permute-start(f32[64,640]{1,0:T(8,128)} %get-tuple-element.37.own), channel_id=1, source_target_pairs={{0,1},{1,2},{2,3},{3,0},{4,5},{5,6},{6,7},{7,4},{8,9},{9,10},{10,1... | collective-permute-start | bytes 491528 | tf_op jit(solution)/shard_map/ppermute | solution.py:127
  20.4 15.2 %collective-permute-start.1 = (f32[64,640]{1,0:T(8,128)}, f32[64,640]{1,0:T(8,128)S(1)}, u32[]{:S(2)}, u32[]{:S(2)}) collective-permute-start(f32[64,640]{1,0:T(8,128)} %get-tuple-element.37.own), channel_id=1, source_target_pairs={{0,2},{1,3},{2,0},{3,1},{4,6},{5,7},{6,4},{7,5},{8,10},{9,11},{10,... | collective-permute-start | bytes 491528 | tf_op jit(solution)/shard_map/ppermute | solution.py:127
  23.0 12.6 %collective-permute-start.2 = (f32[64,640]{1,0:T(8,128)}, f32[64,640]{1,0:T(8,128)S(1)}, u32[]{:S(2)}, u32[]{:S(2)}) collective-permute-start(f32[64,640]{1,0:T(8,128)} %get-tuple-element.37.own), channel_id=1, source_target_pairs={{0,3},{1,0},{2,1},{3,2},{4,7},{5,4},{6,5},{7,6},{8,11},{9,8},{10,9... | collective-permute-start | bytes 491528 | tf_op jit(solution)/shard_map/ppermute | solution.py:127
  25.6 10.0 %collective-permute-start.4 = (f32[64,128]{1,0:T(8,128)S(1)}, f32[64,128]{1,0:T(8,128)S(1)}, u32[]{:S(2)}, u32[]{:S(2)}) collective-permute-start(f32[64,128]{1,0:T(8,128)S(1)} %shard_map.114.q0), channel_id=1, source_target_pairs={{0,1},{1,2},{2,3},{3,0},{4,5},{5,6},{6,7},{7,4},{8,9},{9,10},{10,1... | collective-permute-start | bytes 98312 | tf_op jit(solution)/shard_map/ppermute | solution.py:127
  27.0 8.6 %collective-permute-start.5 = (f32[64,128]{1,0:T(8,128)S(1)}, f32[64,128]{1,0:T(8,128)S(1)}, u32[]{:S(2)}, u32[]{:S(2)}) collective-permute-start(f32[64,128]{1,0:T(8,128)S(1)} %shard_map.114.q0), channel_id=1, source_target_pairs={{0,2},{1,3},{2,0},{3,1},{4,6},{5,7},{6,4},{7,5},{8,10},{9,11},{10,... | collective-permute-start | bytes 98312 | tf_op jit(solution)/shard_map/ppermute | solution.py:127
  29.6 6.0 %collective-permute-start.6 = (f32[64,128]{1,0:T(8,128)S(1)}, f32[64,128]{1,0:T(8,128)S(1)}, u32[]{:S(2)}, u32[]{:S(2)}) collective-permute-start(f32[64,128]{1,0:T(8,128)S(1)} %shard_map.114.q0), channel_id=1, source_target_pairs={{0,3},{1,0},{2,1},{3,2},{4,7},{5,4},{6,5},{7,6},{8,11},{9,8},{10,9... | collective-permute-start | bytes 98312 | tf_op jit(solution)/shard_map/ppermute | solution.py:127
  30.7 1.3 copy-start
  32.0 0.7 copy-start.7
  32.7 3.0 %copy-start.3 = (f32[64,640]{1,0:T(8,128)S(1)}, f32[64,640]{1,0:T(8,128)}, u32[]{:S(2)}) copy-start(f32[64,640]{1,0:T(8,128)} %get-tuple-element.37.own) | copy-start | bytes 491524
  37.9 3.9 %collective-permute-start.7 = (f32[32,1152]{1,0:T(8,128)S(1)}, f32[32,1152]{1,0:T(8,128)S(1)}, u32[]{:S(2)}, u32[]{:S(2)}) collective-permute-start(f32[32,1152]{1,0:T(8,128)S(1)} %get-tuple-element.40), channel_id=1, source_target_pairs={{0,4},{4,0},{1,5},{5,1},{2,6},{6,2},{3,7},{7,3},{8,12},{12,8},{9,1... | collective-permute-start | bytes 442376 | tf_op jit(solution)/shard_map/ppermute | solution.py:123
  41.8 2.9 %collective-permute-start.10 = (f32[8,1152]{1,0:T(8,128)S(1)}, f32[8,1152]{1,0:T(8,128)S(1)}, u32[]{:S(2)}, u32[]{:S(2)}) collective-permute-start(f32[8,1152]{1,0:T(8,128)S(1)} %get-tuple-element.44), channel_id=1, source_target_pairs={{0,24},{8,0},{16,8},{24,16},{1,25},{9,1},{17,9},{25,17},{2,26},{10... | collective-permute-start | bytes 110600 | tf_op jit(solution)/shard_map/ppermute | solution.py:132
  42.9 4.0 %collective-permute-start.8 = (f32[8,1152]{1,0:T(8,128)S(1)}, f32[8,1152]{1,0:T(8,128)S(1)}, u32[]{:S(2)}, u32[]{:S(2)}) collective-permute-start(f32[8,1152]{1,0:T(8,128)S(1)} %get-tuple-element.42), channel_id=1, source_target_pairs={{0,8},{8,16},{16,24},{24,0},{1,9},{9,17},{17,25},{25,1},{2,10},{10... | collective-permute-start | bytes 110600 | tf_op jit(solution)/shard_map/ppermute | solution.py:132
  43.4 4.3 %collective-permute-start.9 = (f32[8,1152]{1,0:T(8,128)S(1)}, f32[8,1152]{1,0:T(8,128)S(1)}, u32[]{:S(2)}, u32[]{:S(2)}) collective-permute-start(f32[8,1152]{1,0:T(8,128)S(1)} %get-tuple-element.43), channel_id=1, source_target_pairs={{0,16},{8,24},{16,0},{24,8},{1,17},{9,25},{17,1},{25,9},{2,18},{10... | collective-permute-start | bytes 110600 | tf_op jit(solution)/shard_map/ppermute | solution.py:132
  70.1 6.2 %collective-permute-start.11 = (f32[4,8,1152]{2,1,0:T(8,128)S(1)}, f32[4,8,1152]{2,1,0:T(8,128)S(1)}, u32[]{:S(2)}, u32[]{:S(2)}) collective-permute-start(f32[4,8,1152]{2,1,0:T(8,128)S(1)} %all_to_all.36.refs_0_), channel_id=1, source_target_pairs={{0,4},{4,0},{1,5},{5,1},{2,6},{6,2},{3,7},{7,3},{8,12},{12,8},{9,1... | collective-permute-start | bytes 442376 | tf_op jit(solution)/shard_map/ppermute | solution.py:123
  79.1 6.5 %collective-permute-start.12 = (bf16[64,832]{1,0:T(8,128)(2,1)S(1)}, bf16[64,832]{1,0:T(8,128)(2,1)S(1)}, u32[]{:S(2)}, u32[]{:S(2)}) collective-permute-start(bf16[64,832]{1,0:T(8,128)(2,1)S(1)} %get-tuple-element.47), channel_id=1, source_target_pairs={{0,1},{1,2},{2,3},{3,0},{4,5},{5,6},{6,7},{7,4},{8,9},{9,10},{10,1... | collective-permute-start | bytes 319496 | tf_op jit(solution)/shard_map/ppermute | solution.py:127
  79.2 9.8 %collective-permute-start.13 = (bf16[64,832]{1,0:T(8,128)(2,1)S(1)}, bf16[64,832]{1,0:T(8,128)(2,1)S(1)}, u32[]{:S(2)}, u32[]{:S(2)}) collective-permute-start(bf16[64,832]{1,0:T(8,128)(2,1)S(1)} %get-tuple-element.47), channel_id=1, source_target_pairs={{0,2},{1,3},{2,0},{3,1},{4,6},{5,7},{6,4},{7,5},{8,10},{9,11},{10,... | collective-permute-start | bytes 319496 | tf_op jit(solution)/shard_map/ppermute | solution.py:127
  83.6 5.4 %collective-permute-start.14 = (bf16[64,832]{1,0:T(8,128)(2,1)S(1)}, bf16[64,832]{1,0:T(8,128)(2,1)S(1)}, u32[]{:S(2)}, u32[]{:S(2)}) collective-permute-start(bf16[64,832]{1,0:T(8,128)(2,1)S(1)} %get-tuple-element.47), channel_id=1, source_target_pairs={{0,3},{1,0},{2,1},{3,2},{4,7},{5,4},{6,5},{7,6},{8,11},{9,8},{10,9... | collective-permute-start | bytes 319496 | tf_op jit(solution)/shard_map/ppermute | solution.py:127
  92.4 2.2 %collective-permute-start.15 = (f32[32,1152]{1,0:T(8,128)S(1)}, f32[32,1152]{1,0:T(8,128)S(1)}, u32[]{:S(2)}, u32[]{:S(2)}) collective-permute-start(f32[32,1152]{1,0:T(8,128)S(1)} %get-tuple-element.50), channel_id=1, source_target_pairs={{0,4},{4,0},{1,5},{5,1},{2,6},{6,2},{3,7},{7,3},{8,12},{12,8},{9,1... | collective-permute-start | bytes 442376 | tf_op jit(solution)/shard_map/ppermute | solution.py:123
  94.6 4.1 %collective-permute-start.16 = (f32[8,1152]{1,0:T(8,128)S(1)}, f32[8,1152]{1,0:T(8,128)S(1)}, u32[]{:S(2)}, u32[]{:S(2)}) collective-permute-start(f32[8,1152]{1,0:T(8,128)S(1)} %get-tuple-element.52), channel_id=1, source_target_pairs={{0,8},{8,16},{16,24},{24,0},{1,9},{9,17},{17,25},{25,1},{2,10},{10... | collective-permute-start | bytes 110600 | tf_op jit(solution)/shard_map/ppermute | solution.py:132
  94.9 4.4 %collective-permute-start.17 = (f32[8,1152]{1,0:T(8,128)S(1)}, f32[8,1152]{1,0:T(8,128)S(1)}, u32[]{:S(2)}, u32[]{:S(2)}) collective-permute-start(f32[8,1152]{1,0:T(8,128)S(1)} %get-tuple-element.53), channel_id=1, source_target_pairs={{0,16},{8,24},{16,0},{24,8},{1,17},{9,25},{17,1},{25,9},{2,18},{10... | collective-permute-start | bytes 110600 | tf_op jit(solution)/shard_map/ppermute | solution.py:132
  96.7 3.2 %collective-permute-start.18 = (f32[8,1152]{1,0:T(8,128)S(1)}, f32[8,1152]{1,0:T(8,128)S(1)}, u32[]{:S(2)}, u32[]{:S(2)}) collective-permute-start(f32[8,1152]{1,0:T(8,128)S(1)} %get-tuple-element.54), channel_id=1, source_target_pairs={{0,24},{8,0},{16,8},{24,16},{1,25},{9,1},{17,9},{25,17},{2,26},{10... | collective-permute-start | bytes 110600 | tf_op jit(solution)/shard_map/ppermute | solution.py:132
  118.9 5.4 %collective-permute-start.19 = (f32[4,8,1152]{2,1,0:T(8,128)S(1)}, f32[4,8,1152]{2,1,0:T(8,128)S(1)}, u32[]{:S(2)}, u32[]{:S(2)}) collective-permute-start(f32[4,8,1152]{2,1,0:T(8,128)S(1)} %all_to_all.38.refs_0_), channel_id=1, source_target_pairs={{0,4},{4,0},{1,5},{5,1},{2,6},{6,2},{3,7},{7,3},{8,12},{12,8},{9,1... | collective-permute-start | bytes 442376 | tf_op jit(solution)/shard_map/ppermute | solution.py:123
  127.1 5.6 %collective-permute-start.20 = (bf16[64,832]{1,0:T(8,128)(2,1)S(1)}, bf16[64,832]{1,0:T(8,128)(2,1)S(1)}, u32[]{:S(2)}, u32[]{:S(2)}) collective-permute-start(bf16[64,832]{1,0:T(8,128)(2,1)S(1)} %get-tuple-element.57), channel_id=1, source_target_pairs={{0,1},{1,2},{2,3},{3,0},{4,5},{5,6},{6,7},{7,4},{8,9},{9,10},{10,1... | collective-permute-start | bytes 319496 | tf_op jit(solution)/shard_map/ppermute | solution.py:127
  128.1 7.5 %collective-permute-start.21 = (bf16[64,832]{1,0:T(8,128)(2,1)S(1)}, bf16[64,832]{1,0:T(8,128)(2,1)S(1)}, u32[]{:S(2)}, u32[]{:S(2)}) collective-permute-start(bf16[64,832]{1,0:T(8,128)(2,1)S(1)} %get-tuple-element.57), channel_id=1, source_target_pairs={{0,2},{1,3},{2,0},{3,1},{4,6},{5,7},{6,4},{7,5},{8,10},{9,11},{10,... | collective-permute-start | bytes 319496 | tf_op jit(solution)/shard_map/ppermute | solution.py:127
  130.3 5.4 %collective-permute-start.22 = (bf16[64,832]{1,0:T(8,128)(2,1)S(1)}, bf16[64,832]{1,0:T(8,128)(2,1)S(1)}, u32[]{:S(2)}, u32[]{:S(2)}) collective-permute-start(bf16[64,832]{1,0:T(8,128)(2,1)S(1)} %get-tuple-element.57), channel_id=1, source_target_pairs={{0,3},{1,0},{2,1},{3,2},{4,7},{5,4},{6,5},{7,6},{8,11},{9,8},{10,9... | collective-permute-start | bytes 319496 | tf_op jit(solution)/shard_map/ppermute | solution.py:127
  139.0 2.4 %collective-permute-start.23 = (f32[32,1152]{1,0:T(8,128)S(1)}, f32[32,1152]{1,0:T(8,128)S(1)}, u32[]{:S(2)}, u32[]{:S(2)}) collective-permute-start(f32[32,1152]{1,0:T(8,128)S(1)} %get-tuple-element.60), channel_id=1, source_target_pairs={{0,4},{4,0},{1,5},{5,1},{2,6},{6,2},{3,7},{7,3},{8,12},{12,8},{9,1... | collective-permute-start | bytes 442376 | tf_op jit(solution)/shard_map/ppermute | solution.py:123
  141.4 4.1 %collective-permute-start.24 = (f32[8,1152]{1,0:T(8,128)S(1)}, f32[8,1152]{1,0:T(8,128)S(1)}, u32[]{:S(2)}, u32[]{:S(2)}) collective-permute-start(f32[8,1152]{1,0:T(8,128)S(1)} %get-tuple-element.62), channel_id=1, source_target_pairs={{0,8},{8,16},{16,24},{24,0},{1,9},{9,17},{17,25},{25,1},{2,10},{10... | collective-permute-start | bytes 110600 | tf_op jit(solution)/shard_map/ppermute | solution.py:132
  141.7 4.4 %collective-permute-start.25 = (f32[8,1152]{1,0:T(8,128)S(1)}, f32[8,1152]{1,0:T(8,128)S(1)}, u32[]{:S(2)}, u32[]{:S(2)}) collective-permute-start(f32[8,1152]{1,0:T(8,128)S(1)} %get-tuple-element.63), channel_id=1, source_target_pairs={{0,16},{8,24},{16,0},{24,8},{1,17},{9,25},{17,1},{25,9},{2,18},{10... | collective-permute-start | bytes 110600 | tf_op jit(solution)/shard_map/ppermute | solution.py:132
  143.5 3.2 %collective-permute-start.26 = (f32[8,1152]{1,0:T(8,128)S(1)}, f32[8,1152]{1,0:T(8,128)S(1)}, u32[]{:S(2)}, u32[]{:S(2)}) collective-permute-start(f32[8,1152]{1,0:T(8,128)S(1)} %get-tuple-element.64), channel_id=1, source_target_pairs={{0,24},{8,0},{16,8},{24,16},{1,25},{9,1},{17,9},{25,17},{2,26},{10... | collective-permute-start | bytes 110600 | tf_op jit(solution)/shard_map/ppermute | solution.py:132
  165.7 5.4 %collective-permute-start.27 = (f32[4,8,1152]{2,1,0:T(8,128)S(1)}, f32[4,8,1152]{2,1,0:T(8,128)S(1)}, u32[]{:S(2)}, u32[]{:S(2)}) collective-permute-start(f32[4,8,1152]{2,1,0:T(8,128)S(1)} %all_to_all.40.refs_0_), channel_id=1, source_target_pairs={{0,4},{4,0},{1,5},{5,1},{2,6},{6,2},{3,7},{7,3},{8,12},{12,8},{9,1... | collective-permute-start | bytes 442376 | tf_op jit(solution)/shard_map/ppermute | solution.py:123

commit v2 on v1

--- a/solution.py
+++ b/solution.py
@@ -14,6 +14,7 @@
 LANES = 128
 SUB = 8
 GROUP = 32
+SHIFTS = (2, 1, 3)
 F32 = jnp.float32
 BF16 = jnp.bfloat16
 HIGH = lax.Precision.HIGHEST
@@ -125,7 +126,7 @@
     def snp_others(value):
         return [
             lax.ppermute(value, "snp", [(i, (i + k) % snp) for i in range(snp)])
-            for k in range(1, snp)
+            for k in SHIFTS
         ]
 
     def x_shift(value, k):
@@ -385,7 +386,7 @@
             own, *sends = call_with_place(
                 split_kernel, (tile_shape,) * ring, mine, swap(other)
             )
-            gots = [x_shift(send, k) for k, send in enumerate(sends, 1)]
+            gots = [x_shift(sends[k - 1], k) for k in ((1, 3, 2) if dtype == F32 else SHIFTS)]
             wide = sum_width if dtype == F32 else col_width + 2 * LANES
             spread = call_with_place(
                 spread_kernel, shape_of((depth, SUB, wide), dtype), own, *gots
@@ -415,7 +416,7 @@
             samples = own[...] + a[...] + b[...] + c[...]
             batch = batch_ids(place, sizes, (1, row_count), 1)
             weight = weight_rows(scale, left)
-            for k, q in enumerate((q0, q1, q2, q3)):
+            for k, q in zip((0, *SHIFTS), (q0, q1, q2, q3)):
                 source = (place[0] + (snp - k)) % snp
                 masked = [
                     jnp.where(gone_in(bits[source * local_blocks + j], batch), weight, 0.0)

time: 175 us -> 175 us (level)
  blocking collectives: 59.7 us -> 61.5 us
    ppermute x9, waiting for transfers between devices: 8.1 us -> 5.42 us  [x_shift(): return lax.ppermute(value, 'x', [(i, (i + k) % ring) for i in range(ring)])]
    ppermute x9, starting transfers between devices: 8.49 us -> 10.9 us  [x_shift(): return lax.ppermute(value, 'x', [(i, (i + k) % ring) for i in range(ring)])]
    all_to_all x3, blocking collectives: 24.2 us -> 26.1 us  [samp_sum(): near = lax.all_to_all(tiles, 'x', 0, 0)]
    ppermute x12, waiting for transfers between devices: 9.9 us -> 11.8 us  [snp_others(): lax.ppermute(value, 'snp', [(i, (i + k) % snp) for i in range(snp)])]
  transfers between devices with their start and end apart: 29 -> 29, of which waited for: 21 -> 18; matrix products, arithmetic and copies ran while one was open for 0% -> 0% of each run, Pallas kernels for 4% -> 4%
where the time goes in v2:
time: 175 us
  blocking collectives  61.5 us (35%)
  starting transfers between devices  59.5 us (34%)
  Pallas kernels  25.6 us (15%)
  waiting for transfers between devices  24.7 us (14%)
  local copies, waits for them, and re-layouts  2.69 us (2%)
    all_to_all x3, blocking collectives, samp_sum(): lax.all_to_all(spread, 'z', 0, 0)  35.3 us
    all_to_all x3, blocking collectives, samp_sum(): near = lax.all_to_all(tiles, 'x', 0, 0)  26.1 us
    pallas_call x18, Pallas kernels, call_with_place(): pl.pallas_call(body, out_shape=outs, in_specs=specs, scratch_shapes=scrat...  22.4 us
    ppermute x7, starting transfers between devices, swap(): return lax.ppermute(value, 'core', [(0, 1), (1, 0)])  21.5 us
    ppermute x12, starting transfers between devices, snp_others(): lax.ppermute(value, 'snp', [(i, (i + k) % snp) for i in range(snp)])  17.8 us
    ppermute x12, waiting for transfers between devices, snp_others(): lax.ppermute(value, 'snp', [(i, (i + k) % snp) for i in range(snp)])  11.8 us
    ppermute x9, starting transfers between devices, x_shift(): return lax.ppermute(value, 'x', [(i, (i + k) % ring) for i in range(ring)])  10.9 us
    all_to_all x1, starting transfers between devices, on_device(): lax.all_to_all(call_with_place(pack_kernel, shape_of((chips, SUB, LANES))...  9.3 us
  transfers between devices with their start and end apart: 29, of which 18 were waited for; matrix products, arithmetic and copies ran while one was open for 0% of the time, Pallas kernels for 4%

profile of v2, /device:TPU:1, one launch (start us, length us, event | category | flops | bytes accessed | tf_op | source)
XLA Modules:
  0.0 174.7 jit_solution(12083114064493902327)
XLA Ops:
  0.6 3.3 %collective-permute-start.3 = (f32[16,20]{1,0:T(8,128)}, f32[16,20]{1,0:T(8,128)S(1)}, u32[]{:S(2)}, u32[]{:S(2)}) collective-permute-start(f32[16,20]{1,0:T(8,128)} %mine.1), channel_id=1, source_target_pairs={{0,4},{4,0},{1,5},{5,1},{2,6},{6,2},{3,7},{7,3},{8,12},{12,8},{9,1... | collective-permute-start | bytes 3848 | tf_op jit(solution)/shard_map/ppermute | solution.py:124
  4.0 1.0 collective-permute-done.3.other
  5.0 0.7 copy-done.4
  5.7 0.7 shard_map.113
  6.4 9.3 %all-to-all-start = ((f32[32,8,128]{2,1,0:T(8,128)}), f32[32,8,128]{2,1,0:T(8,128)S(1)}, u32[]{:S(2)}, u32[]{:S(2)}) async-start(f32[32,8,128]{2,1,0:T(8,128)} %shard_map.113), calls=%async_computation | async-start | bytes 262144 | tf_op jit(solution)/shard_map/all_to_all | solution.py:280
  15.8 3.2 %shard_map.112 = (bf16[640,1024]{1,0:T(8,128)(2,1)}, f32[64,640]{1,0:T(8,128)}, s32[16]{0:T(128)}) custom-call(s32[1]{0:T(128)} %bitcast.place, s32[12]{0:T(128)} %sizes.3, s32[48]{0:T(128)} %batch_in.1, s32[48]{0:T(128)} %block_in.1, s32[640,1024]{1,0:T(8,128)} %geno_in.1, f32[1,1024]{1,0:T(1,128)} %bitcast.11, bf16[64,1024]{1,0:T(8,128)(2,1)} %bitcast.7), custom_call_target="tpu_custom_call" | custom-call | tf_op jit(solution)/shard_map/pallas_call | solution.py:239
  19.0 3.0 %collective-permute-start = (f32[64,640]{1,0:T(8,128)}, f32[64,640]{1,0:T(8,128)S(1)}, u32[]{:S(2)}, u32[]{:S(2)}) collective-permute-start(f32[64,640]{1,0:T(8,128)} %get-tuple-element.37.own), channel_id=1, source_target_pairs={{0,2},{1,3},{2,0},{3,1},{4,6},{5,7},{6,4},{7,5},{8,10},{9,11},{10,... | collective-permute-start | bytes 491528 | tf_op jit(solution)/shard_map/ppermute | solution.py:128
  22.4 2.3 %collective-permute-start.2 = (f32[64,640]{1,0:T(8,128)}, f32[64,640]{1,0:T(8,128)S(1)}, u32[]{:S(2)}, u32[]{:S(2)}) collective-permute-start(f32[64,640]{1,0:T(8,128)} %get-tuple-element.37.own), channel_id=1, source_target_pairs={{0,3},{1,0},{2,1},{3,2},{4,7},{5,4},{6,5},{7,6},{8,11},{9,8},{10,9... | collective-permute-start | bytes 491528 | tf_op jit(solution)/shard_map/ppermute | solution.py:128
  24.7 0.4 all-to-all-done.tiles
  25.1 0.5 shard_map.114.q0
  25.6 3.0 %collective-permute-start.4 = (f32[64,128]{1,0:T(8,128)S(1)}, f32[64,128]{1,0:T(8,128)S(1)}, u32[]{:S(2)}, u32[]{:S(2)}) collective-permute-start(f32[64,128]{1,0:T(8,128)S(1)} %shard_map.114.q0), channel_id=1, source_target_pairs={{0,2},{1,3},{2,0},{3,1},{4,6},{5,7},{6,4},{7,5},{8,10},{9,11},{10,... | collective-permute-start | bytes 98312 | tf_op jit(solution)/shard_map/ppermute | solution.py:128
  29.0 2.3 %collective-permute-start.6 = (f32[64,128]{1,0:T(8,128)S(1)}, f32[64,128]{1,0:T(8,128)S(1)}, u32[]{:S(2)}, u32[]{:S(2)}) collective-permute-start(f32[64,128]{1,0:T(8,128)S(1)} %shard_map.114.q0), channel_id=1, source_target_pairs={{0,3},{1,0},{2,1},{3,2},{4,7},{5,4},{6,5},{7,6},{8,11},{9,8},{10,9... | collective-permute-start | bytes 98312 | tf_op jit(solution)/shard_map/ppermute | solution.py:128
  31.3 1.3 copy-done
  32.6 0.7 copy-done.7
  33.3 2.9 %shard_map.115.x.refs_2_ = bf16[640,1024]{1,0:T(8,128)(2,1)S(1)} custom-call(s32[1]{0:T(128)} %bitcast.place, s32[12]{0:T(128)S(1)} %copy-done.5, s32[16]{0:T(128)S(1)} %copy-done.7, f32[20]{0:T(128)S(1)} %copy-done.6, bf16[640,1024]{1,0:T(8,128)(2,1)S(1)} %copy-done, f32[20,640]{1,0:T(8,128)S(1)} %bitcast.9, f32[32,8,128]{2,1,0:T(8,128)S(1)} %all-to-all-done.tiles), custom_call_target="tpu_custom_call" | custom-call | tf_op jit(solution)/shard_map/pallas_call | solution.py:166
  36.3 2.2 %shard_map.116 = (f32[64,640]{1,0:T(8,128)}, f32[32,1152]{1,0:T(8,128)S(1)}, f32[32,1152]{1,0:T(8,128)S(1)}) custom-call(s32[1]{0:T(128)} %bitcast.place, s32[12]{0:T(128)S(1)} %copy-done.5, s32[16]{0:T(128)S(1)} %copy-done.7, f32[20]{0:T(128)S(1)} %copy-done.6, f32[64,640]{1,0:T(8,128)S(1)} %copy-done.3, f32[64,640]{1,0:T(8,128)S(1)} %collective-permute-done.a, ...), custom_call_target="tpu_custom_call" | custom-call | tf_op jit(solution)/shard_map/pallas_call | solution.py:166
  38.5 2.9 %collective-permute-start.7 = (f32[32,1152]{1,0:T(8,128)S(1)}, f32[32,1152]{1,0:T(8,128)S(1)}, u32[]{:S(2)}, u32[]{:S(2)}) collective-permute-start(f32[32,1152]{1,0:T(8,128)S(1)} %get-tuple-element.40), channel_id=1, source_target_pairs={{0,4},{4,0},{1,5},{5,1},{2,6},{6,2},{3,7},{7,3},{8,12},{12,8},{9,1... | collective-permute-start | bytes 442376 | tf_op jit(solution)/shard_map/ppermute | solution.py:124
  41.4 1.0 collective-permute-done.7.got
  42.4 1.0 collective-permute-start.10
  43.5 0.6 collective-permute-start.8
  44.1 2.1 %collective-permute-start.9 = (f32[8,1152]{1,0:T(8,128)S(1)}, f32[8,1152]{1,0:T(8,128)S(1)}, u32[]{:S(2)}, u32[]{:S(2)}) collective-permute-start(f32[8,1152]{1,0:T(8,128)S(1)} %get-tuple-element.43), channel_id=1, source_target_pairs={{0,24},{8,0},{16,8},{24,16},{1,25},{9,1},{17,9},{25,17},{2,26},{10... | collective-permute-start | bytes 110600 | tf_op jit(solution)/shard_map/ppermute | solution.py:133
  46.1 0.7 collective-permute-done.10.c
  46.8 1.1 collective-permute-done.8.a
  48.0 14.5 %all_to_all.35.parts = f32[8,8,1152]{2,1,0:T(8,128)S(1)} all-to-all(f32[8,8,1152]{2,1,0:T(8,128)S(1)} %shard_map.118), channel_id=1, replica_groups=mesh['z'=8,'x'=4,'core'=2,'snp'=4] {'z'}, dimensions={0} | all-to-all | bytes 589824 | tf_op jit(solution)/shard_map/all_to_all | solution.py:397
  62.5 9.1 %all_to_all.36.refs_0_ = f32[4,8,1152]{2,1,0:T(8,128)S(1)} all-to-all(f32[4,8,1152]{2,1,0:T(8,128)S(1)} %shard_map.119), channel_id=1, replica_groups=mesh['z'=8,'x'=4,'core'=2,'snp'=4] {'x'}, dimensions={0} | all-to-all | bytes 294912 | tf_op jit(solution)/shard_map/all_to_all | solution.py:399
  71.6 5.2 %collective-permute-start.11 = (f32[4,8,1152]{2,1,0:T(8,128)S(1)}, f32[4,8,1152]{2,1,0:T(8,128)S(1)}, u32[]{:S(2)}, u32[]{:S(2)}) collective-permute-start(f32[4,8,1152]{2,1,0:T(8,128)S(1)} %all_to_all.36.refs_0_), channel_id=1, source_target_pairs={{0,4},{4,0},{1,5},{5,1},{2,6},{6,2},{3,7},{7,3},{8,12},{12,8},{9,1... | collective-permute-start | bytes 442376 | tf_op jit(solution)/shard_map/ppermute | solution.py:124
  76.8 1.0 collective-permute-done.11.refs_1_
  77.8 2.9 %shard_map.120 = (f32[64,1024]{1,0:T(8,128)S(1)}, f32[64,640]{1,0:T(8,128)S(1)}, f32[64,64]{1,0:T(8,128)S(1)}, bf16[64,832]{1,0:T(8,128)(2,1)S(1)}) custom-call(s32[1]{0:T(128)} %bitcast.place, f32[4,8,1152]{2,1,0:T(8,128)S(1)} %all_to_all.36.refs_0_, f32[4,8,1152]{2,1,0:T(8,128)S(1)} %collective-permute-done.11.refs_1_, ...), custom_call_target="tpu_custom_call" | custom-call | tf_op jit(solution)/shard_map/pallas_call | solution.py:166
  80.6 0.5 collective-permute-start.12
  81.2 0.6 collective-permute-start.13
  81.7 2.1 %collective-permute-start.14 = (bf16[64,832]{1,0:T(8,128)(2,1)S(1)}, bf16[64,832]{1,0:T(8,128)(2,1)S(1)}, u32[]{:S(2)}, u32[]{:S(2)}) collective-permute-start(bf16[64,832]{1,0:T(8,128)(2,1)S(1)} %get-tuple-element.47), channel_id=1, source_target_pairs={{0,3},{1,0},{2,1},{3,2},{4,7},{5,4},{6,5},{7,6},{8,11},{9,8},{10,9... | collective-permute-start | bytes 319496 | tf_op jit(solution)/shard_map/ppermute | solution.py:128
  83.8 2.7 %collective-permute-done.12.a = bf16[64,832]{1,0:T(8,128)(2,1)S(1)} collective-permute-done((bf16[64,832]{1,0:T(8,128)(2,1)S(1)}, bf16[64,832]{1,0:T(8,128)(2,1)S(1)}, u32[]{:S(2)}, u32[]{:S(2)}) %collective-permute-start.12) | collective-permute-done | bytes 106528 | tf_op jit(solution)/shard_map/ppermute | solution.py:128
  86.6 3.2 %collective-permute-done.13.b = bf16[64,832]{1,0:T(8,128)(2,1)S(1)} collective-permute-done((bf16[64,832]{1,0:T(8,128)(2,1)S(1)}, bf16[64,832]{1,0:T(8,128)(2,1)S(1)}, u32[]{:S(2)}, u32[]{:S(2)}) %collective-permute-start.13) | collective-permute-done | bytes 106528 | tf_op jit(solution)/shard_map/ppermute | solution.py:128
  89.7 3.4 %shard_map.121 = (f32[64,640]{1,0:T(8,128)}, f32[64,1024]{1,0:T(8,128)}, f32[32,1152]{1,0:T(8,128)S(1)}, f32[32,1152]{1,0:T(8,128)S(1)}) custom-call(s32[1]{0:T(128)} %bitcast.place, f32[64,640]{1,0:T(8,128)S(1)} %get-tuple-element.45.product, f32[64,64]{1,0:T(8,128)S(1)} %get-tuple-element.46.gram, bf16[64,832]{1,0:T(8,128)(2,1)S(1)} %collective-permute-done.12.a, ...), custom_call_target="tpu_custom_call" | custom-call | tf_op jit(solution)/shard_map/pallas_call | solution.py:166
  93.1 0.5 collective-permute-start.15
  93.6 1.0 collective-permute-done.15.got
  94.6 0.9 collective-permute-start.16
  95.6 0.6 collective-permute-start.17
  96.2 2.1 %collective-permute-start.18 = (f32[8,1152]{1,0:T(8,128)S(1)}, f32[8,1152]{1,0:T(8,128)S(1)}, u32[]{:S(2)}, u32[]{:S(2)}) collective-permute-start(f32[8,1152]{1,0:T(8,128)S(1)} %get-tuple-element.54), channel_id=1, source_target_pairs={{0,24},{8,0},{16,8},{24,16},{1,25},{9,1},{17,9},{25,17},{2,26},{10... | collective-permute-start | bytes 110600 | tf_op jit(solution)/shard_map/ppermute | solution.py:133
  98.2 0.8 collective-permute-done.16.a
  99.0 1.0 collective-permute-done.17.b
  100.1 10.4 %all_to_all.37.parts = bf16[8,8,1280]{2,1,0:T(8,128)(2,1)S(1)} all-to-all(bf16[8,8,1280]{2,1,0:T(8,128)(2,1)S(1)} %shard_map.123), channel_id=1, replica_groups=mesh['z'=8,'x'=4,'core'=2,'snp'=4] {'z'}, dimensions={0} | all-to-all | bytes 327680 | tf_op jit(solution)/shard_map/all_to_all | solution.py:397
  110.7 8.5 %all_to_all.38.refs_0_ = f32[4,8,1152]{2,1,0:T(8,128)S(1)} all-to-all(f32[4,8,1152]{2,1,0:T(8,128)S(1)} %shard_map.124), channel_id=1, replica_groups=mesh['z'=8,'x'=4,'core'=2,'snp'=4] {'x'}, dimensions={0} | all-to-all | bytes 294912 | tf_op jit(solution)/shard_map/all_to_all | solution.py:399
  119.2 4.6 %collective-permute-start.19 = (f32[4,8,1152]{2,1,0:T(8,128)S(1)}, f32[4,8,1152]{2,1,0:T(8,128)S(1)}, u32[]{:S(2)}, u32[]{:S(2)}) collective-permute-start(f32[4,8,1152]{2,1,0:T(8,128)S(1)} %all_to_all.38.refs_0_), channel_id=1, source_target_pairs={{0,4},{4,0},{1,5},{5,1},{2,6},{6,2},{3,7},{7,3},{8,12},{12,8},{9,1... | collective-permute-start | bytes 442376 | tf_op jit(solution)/shard_map/ppermute | solution.py:124
  123.8 1.0 collective-permute-done.19.refs_1_
  124.8 2.9 %shard_map.125 = (f32[64,1024]{1,0:T(8,128)S(1)}, f32[64,640]{1,0:T(8,128)S(1)}, f32[64,64]{1,0:T(8,128)S(1)}, bf16[64,832]{1,0:T(8,128)(2,1)S(1)}) custom-call(s32[1]{0:T(128)} %bitcast.place, f32[4,8,1152]{2,1,0:T(8,128)S(1)} %all_to_all.38.refs_0_, f32[4,8,1152]{2,1,0:T(8,128)S(1)} %collective-permute-done.19.refs_1_, ...), custom_call_target="tpu_custom_call" | custom-call | tf_op jit(solution)/shard_map/pallas_call | solution.py:166
  127.7 0.5 collective-permute-start.20
  128.2 0.9 collective-permute-start.21
  129.1 1.7 collective-permute-start.22
  130.9 2.7 %collective-permute-done.20.a = bf16[64,832]{1,0:T(8,128)(2,1)S(1)} collective-permute-done((bf16[64,832]{1,0:T(8,128)(2,1)S(1)}, bf16[64,832]{1,0:T(8,128)(2,1)S(1)}, u32[]{:S(2)}, u32[]{:S(2)}) %collective-permute-start.20) | collective-permute-done | bytes 106528 | tf_op jit(solution)/shard_map/ppermute | solution.py:128
  133.6 3.2 %collective-permute-done.21.b = bf16[64,832]{1,0:T(8,128)(2,1)S(1)} collective-permute-done((bf16[64,832]{1,0:T(8,128)(2,1)S(1)}, bf16[64,832]{1,0:T(8,128)(2,1)S(1)}, u32[]{:S(2)}, u32[]{:S(2)}) %collective-permute-start.21) | collective-permute-done | bytes 106528 | tf_op jit(solution)/shard_map/ppermute | solution.py:128
  136.8 3.3 %shard_map.126 = (f32[64,640]{1,0:T(8,128)S(1)}, f32[64,1024]{1,0:T(8,128)}, f32[32,1152]{1,0:T(8,128)S(1)}, f32[32,1152]{1,0:T(8,128)S(1)}) custom-call(s32[1]{0:T(128)} %bitcast.place, f32[64,640]{1,0:T(8,128)S(1)} %get-tuple-element.55.product, f32[64,64]{1,0:T(8,128)S(1)} %get-tuple-element.56.gram, bf16[64,832]{1,0:T(8,128)(2,1)S(1)} %collective-permute-done.20.a, ...), custom_call_target="tpu_custom_call" | custom-call | tf_op jit(solution)/shard_map/pallas_call | solution.py:166
  140.1 0.5 collective-permute-start.23
  140.6 1.0 collective-permute-done.23.got
  141.6 0.9 collective-permute-start.24
  142.5 0.6 collective-permute-start.25
  143.2 2.1 %collective-permute-start.26 = (f32[8,1152]{1,0:T(8,128)S(1)}, f32[8,1152]{1,0:T(8,128)S(1)}, u32[]{:S(2)}, u32[]{:S(2)}) collective-permute-start(f32[8,1152]{1,0:T(8,128)S(1)} %get-tuple-element.64), channel_id=1, source_target_pairs={{0,24},{8,0},{16,8},{24,16},{1,25},{9,1},{17,9},{25,17},{2,26},{10... | collective-permute-start | bytes 110600 | tf_op jit(solution)/shard_map/ppermute | solution.py:133
  145.2 0.8 collective-permute-done.24.a
  146.0 1.0 collective-permute-done.25.b
  147.1 10.4 %all_to_all.39.parts = bf16[8,8,1280]{2,1,0:T(8,128)(2,1)S(1)} all-to-all(bf16[8,8,1280]{2,1,0:T(8,128)(2,1)S(1)} %shard_map.128), channel_id=1, replica_groups=mesh['z'=8,'x'=4,'core'=2,'snp'=4] {'z'}, dimensions={0} | all-to-all | bytes 327680 | tf_op jit(solution)/shard_map/all_to_all | solution.py:397
  157.7 8.5 %all_to_all.40.refs_0_ = f32[4,8,1152]{2,1,0:T(8,128)S(1)} all-to-all(f32[4,8,1152]{2,1,0:T(8,128)S(1)} %shard_map.129), channel_id=1, replica_groups=mesh['z'=8,'x'=4,'core'=2,'snp'=4] {'x'}, dimensions={0} | all-to-all | bytes 294912 | tf_op jit(solution)/shard_map/all_to_all | solution.py:399
  166.2 4.6 %collective-permute-start.27 = (f32[4,8,1152]{2,1,0:T(8,128)S(1)}, f32[4,8,1152]{2,1,0:T(8,128)S(1)}, u32[]{:S(2)}, u32[]{:S(2)}) collective-permute-start(f32[4,8,1152]{2,1,0:T(8,128)S(1)} %all_to_all.40.refs_0_), channel_id=1, source_target_pairs={{0,4},{4,0},{1,5},{5,1},{2,6},{6,2},{3,7},{7,3},{8,12},{12,8},{9,1... | collective-permute-start | bytes 442376 | tf_op jit(solution)/shard_map/ppermute | solution.py:124
  170.7 1.0 collective-permute-done.27.refs_1_
  171.8 3.0 %shard_map.130 = (f32[64,640]{1,0:T(8,128)}, f32[64,1024]{1,0:T(8,128)}) custom-call(s32[1]{0:T(128)} %bitcast.place, f32[4,8,1152]{2,1,0:T(8,128)S(1)} %all_to_all.40.refs_0_, f32[4,8,1152]{2,1,0:T(8,128)S(1)} %collective-permute-done.27.refs_1_, f32[64,640]{1,0:T(8,128)S(1)} %get-tuple-element.65.refs_2_), custom_call_target="tpu_custom_call" | custom-call | tf_op jit(solution)/shard_map/pallas_call | solution.py:166
  (35 shorter events, 1.4 us)
Async XLA Ops:
  0.6 4.4 %collective-permute-start.3 = (f32[16,20]{1,0:T(8,128)}, f32[16,20]{1,0:T(8,128)S(1)}, u32[]{:S(2)}, u32[]{:S(2)}) collective-permute-start(f32[16,20]{1,0:T(8,128)} %mine.1), channel_id=1, source_target_pairs={{0,4},{4,0},{1,5},{5,1},{2,6},{6,2},{3,7},{7,3},{8,12},{12,8},{9,1... | collective-permute-start | bytes 3848 | tf_op jit(solution)/shard_map/ppermute | solution.py:124
  5.0 0.7 copy-start.4
  6.4 18.7 %all-to-all-start = ((f32[32,8,128]{2,1,0:T(8,128)}), f32[32,8,128]{2,1,0:T(8,128)S(1)}, u32[]{:S(2)}, u32[]{:S(2)}) async-start(f32[32,8,128]{2,1,0:T(8,128)} %shard_map.113), calls=%async_computation | async-start | bytes 262144 | tf_op jit(solution)/shard_map/all_to_all | solution.py:280
  15.7 9.3 %copy-start.1 = (bf16[1024,64]{0,1:T(8,128)(2,1)S(1)}, bf16[1024,64]{0,1:T(8,128)(2,1)}, u32[]{:S(2)}) copy-start(bf16[1024,64]{0,1:T(8,128)(2,1)} %param.14) | copy-start | bytes 393220
  15.8 15.6 %copy-start.2 = (f32[640,20]{0,1:T(8,128)S(1)}, f32[640,20]{0,1:T(8,128)}, u32[]{:S(2)}) copy-start(f32[640,20]{0,1:T(8,128)} %param.11) | copy-start | bytes 153604
  15.8 15.5 %copy-start.5 = (s32[12]{0:T(128)S(1)}, s32[12]{0:T(128)}, u32[]{:S(2)}) copy-start(s32[12]{0:T(128)} %sizes.3) | copy-start | bytes 148
  15.8 15.5 %copy-start.6 = (f32[20]{0:T(128)S(1)}, f32[20]{0:T(128)}, u32[]{:S(2)}) copy-start(f32[20]{0:T(128)} %scale.3) | copy-start | bytes 244
  19.0 10.0 %collective-permute-start = (f32[64,640]{1,0:T(8,128)}, f32[64,640]{1,0:T(8,128)S(1)}, u32[]{:S(2)}, u32[]{:S(2)}) collective-permute-start(f32[64,640]{1,0:T(8,128)} %get-tuple-element.37.own), channel_id=1, source_target_pairs={{0,2},{1,3},{2,0},{3,1},{4,6},{5,7},{6,4},{7,5},{8,10},{9,11},{10,... | collective-permute-start | bytes 491528 | tf_op jit(solution)/shard_map/ppermute | solution.py:128
  22.0 14.2 %collective-permute-start.1 = (f32[64,640]{1,0:T(8,128)}, f32[64,640]{1,0:T(8,128)S(1)}, u32[]{:S(2)}, u32[]{:S(2)}) collective-permute-start(f32[64,640]{1,0:T(8,128)} %get-tuple-element.37.own), channel_id=1, source_target_pairs={{0,1},{1,2},{2,3},{3,0},{4,5},{5,6},{6,7},{7,4},{8,9},{9,10},{10,1... | collective-permute-start | bytes 491528 | tf_op jit(solution)/shard_map/ppermute | solution.py:128
  22.4 13.8 %collective-permute-start.2 = (f32[64,640]{1,0:T(8,128)}, f32[64,640]{1,0:T(8,128)S(1)}, u32[]{:S(2)}, u32[]{:S(2)}) collective-permute-start(f32[64,640]{1,0:T(8,128)} %get-tuple-element.37.own), channel_id=1, source_target_pairs={{0,3},{1,0},{2,1},{3,2},{4,7},{5,4},{6,5},{7,6},{8,11},{9,8},{10,9... | collective-permute-start | bytes 491528 | tf_op jit(solution)/shard_map/ppermute | solution.py:128
  25.6 10.6 %collective-permute-start.4 = (f32[64,128]{1,0:T(8,128)S(1)}, f32[64,128]{1,0:T(8,128)S(1)}, u32[]{:S(2)}, u32[]{:S(2)}) collective-permute-start(f32[64,128]{1,0:T(8,128)S(1)} %shard_map.114.q0), channel_id=1, source_target_pairs={{0,2},{1,3},{2,0},{3,1},{4,6},{5,7},{6,4},{7,5},{8,10},{9,11},{10,... | collective-permute-start | bytes 98312 | tf_op jit(solution)/shard_map/ppermute | solution.py:128
  28.6 7.6 %collective-permute-start.5 = (f32[64,128]{1,0:T(8,128)S(1)}, f32[64,128]{1,0:T(8,128)S(1)}, u32[]{:S(2)}, u32[]{:S(2)}) collective-permute-start(f32[64,128]{1,0:T(8,128)S(1)} %shard_map.114.q0), channel_id=1, source_target_pairs={{0,1},{1,2},{2,3},{3,0},{4,5},{5,6},{6,7},{7,4},{8,9},{9,10},{10,1... | collective-permute-start | bytes 98312 | tf_op jit(solution)/shard_map/ppermute | solution.py:128
  29.0 7.2 %collective-permute-start.6 = (f32[64,128]{1,0:T(8,128)S(1)}, f32[64,128]{1,0:T(8,128)S(1)}, u32[]{:S(2)}, u32[]{:S(2)}) collective-permute-start(f32[64,128]{1,0:T(8,128)S(1)} %shard_map.114.q0), channel_id=1, source_target_pairs={{0,3},{1,0},{2,1},{3,2},{4,7},{5,4},{6,5},{7,6},{8,11},{9,8},{10,9... | collective-permute-start | bytes 98312 | tf_op jit(solution)/shard_map/ppermute | solution.py:128
  31.3 1.3 copy-start
  32.6 0.7 copy-start.7
  33.3 3.0 %copy-start.3 = (f32[64,640]{1,0:T(8,128)S(1)}, f32[64,640]{1,0:T(8,128)}, u32[]{:S(2)}) copy-start(f32[64,640]{1,0:T(8,128)} %get-tuple-element.37.own) | copy-start | bytes 491524
  38.5 3.9 %collective-permute-start.7 = (f32[32,1152]{1,0:T(8,128)S(1)}, f32[32,1152]{1,0:T(8,128)S(1)}, u32[]{:S(2)}, u32[]{:S(2)}) collective-permute-start(f32[32,1152]{1,0:T(8,128)S(1)} %get-tuple-element.40), channel_id=1, source_target_pairs={{0,4},{4,0},{1,5},{5,1},{2,6},{6,2},{3,7},{7,3},{8,12},{12,8},{9,1... | collective-permute-start | bytes 442376 | tf_op jit(solution)/shard_map/ppermute | solution.py:124
  42.4 4.4 %collective-permute-start.10 = (f32[8,1152]{1,0:T(8,128)S(1)}, f32[8,1152]{1,0:T(8,128)S(1)}, u32[]{:S(2)}, u32[]{:S(2)}) collective-permute-start(f32[8,1152]{1,0:T(8,128)S(1)} %get-tuple-element.44), channel_id=1, source_target_pairs={{0,16},{8,24},{16,0},{24,8},{1,17},{9,25},{17,1},{25,9},{2,18},{10... | collective-permute-start | bytes 110600 | tf_op jit(solution)/shard_map/ppermute | solution.py:133
  43.5 4.5 %collective-permute-start.8 = (f32[8,1152]{1,0:T(8,128)S(1)}, f32[8,1152]{1,0:T(8,128)S(1)}, u32[]{:S(2)}, u32[]{:S(2)}) collective-permute-start(f32[8,1152]{1,0:T(8,128)S(1)} %get-tuple-element.42), channel_id=1, source_target_pairs={{0,8},{8,16},{16,24},{24,0},{1,9},{9,17},{17,25},{25,1},{2,10},{10... | collective-permute-start | bytes 110600 | tf_op jit(solution)/shard_map/ppermute | solution.py:133
  44.1 3.9 %collective-permute-start.9 = (f32[8,1152]{1,0:T(8,128)S(1)}, f32[8,1152]{1,0:T(8,128)S(1)}, u32[]{:S(2)}, u32[]{:S(2)}) collective-permute-start(f32[8,1152]{1,0:T(8,128)S(1)} %get-tuple-element.43), channel_id=1, source_target_pairs={{0,24},{8,0},{16,8},{24,16},{1,25},{9,1},{17,9},{25,17},{2,26},{10... | collective-permute-start | bytes 110600 | tf_op jit(solution)/shard_map/ppermute | solution.py:133
  71.6 6.2 %collective-permute-start.11 = (f32[4,8,1152]{2,1,0:T(8,128)S(1)}, f32[4,8,1152]{2,1,0:T(8,128)S(1)}, u32[]{:S(2)}, u32[]{:S(2)}) collective-permute-start(f32[4,8,1152]{2,1,0:T(8,128)S(1)} %all_to_all.36.refs_0_), channel_id=1, source_target_pairs={{0,4},{4,0},{1,5},{5,1},{2,6},{6,2},{3,7},{7,3},{8,12},{12,8},{9,1... | collective-permute-start | bytes 442376 | tf_op jit(solution)/shard_map/ppermute | solution.py:124
  80.6 5.9 %collective-permute-start.12 = (bf16[64,832]{1,0:T(8,128)(2,1)S(1)}, bf16[64,832]{1,0:T(8,128)(2,1)S(1)}, u32[]{:S(2)}, u32[]{:S(2)}) collective-permute-start(bf16[64,832]{1,0:T(8,128)(2,1)S(1)} %get-tuple-element.47), channel_id=1, source_target_pairs={{0,2},{1,3},{2,0},{3,1},{4,6},{5,7},{6,4},{7,5},{8,10},{9,11},{10,... | collective-permute-start | bytes 319496 | tf_op jit(solution)/shard_map/ppermute | solution.py:128
  81.2 8.6 %collective-permute-start.13 = (bf16[64,832]{1,0:T(8,128)(2,1)S(1)}, bf16[64,832]{1,0:T(8,128)(2,1)S(1)}, u32[]{:S(2)}, u32[]{:S(2)}) collective-permute-start(bf16[64,832]{1,0:T(8,128)(2,1)S(1)} %get-tuple-element.47), channel_id=1, source_target_pairs={{0,1},{1,2},{2,3},{3,0},{4,5},{5,6},{6,7},{7,4},{8,9},{9,10},{10,1... | collective-permute-start | bytes 319496 | tf_op jit(solution)/shard_map/ppermute | solution.py:128
  81.7 8.0 %collective-permute-start.14 = (bf16[64,832]{1,0:T(8,128)(2,1)S(1)}, bf16[64,832]{1,0:T(8,128)(2,1)S(1)}, u32[]{:S(2)}, u32[]{:S(2)}) collective-permute-start(bf16[64,832]{1,0:T(8,128)(2,1)S(1)} %get-tuple-element.47), channel_id=1, source_target_pairs={{0,3},{1,0},{2,1},{3,2},{4,7},{5,4},{6,5},{7,6},{8,11},{9,8},{10,9... | collective-permute-start | bytes 319496 | tf_op jit(solution)/shard_map/ppermute | solution.py:128
  93.1 1.5 collective-permute-start.15
  94.6 4.4 %collective-permute-start.16 = (f32[8,1152]{1,0:T(8,128)S(1)}, f32[8,1152]{1,0:T(8,128)S(1)}, u32[]{:S(2)}, u32[]{:S(2)}) collective-permute-start(f32[8,1152]{1,0:T(8,128)S(1)} %get-tuple-element.52), channel_id=1, source_target_pairs={{0,16},{8,24},{16,0},{24,8},{1,17},{9,25},{17,1},{25,9},{2,18},{10... | collective-permute-start | bytes 110600 | tf_op jit(solution)/shard_map/ppermute | solution.py:133
  95.6 4.5 %collective-permute-start.17 = (f32[8,1152]{1,0:T(8,128)S(1)}, f32[8,1152]{1,0:T(8,128)S(1)}, u32[]{:S(2)}, u32[]{:S(2)}) collective-permute-start(f32[8,1152]{1,0:T(8,128)S(1)} %get-tuple-element.53), channel_id=1, source_target_pairs={{0,8},{8,16},{16,24},{24,0},{1,9},{9,17},{17,25},{25,1},{2,10},{10... | collective-permute-start | bytes 110600 | tf_op jit(solution)/shard_map/ppermute | solution.py:133
  96.2 3.8 %collective-permute-start.18 = (f32[8,1152]{1,0:T(8,128)S(1)}, f32[8,1152]{1,0:T(8,128)S(1)}, u32[]{:S(2)}, u32[]{:S(2)}) collective-permute-start(f32[8,1152]{1,0:T(8,128)S(1)} %get-tuple-element.54), channel_id=1, source_target_pairs={{0,24},{8,0},{16,8},{24,16},{1,25},{9,1},{17,9},{25,17},{2,26},{10... | collective-permute-start | bytes 110600 | tf_op jit(solution)/shard_map/ppermute | solution.py:133
  119.2 5.6 %collective-permute-start.19 = (f32[4,8,1152]{2,1,0:T(8,128)S(1)}, f32[4,8,1152]{2,1,0:T(8,128)S(1)}, u32[]{:S(2)}, u32[]{:S(2)}) collective-permute-start(f32[4,8,1152]{2,1,0:T(8,128)S(1)} %all_to_all.38.refs_0_), channel_id=1, source_target_pairs={{0,4},{4,0},{1,5},{5,1},{2,6},{6,2},{3,7},{7,3},{8,12},{12,8},{9,1... | collective-permute-start | bytes 442376 | tf_op jit(solution)/shard_map/ppermute | solution.py:124
  127.7 5.9 %collective-permute-start.20 = (bf16[64,832]{1,0:T(8,128)(2,1)S(1)}, bf16[64,832]{1,0:T(8,128)(2,1)S(1)}, u32[]{:S(2)}, u32[]{:S(2)}) collective-permute-start(bf16[64,832]{1,0:T(8,128)(2,1)S(1)} %get-tuple-element.57), channel_id=1, source_target_pairs={{0,2},{1,3},{2,0},{3,1},{4,6},{5,7},{6,4},{7,5},{8,10},{9,11},{10,... | collective-permute-start | bytes 319496 | tf_op jit(solution)/shard_map/ppermute | solution.py:128
  128.2 8.6 %collective-permute-start.21 = (bf16[64,832]{1,0:T(8,128)(2,1)S(1)}, bf16[64,832]{1,0:T(8,128)(2,1)S(1)}, u32[]{:S(2)}, u32[]{:S(2)}) collective-permute-start(bf16[64,832]{1,0:T(8,128)(2,1)S(1)} %get-tuple-element.57), channel_id=1, source_target_pairs={{0,1},{1,2},{2,3},{3,0},{4,5},{5,6},{6,7},{7,4},{8,9},{9,10},{10,1... | collective-permute-start | bytes 319496 | tf_op jit(solution)/shard_map/ppermute | solution.py:128
  129.1 7.6 %collective-permute-start.22 = (bf16[64,832]{1,0:T(8,128)(2,1)S(1)}, bf16[64,832]{1,0:T(8,128)(2,1)S(1)}, u32[]{:S(2)}, u32[]{:S(2)}) collective-permute-start(bf16[64,832]{1,0:T(8,128)(2,1)S(1)} %get-tuple-element.57), channel_id=1, source_target_pairs={{0,3},{1,0},{2,1},{3,2},{4,7},{5,4},{6,5},{7,6},{8,11},{9,8},{10,9... | collective-permute-start | bytes 319496 | tf_op jit(solution)/shard_map/ppermute | solution.py:128
  140.1 1.5 collective-permute-start.23
  141.6 4.4 %collective-permute-start.24 = (f32[8,1152]{1,0:T(8,128)S(1)}, f32[8,1152]{1,0:T(8,128)S(1)}, u32[]{:S(2)}, u32[]{:S(2)}) collective-permute-start(f32[8,1152]{1,0:T(8,128)S(1)} %get-tuple-element.62), channel_id=1, source_target_pairs={{0,16},{8,24},{16,0},{24,8},{1,17},{9,25},{17,1},{25,9},{2,18},{10... | collective-permute-start | bytes 110600 | tf_op jit(solution)/shard_map/ppermute | solution.py:133
  142.5 4.5 %collective-permute-start.25 = (f32[8,1152]{1,0:T(8,128)S(1)}, f32[8,1152]{1,0:T(8,128)S(1)}, u32[]{:S(2)}, u32[]{:S(2)}) collective-permute-start(f32[8,1152]{1,0:T(8,128)S(1)} %get-tuple-element.63), channel_id=1, source_target_pairs={{0,8},{8,16},{16,24},{24,0},{1,9},{9,17},{17,25},{25,1},{2,10},{10... | collective-permute-start | bytes 110600 | tf_op jit(solution)/shard_map/ppermute | solution.py:133
  143.2 3.9 %collective-permute-start.26 = (f32[8,1152]{1,0:T(8,128)S(1)}, f32[8,1152]{1,0:T(8,128)S(1)}, u32[]{:S(2)}, u32[]{:S(2)}) collective-permute-start(f32[8,1152]{1,0:T(8,128)S(1)} %get-tuple-element.64), channel_id=1, source_target_pairs={{0,24},{8,0},{16,8},{24,16},{1,25},{9,1},{17,9},{25,17},{2,26},{10... | collective-permute-start | bytes 110600 | tf_op jit(solution)/shard_map/ppermute | solution.py:133
  166.2 5.6 %collective-permute-start.27 = (f32[4,8,1152]{2,1,0:T(8,128)S(1)}, f32[4,8,1152]{2,1,0:T(8,128)S(1)}, u32[]{:S(2)}, u32[]{:S(2)}) collective-permute-start(f32[4,8,1152]{2,1,0:T(8,128)S(1)} %all_to_all.40.refs_0_), channel_id=1, source_target_pairs={{0,4},{4,0},{1,5},{5,1},{2,6},{6,2},{3,7},{7,3},{8,12},{12,8},{9,1... | collective-permute-start | bytes 442376 | tf_op jit(solution)/shard_map/ppermute | solution.py:124

commit v3 on v2

--- a/solution.py
+++ b/solution.py
@@ -380,7 +380,7 @@
                     ],
                     axis=1,
                 )
-            out[...] = jnp.broadcast_to(total[None], out.shape)
+            out[...] = total
 
         def samp_sum(mine, other, dtype):
             own, *sends = call_with_place(
@@ -391,20 +391,18 @@
             spread = call_with_place(
                 spread_kernel, shape_of((depth, SUB, wide), dtype), own, *gots
             )
-            tiles = call_with_place(
-                gather_kernel,
-                shape_of((ring, *tile_shape.shape)),
-                lax.all_to_all(spread, "z", 0, 0),
-            )
-            near = lax.all_to_all(tiles, "x", 0, 0)
-            return [near, swap(near)]
+            tile = call_with_place(
+                gather_kernel, tile_shape, lax.all_to_all(spread, "z", 0, 0)
+            )
+            near = [tile] + [x_shift(tile, k) for k in SHIFTS]
+            return (*near, *[swap(value) for value in near])
 
         def read_sum(place, tiles, whole):
-            half = width // 2
-            for side, ref in zip((core_of(place), 1 - core_of(place)), tiles):
-                whole[pl.ds(pl.multiple_of(side * half, half), half), :] = ref[...].reshape(
-                    half, sum_width
-                )
+            for n, ref in enumerate(tiles):
+                side = core_of(place) if n < ring else 1 - core_of(place)
+                back = ring - (0, *SHIFTS)[n % ring]
+                tile = side * ring + (x_of(place) + back) % ring
+                whole[pl.ds(pl.multiple_of(tile * SUB, SUB), SUB), :] = ref[...]
             return whole[:, :col_width], whole[:, col_width : col_width + width]
 
         whole_scratch = [pltpu.VMEM((width, sum_width), F32)]
@@ -433,7 +431,7 @@
             )
 
         def forward_kernel(place, *refs):
-            tiles, (x, raw_out, product_out, gram_out, wire, whole) = refs[:2], refs[2:]
+            tiles, (x, raw_out, product_out, gram_out, wire, whole) = refs[: 2 * ring], refs[2 * ring :]
             columns, gram = read_sum(place, tiles, whole)
             raw = exact_dot(inverse_factor(gram / sample_count, True), columns, 1, 0)
             raw_out[...] = raw
@@ -467,7 +465,7 @@
             )
 
         def last_kernel(place, *refs):
-            tiles, (samples, basis, projection, whole) = refs[:2], refs[2:]
+            tiles, (samples, basis, projection, whole) = refs[: 2 * ring], refs[2 * ring :]
             columns, gram = read_sum(place, tiles, whole)
             factor = inverse_factor(gram / sample_count, True)
             basis[...] = exact_dot(factor, samples[...], 1, 0)
@@ -486,8 +484,7 @@
             matrix,
             scalars=(batch_sizes, bits, singular),
         )
-        columns, dtype = None, F32
-        for _ in range(ITERS):
+        def sweep(index, carry):
             raw, product, gram, wire = call_with_place(
                 forward_kernel,
                 (
@@ -496,11 +493,10 @@
                     shape_of((width, width)),
                     shape_of((width, packed), BF16),
                 ),
-                *samp_sum(mine, other, dtype),
+                *carry[0],
                 matrix,
                 scratch=whole_scratch,
             )
-            dtype = BF16
             samples, columns, mine, other = call_with_place(
                 backward_kernel,
                 (samples_shape, columns_shape, part_shape, part_shape),
@@ -510,10 +506,18 @@
                 raw,
                 matrix,
             )
+            return samp_sum(mine, other, BF16), samples, columns
+
+        tiles, samples, columns = lax.fori_loop(
+            0,
+            ITERS,
+            sweep,
+            (samp_sum(mine, other, F32), samples, jnp.zeros(columns_shape.shape, F32)),
+        )
         basis, projection = call_with_place(
             last_kernel,
             (samples_shape, columns_shape),
-            *samp_sum(mine, other, dtype),
+            *tiles,
             samples,
             scratch=whole_scratch,
         )

time: 175 us -> 169 us (0.966)
  blocking collectives: 61.5 us -> 35 us
  starting transfers between devices: 59.5 us -> 75.4 us
  waiting for transfers between devices: 24.7 us -> 28 us
    all_to_all x3 -> x0, blocking collectives: 26.1 us -> none  [samp_sum(): near = lax.all_to_all(tiles, 'x', 0, 0)]
    ppermute x9 -> x18, starting transfers between devices: 10.9 us -> 21.6 us  [x_shift(): return lax.ppermute(value, 'x', [(i, (i + k) % ring) for i in range(ring)])]
    ppermute x7 -> x16, starting transfers between devices: 21.5 us -> 26.7 us  [swap(): return lax.ppermute(value, 'core', [(0, 1), (1, 0)])]
    ppermute x9 -> x18, waiting for transfers between devices: 5.42 us -> 8.84 us  [x_shift(): return lax.ppermute(value, 'x', [(i, (i + k) % ring) for i in range(ring)])]
    ppermute x7 -> x16, waiting for transfers between devices: 7.08 us -> 6.98 us  [swap(): return lax.ppermute(value, 'core', [(0, 1), (1, 0)])]
  transfers between devices with their start and end apart: 29 -> 47, of which waited for: 18 -> 22; matrix products, arithmetic and copies ran while one was open for 0% -> 0% of each run, Pallas kernels for 4% -> 4%
where the time goes in v3:
time: 169 us
  starting transfers between devices  75.4 us (45%)
  blocking collectives  35 us (21%)
  waiting for transfers between devices  28 us (17%)
  Pallas kernels  26.5 us (16%)
  local copies, waits for them, and re-layouts  2.69 us (2%)
    all_to_all x3, blocking collectives, samp_sum(): lax.all_to_all(spread, 'z', 0, 0)  35 us
    ppermute x16, starting transfers between devices, swap(): return lax.ppermute(value, 'core', [(0, 1), (1, 0)])  26.7 us
    pallas_call x18, Pallas kernels, call_with_place(): pl.pallas_call(body, out_shape=outs, in_specs=specs, scratch_shapes=scrat...  23.3 us
    ppermute x18, starting transfers between devices, x_shift(): return lax.ppermute(value, 'x', [(i, (i + k) % ring) for i in range(ring)])  21.6 us
    ppermute x12, starting transfers between devices, snp_others(): lax.ppermute(value, 'snp', [(i, (i + k) % snp) for i in range(snp)])  17.8 us
    ppermute x12, waiting for transfers between devices, snp_others(): lax.ppermute(value, 'snp', [(i, (i + k) % snp) for i in range(snp)])  11.8 us
    all_to_all x1, starting transfers between devices, on_device(): lax.all_to_all(call_with_place(pack_kernel, shape_of((chips, SUB, LANES))...  9.3 us
    ppermute x18, waiting for transfers between devices, x_shift(): return lax.ppermute(value, 'x', [(i, (i + k) % ring) for i in range(ring)])  8.84 us
  transfers between devices with their start and end apart: 47, of which 22 were waited for; matrix products, arithmetic and copies ran while one was open for 0% of the time, Pallas kernels for 4%

profile of v3, /device:TPU:1, one launch (start us, length us, event | category | flops | bytes accessed | tf_op | source)
XLA Modules:
  0.0 168.5 jit_solution(5164493159511136338)
XLA Ops:
  0.6 3.3 %collective-permute-start.17 = (f32[16,20]{1,0:T(8,128)}, f32[16,20]{1,0:T(8,128)S(1)}, u32[]{:S(2)}, u32[]{:S(2)}) collective-permute-start(f32[16,20]{1,0:T(8,128)} %mine.1), channel_id=1, source_target_pairs={{0,4},{4,0},{1,5},{5,1},{2,6},{6,2},{3,7},{7,3},{8,12},{12,8},{9,1... | collective-permute-start | bytes 3848 | tf_op jit(solution)/shard_map/ppermute | solution.py:124
  4.0 1.0 collective-permute-done.17.other
  5.0 0.7 copy-done.4
  5.7 0.7 shard_map.113
  6.4 9.3 %all-to-all-start.1 = ((f32[32,8,128]{2,1,0:T(8,128)}), f32[32,8,128]{2,1,0:T(8,128)S(1)}, u32[]{:S(2)}, u32[]{:S(2)}) async-start(f32[32,8,128]{2,1,0:T(8,128)} %shard_map.113), calls=%async_computation.1 | async-start | bytes 262144 | tf_op jit(solution)/shard_map/all_to_all | solution.py:280
  15.8 3.2 %shard_map.112 = (bf16[640,1024]{1,0:T(8,128)(2,1)}, f32[64,640]{1,0:T(8,128)}, s32[16]{0:T(128)}) custom-call(s32[1]{0:T(128)} %bitcast.place, s32[12]{0:T(128)} %sizes.3, s32[48]{0:T(128)} %batch_in.1, s32[48]{0:T(128)} %block_in.1, s32[640,1024]{1,0:T(8,128)} %geno_in.1, f32[1,1024]{1,0:T(1,128)} %bitcast.11, bf16[64,1024]{1,0:T(8,128)(2,1)} %bitcast.7), custom_call_target="tpu_custom_call" | custom-call | tf_op jit(solution)/shard_map/pallas_call | solution.py:239
  19.0 3.0 %collective-permute-start.14 = (f32[64,640]{1,0:T(8,128)}, f32[64,640]{1,0:T(8,128)S(1)}, u32[]{:S(2)}, u32[]{:S(2)}) collective-permute-start(f32[64,640]{1,0:T(8,128)} %get-tuple-element.102.own), channel_id=1, source_target_pairs={{0,2},{1,3},{2,0},{3,1},{4,6},{5,7},{6,4},{7,5},{8,10},{9,11},{10,... | collective-permute-start | bytes 491528 | tf_op jit(solution)/shard_map/ppermute | solution.py:128
  22.4 2.3 %collective-permute-start.16 = (f32[64,640]{1,0:T(8,128)}, f32[64,640]{1,0:T(8,128)S(1)}, u32[]{:S(2)}, u32[]{:S(2)}) collective-permute-start(f32[64,640]{1,0:T(8,128)} %get-tuple-element.102.own), channel_id=1, source_target_pairs={{0,3},{1,0},{2,1},{3,2},{4,7},{5,4},{6,5},{7,6},{8,11},{9,8},{10,9... | collective-permute-start | bytes 491528 | tf_op jit(solution)/shard_map/ppermute | solution.py:128
  25.6 3.0 %collective-permute-start.18 = (f32[64,128]{1,0:T(8,128)S(1)}, f32[64,128]{1,0:T(8,128)S(1)}, u32[]{:S(2)}, u32[]{:S(2)}) collective-permute-start(f32[64,128]{1,0:T(8,128)S(1)} %shard_map.114.q0), channel_id=1, source_target_pairs={{0,2},{1,3},{2,0},{3,1},{4,6},{5,7},{6,4},{7,5},{8,10},{9,11},{10,... | collective-permute-start | bytes 98312 | tf_op jit(solution)/shard_map/ppermute | solution.py:128
  29.0 2.3 %collective-permute-start.20 = (f32[64,128]{1,0:T(8,128)S(1)}, f32[64,128]{1,0:T(8,128)S(1)}, u32[]{:S(2)}, u32[]{:S(2)}) collective-permute-start(f32[64,128]{1,0:T(8,128)S(1)} %shard_map.114.q0), channel_id=1, source_target_pairs={{0,3},{1,0},{2,1},{3,2},{4,7},{5,4},{6,5},{7,6},{8,11},{9,8},{10,9... | collective-permute-start | bytes 98312 | tf_op jit(solution)/shard_map/ppermute | solution.py:128
  31.3 1.3 copy-done
  32.6 0.7 copy-done.7
  33.3 2.9 %shard_map.115.x = bf16[640,1024]{1,0:T(8,128)(2,1)S(1)} custom-call(s32[1]{0:T(128)} %bitcast.place, s32[12]{0:T(128)S(1)} %copy-done.5, s32[16]{0:T(128)S(1)} %copy-done.7, f32[20]{0:T(128)S(1)} %copy-done.6, bf16[640,1024]{1,0:T(8,128)(2,1)S(1)} %copy-done, f32[20,640]{1,0:T(8,128)S(1)} %bitcast.9, f32[32,8,128]{2,1,0:T(8,128)S(1)} %all-to-all-done.1.tiles), custom_call_target="tpu_custom_call" | custom-call | tf_op jit(solution)/shard_map/pallas_call | solution.py:166
  36.3 2.2 %shard_map.116 = (f32[64,640]{1,0:T(8,128)}, f32[32,1152]{1,0:T(8,128)S(1)}, f32[32,1152]{1,0:T(8,128)S(1)}) custom-call(s32[1]{0:T(128)} %bitcast.place, s32[12]{0:T(128)S(1)} %copy-done.5, s32[16]{0:T(128)S(1)} %copy-done.7, f32[20]{0:T(128)S(1)} %copy-done.6, f32[64,640]{1,0:T(8,128)S(1)} %copy-done.3, f32[64,640]{1,0:T(8,128)S(1)} %collective-permute-done.14.a, ...), custom_call_target="tpu_custom_call" | custom-call | tf_op jit(solution)/shard_map/pallas_call | solution.py:166
  38.5 2.9 %collective-permute-start.21 = (f32[32,1152]{1,0:T(8,128)S(1)}, f32[32,1152]{1,0:T(8,128)S(1)}, u32[]{:S(2)}, u32[]{:S(2)}) collective-permute-start(f32[32,1152]{1,0:T(8,128)S(1)} %get-tuple-element.105), channel_id=1, source_target_pairs={{0,4},{4,0},{1,5},{5,1},{2,6},{6,2},{3,7},{7,3},{8,12},{12,8},{9,1... | collective-permute-start | bytes 442376 | tf_op jit(solution)/shard_map/ppermute | solution.py:124
  41.4 1.0 collective-permute-done.21.got
  42.5 2.7 %collective-permute-start.23 = (f32[8,1152]{1,0:T(8,128)S(1)}, f32[8,1152]{1,0:T(8,128)S(1)}, u32[]{:S(2)}, u32[]{:S(2)}) collective-permute-start(f32[8,1152]{1,0:T(8,128)S(1)} %get-tuple-element.108), channel_id=1, source_target_pairs={{0,24},{8,0},{16,8},{24,16},{1,25},{9,1},{17,9},{25,17},{2,26},{10... | collective-permute-start | bytes 110600 | tf_op jit(solution)/shard_map/ppermute | solution.py:133
  45.2 1.3 collective-permute-done.22.a
  46.5 3.0 %collective-permute-done.24.c = f32[8,1152]{1,0:T(8,128)S(1)} collective-permute-done((f32[8,1152]{1,0:T(8,128)S(1)}, f32[8,1152]{1,0:T(8,128)S(1)}, u32[]{:S(2)}, u32[]{:S(2)}) %collective-permute-start.24) | collective-permute-done | bytes 36896 | tf_op jit(solution)/shard_map/ppermute | solution.py:133
  49.5 13.6 %all_to_all.16.parts = f32[8,8,1152]{2,1,0:T(8,128)S(1)} all-to-all(f32[8,8,1152]{2,1,0:T(8,128)S(1)} %shard_map.118), channel_id=1, replica_groups=mesh['z'=8,'x'=4,'core'=2,'snp'=4] {'z'}, dimensions={0} | all-to-all | bytes 589824 | tf_op jit(solution)/shard_map/all_to_all | solution.py:395
  63.2 1.6 collective-permute-start.25
  65.1 2.4 %collective-permute-start.27 = (f32[8,1152]{1,0:T(8,128)S(1)}, f32[8,1152]{1,0:T(8,128)S(1)}, u32[]{:S(2)}, u32[]{:S(2)}) collective-permute-start(f32[8,1152]{1,0:T(8,128)S(1)} %shard_map.119), channel_id=1, source_target_pairs={{0,24},{8,0},{16,8},{24,16},{1,25},{9,1},{17,9},{25,17},{2,26},{10... | collective-permute-start | bytes 110600 | tf_op jit(solution)/shard_map/ppermute | solution.py:133
  67.4 4.6 %collective-permute-start.28 = (f32[8,1152]{1,0:T(8,128)S(1)}, f32[8,1152]{1,0:T(8,128)S(1)}, u32[]{:S(2)}, u32[]{:S(2)}) collective-permute-start(f32[8,1152]{1,0:T(8,128)S(1)} %shard_map.119), channel_id=1, source_target_pairs={{0,4},{4,0},{1,5},{5,1},{2,6},{6,2},{3,7},{7,3},{8,12},{12,8},{9,1... | collective-permute-start | bytes 110600 | tf_op jit(solution)/shard_map/ppermute | solution.py:124
  72.5 1.5 collective-permute-start.30
  74.0 0.8 collective-permute-done.30
  75.2 89.4 %while.28 = (s32[]{:T(128)}, f32[8,1152]{1,0:T(8,128)S(1)}, f32[8,1152]{1,0:T(8,128)S(1)}, f32[8,1152]{1,0:T(8,128)S(1)}, f32[8,1152]{1,0:T(8,128)S(1)}, /*index...) while((s32[]{:T(128)}, f32[8,1152]{1,0:T(8,128)S(1)}, ...), condition=%wide.region_1.0_spmd, body=%wide.region_0.0_spmd.sunk | while | flops 2 | bytes 3670709 | solution.py:511
  75.2 2.9 %eval_jaxpr.5 = (f32[64,1024]{1,0:T(8,128)S(1)}, f32[64,640]{1,0:T(8,128)S(1)}, f32[64,64]{1,0:T(8,128)S(1)}, bf16[64,832]{1,0:T(8,128)(2,1)S(1)}) custom-call(s32[1]{0:T(128)} %get-tuple-element.287.place, f32[8,1152]{1,0:T(8,128)S(1)} %get-tuple-element.263.refs_0_, f32[8,1152]{1,0:T(8,128)S(1)} %get-tuple-element.264.refs_1_, ...), custom_call_target="tpu_custom_call" | custom-call | tf_op jit(solution)/shard_map/while/body/eval_jaxpr/pallas_call | solution.py:166
  79.1 2.1 %collective-permute-start.2 = (bf16[64,832]{1,0:T(8,128)(2,1)S(1)}, bf16[64,832]{1,0:T(8,128)(2,1)S(1)}, u32[]{:S(2)}, u32[]{:S(2)}) collective-permute-start(bf16[64,832]{1,0:T(8,128)(2,1)S(1)} %get-tuple-element.238), channel_id=1, source_target_pairs={{0,3},{1,0},{2,1},{3,2},{4,7},{5,4},{6,5},{7,6},{8,11},{9,8},{10,9... | collective-permute-start | bytes 319496 | tf_op jit(solution)/shard_map/while/body/eval_jaxpr/ppermute | solution.py:128
  81.2 3.0 %collective-permute-done.a = bf16[64,832]{1,0:T(8,128)(2,1)S(1)} collective-permute-done((bf16[64,832]{1,0:T(8,128)(2,1)S(1)}, bf16[64,832]{1,0:T(8,128)(2,1)S(1)}, u32[]{:S(2)}, u32[]{:S(2)}) %collective-permute-start) | collective-permute-done | bytes 106528 | tf_op jit(solution)/shard_map/while/body/eval_jaxpr/ppermute | solution.py:128
  84.2 2.9 %collective-permute-done.1.b = bf16[64,832]{1,0:T(8,128)(2,1)S(1)} collective-permute-done((bf16[64,832]{1,0:T(8,128)(2,1)S(1)}, bf16[64,832]{1,0:T(8,128)(2,1)S(1)}, u32[]{:S(2)}, u32[]{:S(2)}) %collective-permute-start.1) | collective-permute-done | bytes 106528 | tf_op jit(solution)/shard_map/while/body/eval_jaxpr/ppermute | solution.py:128
  87.1 3.4 %eval_jaxpr.6 = (f32[64,640]{1,0:T(8,128)}, f32[64,1024]{1,0:T(8,128)}, f32[32,1152]{1,0:T(8,128)S(1)}, f32[32,1152]{1,0:T(8,128)S(1)}) custom-call(s32[1]{0:T(128)} %get-tuple-element.287.place, f32[64,640]{1,0:T(8,128)S(1)} %get-tuple-element.236.product, f32[64,64]{1,0:T(8,128)S(1)} %get-tuple-element.237.gram, ...), custom_call_target="tpu_custom_call" | custom-call | tf_op jit(solution)/shard_map/while/body/eval_jaxpr/pallas_call | solution.py:166
  91.0 1.0 collective-permute-done.3.got
  92.0 1.2 collective-permute-start.4
  93.2 2.1 %collective-permute-start.5 = (f32[8,1152]{1,0:T(8,128)S(1)}, f32[8,1152]{1,0:T(8,128)S(1)}, u32[]{:S(2)}, u32[]{:S(2)}) collective-permute-start(f32[8,1152]{1,0:T(8,128)S(1)} %get-tuple-element.244), channel_id=1, source_target_pairs={{0,8},{8,16},{16,24},{24,0},{1,9},{9,17},{17,25},{25,1},{2,10},{10... | collective-permute-start | bytes 110600 | tf_op jit(solution)/shard_map/while/body/eval_jaxpr/ppermute | solution.py:133
  95.3 0.6 collective-permute-start.6
  96.4 1.4 collective-permute-done.5.b
  98.5 10.7 %all_to_all.17.parts = bf16[8,8,1280]{2,1,0:T(8,128)(2,1)S(1)} all-to-all(bf16[8,8,1280]{2,1,0:T(8,128)(2,1)S(1)} %eval_jaxpr.8), channel_id=1, replica_groups=mesh['z'=8,'x'=4,'core'=2,'snp'=4] {'z'}, dimensions={0} | all-to-all | bytes 327680 | tf_op jit(solution)/shard_map/while/body/eval_jaxpr/all_to_all | solution.py:395
  109.7 2.1 %collective-permute-start.8 = (f32[8,1152]{1,0:T(8,128)S(1)}, f32[8,1152]{1,0:T(8,128)S(1)}, u32[]{:S(2)}, u32[]{:S(2)}) collective-permute-start(f32[8,1152]{1,0:T(8,128)S(1)} %eval_jaxpr.9), channel_id=1, source_target_pairs={{0,8},{8,16},{16,24},{24,0},{1,9},{9,17},{17,25},{25,1},{2,10},{10... | collective-permute-start | bytes 110600 | tf_op jit(solution)/shard_map/while/body/eval_jaxpr/ppermute | solution.py:133
  112.4 3.7 %collective-permute-start.10 = (f32[8,1152]{1,0:T(8,128)S(1)}, f32[8,1152]{1,0:T(8,128)S(1)}, u32[]{:S(2)}, u32[]{:S(2)}) collective-permute-start(f32[8,1152]{1,0:T(8,128)S(1)} %eval_jaxpr.9), channel_id=1, source_target_pairs={{0,4},{4,0},{1,5},{5,1},{2,6},{6,2},{3,7},{7,3},{8,12},{12,8},{9,1... | collective-permute-start | bytes 110600 | tf_op jit(solution)/shard_map/while/body/eval_jaxpr/ppermute | solution.py:124
  116.1 1.5 collective-permute-start.11
  118.1 1.0 collective-permute-start.13
  119.1 0.9 collective-permute-done.13
  120.0 2.9 %eval_jaxpr.5 = (f32[64,1024]{1,0:T(8,128)S(1)}, f32[64,640]{1,0:T(8,128)S(1)}, f32[64,64]{1,0:T(8,128)S(1)}, bf16[64,832]{1,0:T(8,128)(2,1)S(1)}) custom-call(s32[1]{0:T(128)} %get-tuple-element.287.place, f32[8,1152]{1,0:T(8,128)S(1)} %get-tuple-element.263.refs_0_, f32[8,1152]{1,0:T(8,128)S(1)} %get-tuple-element.264.refs_1_, ...), custom_call_target="tpu_custom_call" | custom-call | tf_op jit(solution)/shard_map/while/body/eval_jaxpr/pallas_call | solution.py:166
  123.4 0.9 collective-permute-start.1
  124.3 1.7 %collective-permute-start.2 = (bf16[64,832]{1,0:T(8,128)(2,1)S(1)}, bf16[64,832]{1,0:T(8,128)(2,1)S(1)}, u32[]{:S(2)}, u32[]{:S(2)}) collective-permute-start(bf16[64,832]{1,0:T(8,128)(2,1)S(1)} %get-tuple-element.238), channel_id=1, source_target_pairs={{0,3},{1,0},{2,1},{3,2},{4,7},{5,4},{6,5},{7,6},{8,11},{9,8},{10,9... | collective-permute-start | bytes 319496 | tf_op jit(solution)/shard_map/while/body/eval_jaxpr/ppermute | solution.py:128
  126.1 2.7 %collective-permute-done.a = bf16[64,832]{1,0:T(8,128)(2,1)S(1)} collective-permute-done((bf16[64,832]{1,0:T(8,128)(2,1)S(1)}, bf16[64,832]{1,0:T(8,128)(2,1)S(1)}, u32[]{:S(2)}, u32[]{:S(2)}) %collective-permute-start) | collective-permute-done | bytes 106528 | tf_op jit(solution)/shard_map/while/body/eval_jaxpr/ppermute | solution.py:128
  128.8 3.1 %collective-permute-done.1.b = bf16[64,832]{1,0:T(8,128)(2,1)S(1)} collective-permute-done((bf16[64,832]{1,0:T(8,128)(2,1)S(1)}, bf16[64,832]{1,0:T(8,128)(2,1)S(1)}, u32[]{:S(2)}, u32[]{:S(2)}) %collective-permute-start.1) | collective-permute-done | bytes 106528 | tf_op jit(solution)/shard_map/while/body/eval_jaxpr/ppermute | solution.py:128
  131.9 3.4 %eval_jaxpr.6 = (f32[64,640]{1,0:T(8,128)}, f32[64,1024]{1,0:T(8,128)}, f32[32,1152]{1,0:T(8,128)S(1)}, f32[32,1152]{1,0:T(8,128)S(1)}) custom-call(s32[1]{0:T(128)} %get-tuple-element.287.place, f32[64,640]{1,0:T(8,128)S(1)} %get-tuple-element.236.product, f32[64,64]{1,0:T(8,128)S(1)} %get-tuple-element.237.gram, ...), custom_call_target="tpu_custom_call" | custom-call | tf_op jit(solution)/shard_map/while/body/eval_jaxpr/pallas_call | solution.py:166
  135.8 1.0 collective-permute-done.3.got
  136.8 1.0 collective-permute-start.4
  137.8 1.6 collective-permute-start.5
  139.4 1.1 collective-permute-start.6
  140.5 0.7 collective-permute-done.4.a
  141.2 1.2 collective-permute-done.5.b
  142.6 10.7 %all_to_all.17.parts = bf16[8,8,1280]{2,1,0:T(8,128)(2,1)S(1)} all-to-all(bf16[8,8,1280]{2,1,0:T(8,128)(2,1)S(1)} %eval_jaxpr.8), channel_id=1, replica_groups=mesh['z'=8,'x'=4,'core'=2,'snp'=4] {'z'}, dimensions={0} | all-to-all | bytes 327680 | tf_op jit(solution)/shard_map/while/body/eval_jaxpr/all_to_all | solution.py:395
  153.5 1.3 collective-permute-start.7
  154.8 1.3 collective-permute-start.8
  156.1 1.4 collective-permute-start.9
  157.5 3.7 %collective-permute-start.10 = (f32[8,1152]{1,0:T(8,128)S(1)}, f32[8,1152]{1,0:T(8,128)S(1)}, u32[]{:S(2)}, u32[]{:S(2)}) collective-permute-start(f32[8,1152]{1,0:T(8,128)S(1)} %eval_jaxpr.9), channel_id=1, source_target_pairs={{0,4},{4,0},{1,5},{5,1},{2,6},{6,2},{3,7},{7,3},{8,12},{12,8},{9,1... | collective-permute-start | bytes 110600 | tf_op jit(solution)/shard_map/while/body/eval_jaxpr/ppermute | solution.py:124
  161.2 0.6 collective-permute-start.11
  161.8 1.3 collective-permute-start.12
  163.1 0.6 collective-permute-start.13
  164.0 0.6 collective-permute-done.13
  164.6 3.9 %shard_map.120 = (f32[64,640]{1,0:T(8,128)}, f32[64,1024]{1,0:T(8,128)}) custom-call(s32[1]{0:T(128)} %bitcast.place, f32[8,1152]{1,0:T(8,128)S(1)} %get-tuple-element.111.refs_0_, f32[8,1152]{1,0:T(8,128)S(1)} %get-tuple-element.112.refs_1_, f32[8,1152]{1,0:T(8,128)S(1)} %get-tuple-element.113.refs_2_, f32[8,1152]{1,0:T(8,128)S(1)} %get-tuple-element.114.refs_3_, ...), custom_call_target="tpu_custom_call" | custom-call | tf_op jit(solution)/shard_map/pallas_call | solution.py:166
  (70 shorter events, 9.0 us)
Async XLA Ops:
  0.6 4.4 %collective-permute-start.17 = (f32[16,20]{1,0:T(8,128)}, f32[16,20]{1,0:T(8,128)S(1)}, u32[]{:S(2)}, u32[]{:S(2)}) collective-permute-start(f32[16,20]{1,0:T(8,128)} %mine.1), channel_id=1, source_target_pairs={{0,4},{4,0},{1,5},{5,1},{2,6},{6,2},{3,7},{7,3},{8,12},{12,8},{9,1... | collective-permute-start | bytes 3848 | tf_op jit(solution)/shard_map/ppermute | solution.py:124
  5.0 0.7 copy-start.4
  6.4 18.7 %all-to-all-start.1 = ((f32[32,8,128]{2,1,0:T(8,128)}), f32[32,8,128]{2,1,0:T(8,128)S(1)}, u32[]{:S(2)}, u32[]{:S(2)}) async-start(f32[32,8,128]{2,1,0:T(8,128)} %shard_map.113), calls=%async_computation.1 | async-start | bytes 262144 | tf_op jit(solution)/shard_map/all_to_all | solution.py:280
  15.7 9.3 %copy-start.1 = (bf16[1024,64]{0,1:T(8,128)(2,1)S(1)}, bf16[1024,64]{0,1:T(8,128)(2,1)}, u32[]{:S(2)}) copy-start(bf16[1024,64]{0,1:T(8,128)(2,1)} %param.16) | copy-start | bytes 393220
  15.8 15.6 %copy-start.2 = (f32[640,20]{0,1:T(8,128)S(1)}, f32[640,20]{0,1:T(8,128)}, u32[]{:S(2)}) copy-start(f32[640,20]{0,1:T(8,128)} %param.13) | copy-start | bytes 153604
  15.8 15.5 %copy-start.5 = (s32[12]{0:T(128)S(1)}, s32[12]{0:T(128)}, u32[]{:S(2)}) copy-start(s32[12]{0:T(128)} %sizes.3) | copy-start | bytes 148
  15.8 15.5 %copy-start.6 = (f32[20]{0:T(128)S(1)}, f32[20]{0:T(128)}, u32[]{:S(2)}) copy-start(f32[20]{0:T(128)} %scale.3) | copy-start | bytes 244
  19.0 10.0 %collective-permute-start.14 = (f32[64,640]{1,0:T(8,128)}, f32[64,640]{1,0:T(8,128)S(1)}, u32[]{:S(2)}, u32[]{:S(2)}) collective-permute-start(f32[64,640]{1,0:T(8,128)} %get-tuple-element.102.own), channel_id=1, source_target_pairs={{0,2},{1,3},{2,0},{3,1},{4,6},{5,7},{6,4},{7,5},{8,10},{9,11},{10,... | collective-permute-start | bytes 491528 | tf_op jit(solution)/shard_map/ppermute | solution.py:128
  22.0 14.2 %collective-permute-start.15 = (f32[64,640]{1,0:T(8,128)}, f32[64,640]{1,0:T(8,128)S(1)}, u32[]{:S(2)}, u32[]{:S(2)}) collective-permute-start(f32[64,640]{1,0:T(8,128)} %get-tuple-element.102.own), channel_id=1, source_target_pairs={{0,1},{1,2},{2,3},{3,0},{4,5},{5,6},{6,7},{7,4},{8,9},{9,10},{10,1... | collective-permute-start | bytes 491528 | tf_op jit(solution)/shard_map/ppermute | solution.py:128
  22.4 13.8 %collective-permute-start.16 = (f32[64,640]{1,0:T(8,128)}, f32[64,640]{1,0:T(8,128)S(1)}, u32[]{:S(2)}, u32[]{:S(2)}) collective-permute-start(f32[64,640]{1,0:T(8,128)} %get-tuple-element.102.own), channel_id=1, source_target_pairs={{0,3},{1,0},{2,1},{3,2},{4,7},{5,4},{6,5},{7,6},{8,11},{9,8},{10,9... | collective-permute-start | bytes 491528 | tf_op jit(solution)/shard_map/ppermute | solution.py:128
  25.6 10.6 %collective-permute-start.18 = (f32[64,128]{1,0:T(8,128)S(1)}, f32[64,128]{1,0:T(8,128)S(1)}, u32[]{:S(2)}, u32[]{:S(2)}) collective-permute-start(f32[64,128]{1,0:T(8,128)S(1)} %shard_map.114.q0), channel_id=1, source_target_pairs={{0,2},{1,3},{2,0},{3,1},{4,6},{5,7},{6,4},{7,5},{8,10},{9,11},{10,... | collective-permute-start | bytes 98312 | tf_op jit(solution)/shard_map/ppermute | solution.py:128
  28.6 7.6 %collective-permute-start.19 = (f32[64,128]{1,0:T(8,128)S(1)}, f32[64,128]{1,0:T(8,128)S(1)}, u32[]{:S(2)}, u32[]{:S(2)}) collective-permute-start(f32[64,128]{1,0:T(8,128)S(1)} %shard_map.114.q0), channel_id=1, source_target_pairs={{0,1},{1,2},{2,3},{3,0},{4,5},{5,6},{6,7},{7,4},{8,9},{9,10},{10,1... | collective-permute-start | bytes 98312 | tf_op jit(solution)/shard_map/ppermute | solution.py:128
  29.0 7.2 %collective-permute-start.20 = (f32[64,128]{1,0:T(8,128)S(1)}, f32[64,128]{1,0:T(8,128)S(1)}, u32[]{:S(2)}, u32[]{:S(2)}) collective-permute-start(f32[64,128]{1,0:T(8,128)S(1)} %shard_map.114.q0), channel_id=1, source_target_pairs={{0,3},{1,0},{2,1},{3,2},{4,7},{5,4},{6,5},{7,6},{8,11},{9,8},{10,9... | collective-permute-start | bytes 98312 | tf_op jit(solution)/shard_map/ppermute | solution.py:128
  31.3 1.3 copy-start
  32.6 0.7 copy-start.7
  33.3 3.0 %copy-start.3 = (f32[64,640]{1,0:T(8,128)S(1)}, f32[64,640]{1,0:T(8,128)}, u32[]{:S(2)}) copy-start(f32[64,640]{1,0:T(8,128)} %get-tuple-element.102.own) | copy-start | bytes 491524
  38.5 3.9 %collective-permute-start.21 = (f32[32,1152]{1,0:T(8,128)S(1)}, f32[32,1152]{1,0:T(8,128)S(1)}, u32[]{:S(2)}, u32[]{:S(2)}) collective-permute-start(f32[32,1152]{1,0:T(8,128)S(1)} %get-tuple-element.105), channel_id=1, source_target_pairs={{0,4},{4,0},{1,5},{5,1},{2,6},{6,2},{3,7},{7,3},{8,12},{12,8},{9,1... | collective-permute-start | bytes 442376 | tf_op jit(solution)/shard_map/ppermute | solution.py:124
  42.4 4.1 %collective-permute-start.22 = (f32[8,1152]{1,0:T(8,128)S(1)}, f32[8,1152]{1,0:T(8,128)S(1)}, u32[]{:S(2)}, u32[]{:S(2)}) collective-permute-start(f32[8,1152]{1,0:T(8,128)S(1)} %get-tuple-element.107), channel_id=1, source_target_pairs={{0,8},{8,16},{16,24},{24,0},{1,9},{9,17},{17,25},{25,1},{2,10},{10... | collective-permute-start | bytes 110600 | tf_op jit(solution)/shard_map/ppermute | solution.py:133
  42.5 4.0 %collective-permute-start.23 = (f32[8,1152]{1,0:T(8,128)S(1)}, f32[8,1152]{1,0:T(8,128)S(1)}, u32[]{:S(2)}, u32[]{:S(2)}) collective-permute-start(f32[8,1152]{1,0:T(8,128)S(1)} %get-tuple-element.108), channel_id=1, source_target_pairs={{0,24},{8,0},{16,8},{24,16},{1,25},{9,1},{17,9},{25,17},{2,26},{10... | collective-permute-start | bytes 110600 | tf_op jit(solution)/shard_map/ppermute | solution.py:133
  45.2 4.3 %collective-permute-start.24 = (f32[8,1152]{1,0:T(8,128)S(1)}, f32[8,1152]{1,0:T(8,128)S(1)}, u32[]{:S(2)}, u32[]{:S(2)}) collective-permute-start(f32[8,1152]{1,0:T(8,128)S(1)} %get-tuple-element.109), channel_id=1, source_target_pairs={{0,16},{8,24},{16,0},{24,8},{1,17},{9,25},{17,1},{25,9},{2,18},{10... | collective-permute-start | bytes 110600 | tf_op jit(solution)/shard_map/ppermute | solution.py:133
  63.2 8.8 %collective-permute-start.25 = (f32[8,1152]{1,0:T(8,128)S(1)}, f32[8,1152]{1,0:T(8,128)S(1)}, u32[]{:S(2)}, u32[]{:S(2)}) collective-permute-start(f32[8,1152]{1,0:T(8,128)S(1)} %shard_map.119), channel_id=1, source_target_pairs={{0,16},{8,24},{16,0},{24,8},{1,17},{9,25},{17,1},{25,9},{2,18},{10... | collective-permute-start | bytes 110600 | tf_op jit(solution)/shard_map/ppermute | solution.py:133
  64.8 7.7 %collective-permute-start.26 = (f32[8,1152]{1,0:T(8,128)S(1)}, f32[8,1152]{1,0:T(8,128)S(1)}, u32[]{:S(2)}, u32[]{:S(2)}) collective-permute-start(f32[8,1152]{1,0:T(8,128)S(1)} %shard_map.119), channel_id=1, source_target_pairs={{0,8},{8,16},{16,24},{24,0},{1,9},{9,17},{17,25},{25,1},{2,10},{10... | collective-permute-start | bytes 110600 | tf_op jit(solution)/shard_map/ppermute | solution.py:133
  65.1 8.9 %collective-permute-start.27 = (f32[8,1152]{1,0:T(8,128)S(1)}, f32[8,1152]{1,0:T(8,128)S(1)}, u32[]{:S(2)}, u32[]{:S(2)}) collective-permute-start(f32[8,1152]{1,0:T(8,128)S(1)} %shard_map.119), channel_id=1, source_target_pairs={{0,24},{8,0},{16,8},{24,16},{1,25},{9,1},{17,9},{25,17},{2,26},{10... | collective-permute-start | bytes 110600 | tf_op jit(solution)/shard_map/ppermute | solution.py:133
  67.4 6.5 %collective-permute-start.28 = (f32[8,1152]{1,0:T(8,128)S(1)}, f32[8,1152]{1,0:T(8,128)S(1)}, u32[]{:S(2)}, u32[]{:S(2)}) collective-permute-start(f32[8,1152]{1,0:T(8,128)S(1)} %shard_map.119), channel_id=1, source_target_pairs={{0,4},{4,0},{1,5},{5,1},{2,6},{6,2},{3,7},{7,3},{8,12},{12,8},{9,1... | collective-permute-start | bytes 110600 | tf_op jit(solution)/shard_map/ppermute | solution.py:124
  72.0 1.9 %collective-permute-start.29 = (f32[8,1152]{1,0:T(8,128)S(1)}, f32[8,1152]{1,0:T(8,128)S(1)}, u32[]{:S(2)}, u32[]{:S(2)}) collective-permute-start(f32[8,1152]{1,0:T(8,128)S(1)} %collective-permute-done.25), channel_id=1, source_target_pairs={{0,4},{4,0},{1,5},{5,1},{2,6},{6,2},{3,7},{7,3},{8,12},{12,8},{9,1... | collective-permute-start | bytes 110600 | tf_op jit(solution)/shard_map/ppermute | solution.py:124
  72.5 2.3 %collective-permute-start.30 = (f32[8,1152]{1,0:T(8,128)S(1)}, f32[8,1152]{1,0:T(8,128)S(1)}, u32[]{:S(2)}, u32[]{:S(2)}) collective-permute-start(f32[8,1152]{1,0:T(8,128)S(1)} %collective-permute-done.26), channel_id=1, source_target_pairs={{0,4},{4,0},{1,5},{5,1},{2,6},{6,2},{3,7},{7,3},{8,12},{12,8},{9,1... | collective-permute-start | bytes 110600 | tf_op jit(solution)/shard_map/ppermute | solution.py:124
  74.0 1.2 collective-permute-start.31
  78.0 6.2 %collective-permute-start = (bf16[64,832]{1,0:T(8,128)(2,1)S(1)}, bf16[64,832]{1,0:T(8,128)(2,1)S(1)}, u32[]{:S(2)}, u32[]{:S(2)}) collective-permute-start(bf16[64,832]{1,0:T(8,128)(2,1)S(1)} %get-tuple-element.238), channel_id=1, source_target_pairs={{0,2},{1,3},{2,0},{3,1},{4,6},{5,7},{6,4},{7,5},{8,10},{9,11},{10,... | collective-permute-start | bytes 319496 | tf_op jit(solution)/shard_map/while/body/eval_jaxpr/ppermute | solution.py:128
  78.6 8.6 %collective-permute-start.1 = (bf16[64,832]{1,0:T(8,128)(2,1)S(1)}, bf16[64,832]{1,0:T(8,128)(2,1)S(1)}, u32[]{:S(2)}, u32[]{:S(2)}) collective-permute-start(bf16[64,832]{1,0:T(8,128)(2,1)S(1)} %get-tuple-element.238), channel_id=1, source_target_pairs={{0,1},{1,2},{2,3},{3,0},{4,5},{5,6},{6,7},{7,4},{8,9},{9,10},{10,1... | collective-permute-start | bytes 319496 | tf_op jit(solution)/shard_map/while/body/eval_jaxpr/ppermute | solution.py:128
  79.1 8.0 %collective-permute-start.2 = (bf16[64,832]{1,0:T(8,128)(2,1)S(1)}, bf16[64,832]{1,0:T(8,128)(2,1)S(1)}, u32[]{:S(2)}, u32[]{:S(2)}) collective-permute-start(bf16[64,832]{1,0:T(8,128)(2,1)S(1)} %get-tuple-element.238), channel_id=1, source_target_pairs={{0,3},{1,0},{2,1},{3,2},{4,7},{5,4},{6,5},{7,6},{8,11},{9,8},{10,9... | collective-permute-start | bytes 319496 | tf_op jit(solution)/shard_map/while/body/eval_jaxpr/ppermute | solution.py:128
  90.5 1.5 collective-permute-start.3
  92.0 4.4 %collective-permute-start.4 = (f32[8,1152]{1,0:T(8,128)S(1)}, f32[8,1152]{1,0:T(8,128)S(1)}, u32[]{:S(2)}, u32[]{:S(2)}) collective-permute-start(f32[8,1152]{1,0:T(8,128)S(1)} %get-tuple-element.243), channel_id=1, source_target_pairs={{0,16},{8,24},{16,0},{24,8},{1,17},{9,25},{17,1},{25,9},{2,18},{10... | collective-permute-start | bytes 110600 | tf_op jit(solution)/shard_map/while/body/eval_jaxpr/ppermute | solution.py:133
  93.2 4.6 %collective-permute-start.5 = (f32[8,1152]{1,0:T(8,128)S(1)}, f32[8,1152]{1,0:T(8,128)S(1)}, u32[]{:S(2)}, u32[]{:S(2)}) collective-permute-start(f32[8,1152]{1,0:T(8,128)S(1)} %get-tuple-element.244), channel_id=1, source_target_pairs={{0,8},{8,16},{16,24},{24,0},{1,9},{9,17},{17,25},{25,1},{2,10},{10... | collective-permute-start | bytes 110600 | tf_op jit(solution)/shard_map/while/body/eval_jaxpr/ppermute | solution.py:133
  95.3 3.1 %collective-permute-start.6 = (f32[8,1152]{1,0:T(8,128)S(1)}, f32[8,1152]{1,0:T(8,128)S(1)}, u32[]{:S(2)}, u32[]{:S(2)}) collective-permute-start(f32[8,1152]{1,0:T(8,128)S(1)} %get-tuple-element.245), channel_id=1, source_target_pairs={{0,24},{8,0},{16,8},{24,16},{1,25},{9,1},{17,9},{25,17},{2,26},{10... | collective-permute-start | bytes 110600 | tf_op jit(solution)/shard_map/while/body/eval_jaxpr/ppermute | solution.py:133
  109.3 6.8 %collective-permute-start.7 = (f32[8,1152]{1,0:T(8,128)S(1)}, f32[8,1152]{1,0:T(8,128)S(1)}, u32[]{:S(2)}, u32[]{:S(2)}) collective-permute-start(f32[8,1152]{1,0:T(8,128)S(1)} %eval_jaxpr.9), channel_id=1, source_target_pairs={{0,16},{8,24},{16,0},{24,8},{1,17},{9,25},{17,1},{25,9},{2,18},{10... | collective-permute-start | bytes 110600 | tf_op jit(solution)/shard_map/while/body/eval_jaxpr/ppermute | solution.py:133
  109.7 8.0 %collective-permute-start.8 = (f32[8,1152]{1,0:T(8,128)S(1)}, f32[8,1152]{1,0:T(8,128)S(1)}, u32[]{:S(2)}, u32[]{:S(2)}) collective-permute-start(f32[8,1152]{1,0:T(8,128)S(1)} %eval_jaxpr.9), channel_id=1, source_target_pairs={{0,8},{8,16},{16,24},{24,0},{1,9},{9,17},{17,25},{25,1},{2,10},{10... | collective-permute-start | bytes 110600 | tf_op jit(solution)/shard_map/while/body/eval_jaxpr/ppermute | solution.py:133
  111.8 6.3 %collective-permute-start.9 = (f32[8,1152]{1,0:T(8,128)S(1)}, f32[8,1152]{1,0:T(8,128)S(1)}, u32[]{:S(2)}, u32[]{:S(2)}) collective-permute-start(f32[8,1152]{1,0:T(8,128)S(1)} %eval_jaxpr.9), channel_id=1, source_target_pairs={{0,24},{8,0},{16,8},{24,16},{1,25},{9,1},{17,9},{25,17},{2,26},{10... | collective-permute-start | bytes 110600 | tf_op jit(solution)/shard_map/while/body/eval_jaxpr/ppermute | solution.py:133
  112.4 6.7 %collective-permute-start.10 = (f32[8,1152]{1,0:T(8,128)S(1)}, f32[8,1152]{1,0:T(8,128)S(1)}, u32[]{:S(2)}, u32[]{:S(2)}) collective-permute-start(f32[8,1152]{1,0:T(8,128)S(1)} %eval_jaxpr.9), channel_id=1, source_target_pairs={{0,4},{4,0},{1,5},{5,1},{2,6},{6,2},{3,7},{7,3},{8,12},{12,8},{9,1... | collective-permute-start | bytes 110600 | tf_op jit(solution)/shard_map/while/body/eval_jaxpr/ppermute | solution.py:124
  116.1 3.0 %collective-permute-start.11 = (f32[8,1152]{1,0:T(8,128)S(1)}, f32[8,1152]{1,0:T(8,128)S(1)}, u32[]{:S(2)}, u32[]{:S(2)}) collective-permute-start(f32[8,1152]{1,0:T(8,128)S(1)} %collective-permute-done.7), channel_id=1, source_target_pairs={{0,4},{4,0},{1,5},{5,1},{2,6},{6,2},{3,7},{7,3},{8,12},{12,8},{9,1... | collective-permute-start | bytes 110600 | tf_op jit(solution)/shard_map/while/body/eval_jaxpr/ppermute | solution.py:124
  117.7 1.5 collective-permute-start.12
  118.1 1.9 %collective-permute-start.13 = (f32[8,1152]{1,0:T(8,128)S(1)}, f32[8,1152]{1,0:T(8,128)S(1)}, u32[]{:S(2)}, u32[]{:S(2)}) collective-permute-start(f32[8,1152]{1,0:T(8,128)S(1)} %collective-permute-done.9), channel_id=1, source_target_pairs={{0,4},{4,0},{1,5},{5,1},{2,6},{6,2},{3,7},{7,3},{8,12},{12,8},{9,1... | collective-permute-start | bytes 110600 | tf_op jit(solution)/shard_map/while/body/eval_jaxpr/ppermute | solution.py:124
  122.8 5.9 %collective-permute-start = (bf16[64,832]{1,0:T(8,128)(2,1)S(1)}, bf16[64,832]{1,0:T(8,128)(2,1)S(1)}, u32[]{:S(2)}, u32[]{:S(2)}) collective-permute-start(bf16[64,832]{1,0:T(8,128)(2,1)S(1)} %get-tuple-element.238), channel_id=1, source_target_pairs={{0,2},{1,3},{2,0},{3,1},{4,6},{5,7},{6,4},{7,5},{8,10},{9,11},{10,... | collective-permute-start | bytes 319496 | tf_op jit(solution)/shard_map/while/body/eval_jaxpr/ppermute | solution.py:128
  123.4 8.6 %collective-permute-start.1 = (bf16[64,832]{1,0:T(8,128)(2,1)S(1)}, bf16[64,832]{1,0:T(8,128)(2,1)S(1)}, u32[]{:S(2)}, u32[]{:S(2)}) collective-permute-start(bf16[64,832]{1,0:T(8,128)(2,1)S(1)} %get-tuple-element.238), channel_id=1, source_target_pairs={{0,1},{1,2},{2,3},{3,0},{4,5},{5,6},{6,7},{7,4},{8,9},{9,10},{10,1... | collective-permute-start | bytes 319496 | tf_op jit(solution)/shard_map/while/body/eval_jaxpr/ppermute | solution.py:128
  124.3 7.6 %collective-permute-start.2 = (bf16[64,832]{1,0:T(8,128)(2,1)S(1)}, bf16[64,832]{1,0:T(8,128)(2,1)S(1)}, u32[]{:S(2)}, u32[]{:S(2)}) collective-permute-start(bf16[64,832]{1,0:T(8,128)(2,1)S(1)} %get-tuple-element.238), channel_id=1, source_target_pairs={{0,3},{1,0},{2,1},{3,2},{4,7},{5,4},{6,5},{7,6},{8,11},{9,8},{10,9... | collective-permute-start | bytes 319496 | tf_op jit(solution)/shard_map/while/body/eval_jaxpr/ppermute | solution.py:128
  135.3 1.5 collective-permute-start.3
  136.8 4.4 %collective-permute-start.4 = (f32[8,1152]{1,0:T(8,128)S(1)}, f32[8,1152]{1,0:T(8,128)S(1)}, u32[]{:S(2)}, u32[]{:S(2)}) collective-permute-start(f32[8,1152]{1,0:T(8,128)S(1)} %get-tuple-element.243), channel_id=1, source_target_pairs={{0,16},{8,24},{16,0},{24,8},{1,17},{9,25},{17,1},{25,9},{2,18},{10... | collective-permute-start | bytes 110600 | tf_op jit(solution)/shard_map/while/body/eval_jaxpr/ppermute | solution.py:133
  137.8 4.5 %collective-permute-start.5 = (f32[8,1152]{1,0:T(8,128)S(1)}, f32[8,1152]{1,0:T(8,128)S(1)}, u32[]{:S(2)}, u32[]{:S(2)}) collective-permute-start(f32[8,1152]{1,0:T(8,128)S(1)} %get-tuple-element.244), channel_id=1, source_target_pairs={{0,8},{8,16},{16,24},{24,0},{1,9},{9,17},{17,25},{25,1},{2,10},{10... | collective-permute-start | bytes 110600 | tf_op jit(solution)/shard_map/while/body/eval_jaxpr/ppermute | solution.py:133
  139.4 3.1 %collective-permute-start.6 = (f32[8,1152]{1,0:T(8,128)S(1)}, f32[8,1152]{1,0:T(8,128)S(1)}, u32[]{:S(2)}, u32[]{:S(2)}) collective-permute-start(f32[8,1152]{1,0:T(8,128)S(1)} %get-tuple-element.245), channel_id=1, source_target_pairs={{0,24},{8,0},{16,8},{24,16},{1,25},{9,1},{17,9},{25,17},{2,26},{10... | collective-permute-start | bytes 110600 | tf_op jit(solution)/shard_map/while/body/eval_jaxpr/ppermute | solution.py:133
  153.5 7.8 %collective-permute-start.7 = (f32[8,1152]{1,0:T(8,128)S(1)}, f32[8,1152]{1,0:T(8,128)S(1)}, u32[]{:S(2)}, u32[]{:S(2)}) collective-permute-start(f32[8,1152]{1,0:T(8,128)S(1)} %eval_jaxpr.9), channel_id=1, source_target_pairs={{0,16},{8,24},{16,0},{24,8},{1,17},{9,25},{17,1},{25,9},{2,18},{10... | collective-permute-start | bytes 110600 | tf_op jit(solution)/shard_map/while/body/eval_jaxpr/ppermute | solution.py:133
  154.8 7.0 %collective-permute-start.8 = (f32[8,1152]{1,0:T(8,128)S(1)}, f32[8,1152]{1,0:T(8,128)S(1)}, u32[]{:S(2)}, u32[]{:S(2)}) collective-permute-start(f32[8,1152]{1,0:T(8,128)S(1)} %eval_jaxpr.9), channel_id=1, source_target_pairs={{0,8},{8,16},{16,24},{24,0},{1,9},{9,17},{17,25},{25,1},{2,10},{10... | collective-permute-start | bytes 110600 | tf_op jit(solution)/shard_map/while/body/eval_jaxpr/ppermute | solution.py:133
  156.1 7.0 %collective-permute-start.9 = (f32[8,1152]{1,0:T(8,128)S(1)}, f32[8,1152]{1,0:T(8,128)S(1)}, u32[]{:S(2)}, u32[]{:S(2)}) collective-permute-start(f32[8,1152]{1,0:T(8,128)S(1)} %eval_jaxpr.9), channel_id=1, source_target_pairs={{0,24},{8,0},{16,8},{24,16},{1,25},{9,1},{17,9},{25,17},{2,26},{10... | collective-permute-start | bytes 110600 | tf_op jit(solution)/shard_map/while/body/eval_jaxpr/ppermute | solution.py:133
  157.5 6.3 %collective-permute-start.10 = (f32[8,1152]{1,0:T(8,128)S(1)}, f32[8,1152]{1,0:T(8,128)S(1)}, u32[]{:S(2)}, u32[]{:S(2)}) collective-permute-start(f32[8,1152]{1,0:T(8,128)S(1)} %eval_jaxpr.9), channel_id=1, source_target_pairs={{0,4},{4,0},{1,5},{5,1},{2,6},{6,2},{3,7},{7,3},{8,12},{12,8},{9,1... | collective-permute-start | bytes 110600 | tf_op jit(solution)/shard_map/while/body/eval_jaxpr/ppermute | solution.py:124
  161.2 2.5 %collective-permute-start.11 = (f32[8,1152]{1,0:T(8,128)S(1)}, f32[8,1152]{1,0:T(8,128)S(1)}, u32[]{:S(2)}, u32[]{:S(2)}) collective-permute-start(f32[8,1152]{1,0:T(8,128)S(1)} %collective-permute-done.7), channel_id=1, source_target_pairs={{0,4},{4,0},{1,5},{5,1},{2,6},{6,2},{3,7},{7,3},{8,12},{12,8},{9,1... | collective-permute-start | bytes 110600 | tf_op jit(solution)/shard_map/while/body/eval_jaxpr/ppermute | solution.py:124
  161.8 2.2 %collective-permute-start.12 = (f32[8,1152]{1,0:T(8,128)S(1)}, f32[8,1152]{1,0:T(8,128)S(1)}, u32[]{:S(2)}, u32[]{:S(2)}) collective-permute-start(f32[8,1152]{1,0:T(8,128)S(1)} %collective-permute-done.8), channel_id=1, source_target_pairs={{0,4},{4,0},{1,5},{5,1},{2,6},{6,2},{3,7},{7,3},{8,12},{12,8},{9,1... | collective-permute-start | bytes 110600 | tf_op jit(solution)/shard_map/while/body/eval_jaxpr/ppermute | solution.py:124
  163.1 1.5 collective-permute-start.13

commit v4 on v3

--- a/solution.py
+++ b/solution.py
@@ -288,7 +288,6 @@
             0,
             0,
         )
-        start_others = snp_others(start)
 
         def right_rows(tiles):
             value = tiles[...]
@@ -301,7 +300,7 @@
                 [*rows, jnp.zeros((GROUP - rank, row_count), F32)], axis=0
             )
 
-        def mix_kernel(place, tiles, om, mixed):
+        def mix_kernel(place, tiles, om, start, mixed):
             right = right_rows(tiles)
             pieces = [
                 exact_dot(
@@ -312,7 +311,8 @@
                 )
                 for j in range(local_blocks)
             ]
-            mixed[...] = jnp.concatenate(pieces, axis=1)
+            mixed[:, :row_count] = start[...]
+            mixed[:, row_count:] = jnp.concatenate(pieces, axis=1)
 
         def build_kernel(place, sizes, bits, scale, obs, left, tiles, x_out):
             right = right_rows(tiles)
@@ -326,9 +326,10 @@
 
         mixed = call_with_place(
             mix_kernel,
-            shape_of((width, local_blocks * GROUP)),
+            shape_of((width, row_count + local_blocks * GROUP)),
             right_tiles,
             omega,
+            start,
         )
         mixed_others = snp_others(mixed)
         left_rows = left_factors.T
@@ -408,19 +409,19 @@
         whole_scratch = [pltpu.VMEM((width, sum_width), F32)]
 
         def first_kernel(
-            place, sizes, bits, scale, own, a, b, c, q0, q1, q2, q3, left, x,
-            samples_out, mine, other,
+            place, sizes, bits, scale, w0, w1, w2, w3, left, x, samples_out, mine, other
         ):
-            samples = own[...] + a[...] + b[...] + c[...]
             batch = batch_ids(place, sizes, (1, row_count), 1)
             weight = weight_rows(scale, left)
-            for k, q in zip((0, *SHIFTS), (q0, q1, q2, q3)):
+            samples = jnp.zeros((width, row_count), F32)
+            for k, ref in zip((0, *SHIFTS), (w0, w1, w2, w3)):
                 source = (place[0] + (snp - k)) % snp
                 masked = [
                     jnp.where(gone_in(bits[source * local_blocks + j], batch), weight, 0.0)
                     for j in range(local_blocks)
                 ]
-                samples = samples + exact_dot(q[...], jnp.concatenate(masked, axis=0), 1, 0)
+                missed = exact_dot(ref[:, row_count:], jnp.concatenate(masked, axis=0), 1, 0)
+                samples = samples + (ref[:, :row_count] + missed)
             samples_out[...] = samples
             write_send(
                 split_dot(samples, x[...], 0),
@@ -442,7 +443,7 @@
             wire[...] = jnp.concatenate([product.astype(BF16), *three_parts(own)], axis=1)
 
         def backward_kernel(
-            place, product, gram, a, b, c, raw, x, samples_out, columns_out, mine, other
+            place, product, gram, a, b, c, x, samples_out, factor_out, mine, other
         ):
             total, own = product[...], gram[...]
             for ref in (a, b, c):
@@ -455,7 +456,7 @@
             factor = inverse_factor(own / snp_count, False)
             samples = exact_dot(factor, total, 1, 0)
             samples_out[...] = samples
-            columns_out[...] = exact_dot(factor, raw[...], 1, 0)
+            factor_out[...] = factor
             write_send(
                 split_dot(samples, x[...], 0),
                 exact_dot(samples, samples, 1, 1),
@@ -464,6 +465,9 @@
                 other,
             )
 
+        def columns_kernel(place, factor, raw, columns):
+            columns[...] = exact_dot(factor[...], raw[...], 1, 0)
+
         def last_kernel(place, *refs):
             tiles, (samples, basis, projection, whole) = refs[: 2 * ring], refs[2 * ring :]
             columns, gram = read_sum(place, tiles, whole)
@@ -476,8 +480,6 @@
         samples, mine, other = call_with_place(
             first_kernel,
             (samples_shape, part_shape, part_shape),
-            start,
-            *start_others,
             mixed,
             *mixed_others,
             left_rows,
@@ -497,15 +499,15 @@
                 matrix,
                 scratch=whole_scratch,
             )
-            samples, columns, mine, other = call_with_place(
+            samples, factor, mine, other = call_with_place(
                 backward_kernel,
-                (samples_shape, columns_shape, part_shape, part_shape),
+                (samples_shape, shape_of((width, width)), part_shape, part_shape),
                 product,
                 gram,
                 *snp_others(wire),
-                raw,
                 matrix,
             )
+            columns = call_with_place(columns_kernel, columns_shape, factor, raw)
             return samp_sum(mine, other, BF16), samples, columns
 
         tiles, samples, columns = lax.fori_loop(

time: 169 us -> 168 us (level)
  starting transfers between devices: 75.4 us -> 71.2 us
  Pallas kernels: 26.5 us -> 28.3 us
  waiting for transfers between devices: 28 us -> 29.8 us
    all_to_all x1, waiting for transfers between devices: 0.4 us -> 6.08 us  [on_device(): lax.all_to_all(call_with_place(pack_kernel, shape_of((chips, SUB, LANES))...]
    ppermute x12 -> x9, starting transfers between devices: 17.8 us -> 14.7 us  [snp_others(): lax.ppermute(value, 'snp', [(i, (i + k) % snp) for i in range(snp)])]
    ppermute x16, waiting for transfers between devices: 6.98 us -> 5.06 us  [swap(): return lax.ppermute(value, 'core', [(0, 1), (1, 0)])]
    pallas_call x18 -> x20, Pallas kernels: 23.3 us -> 25.1 us  [call_with_place(): pl.pallas_call(body, out_shape=outs, in_specs=specs, scratch_shapes=scrat...]
    ppermute x12 -> x9, waiting for transfers between devices: 11.8 us -> 10 us  [snp_others(): lax.ppermute(value, 'snp', [(i, (i + k) % snp) for i in range(snp)])]
  transfers between devices with their start and end apart: 47 -> 44, of which waited for: 22 -> 21; matrix products, arithmetic and copies ran while one was open for 0% -> 0% of each run, Pallas kernels for 4% -> 5%
where the time goes in v4:
time: 168 us
  starting transfers between devices  71.2 us (42%)
  blocking collectives  33.8 us (20%)
  waiting for transfers between devices  29.8 us (18%)
  Pallas kernels  28.3 us (17%)
  local copies, waits for them, and re-layouts  3.61 us (2%)
    all_to_all x3, blocking collectives, samp_sum(): lax.all_to_all(spread, 'z', 0, 0)  33.8 us
    ppermute x16, starting transfers between devices, swap(): return lax.ppermute(value, 'core', [(0, 1), (1, 0)])  26.2 us
    pallas_call x20, Pallas kernels, call_with_place(): pl.pallas_call(body, out_shape=outs, in_specs=specs, scratch_shapes=scrat...  25.1 us
    ppermute x18, starting transfers between devices, x_shift(): return lax.ppermute(value, 'x', [(i, (i + k) % ring) for i in range(ring)])  21.1 us
    ppermute x9, starting transfers between devices, snp_others(): lax.ppermute(value, 'snp', [(i, (i + k) % snp) for i in range(snp)])  14.7 us
    ppermute x9, waiting for transfers between devices, snp_others(): lax.ppermute(value, 'snp', [(i, (i + k) % snp) for i in range(snp)])  10 us
    all_to_all x1, starting transfers between devices, on_device(): lax.all_to_all(call_with_place(pack_kernel, shape_of((chips, SUB, LANES))...  9.3 us
    ppermute x18, waiting for transfers between devices, x_shift(): return lax.ppermute(value, 'x', [(i, (i + k) % ring) for i in range(ring)])  8.62 us
  transfers between devices with their start and end apart: 44, of which 21 were waited for; matrix products, arithmetic and copies ran while one was open for 0% of the time, Pallas kernels for 5%

profile of v4, /device:TPU:1, one launch (start us, length us, event | category | flops | bytes accessed | tf_op | source)
XLA Modules:
  0.0 167.6 jit_solution(11171004329147500738)
XLA Ops:
  0.6 3.3 %collective-permute-start.14 = (f32[16,20]{1,0:T(8,128)}, f32[16,20]{1,0:T(8,128)S(1)}, u32[]{:S(2)}, u32[]{:S(2)}) collective-permute-start(f32[16,20]{1,0:T(8,128)} %mine.1), channel_id=1, source_target_pairs={{0,4},{4,0},{1,5},{5,1},{2,6},{6,2},{3,7},{7,3},{8,12},{12,8},{9,1... | collective-permute-start | bytes 3848 | tf_op jit(solution)/shard_map/ppermute | solution.py:124
  4.0 1.0 collective-permute-done.14.other
  5.0 0.7 copy-done.4
  5.7 0.7 shard_map.113
  6.4 9.3 %all-to-all-start.1 = ((f32[32,8,128]{2,1,0:T(8,128)}), f32[32,8,128]{2,1,0:T(8,128)S(1)}, u32[]{:S(2)}, u32[]{:S(2)}) async-start(f32[32,8,128]{2,1,0:T(8,128)} %shard_map.113), calls=%async_computation.1 | async-start | bytes 262144 | tf_op jit(solution)/shard_map/all_to_all | solution.py:280
  15.8 3.2 %shard_map.112 = (bf16[640,1024]{1,0:T(8,128)(2,1)}, f32[64,640]{1,0:T(8,128)}, s32[16]{0:T(128)}) custom-call(s32[1]{0:T(128)} %bitcast.place, s32[12]{0:T(128)} %sizes.3, s32[48]{0:T(128)} %batch_in.1, s32[48]{0:T(128)} %block_in.1, s32[640,1024]{1,0:T(8,128)} %geno_in.1, f32[1,1024]{1,0:T(1,128)} %bitcast.11, bf16[64,1024]{1,0:T(8,128)(2,1)} %bitcast.7), custom_call_target="tpu_custom_call" | custom-call | tf_op jit(solution)/shard_map/pallas_call | solution.py:239
  19.0 6.1 %all-to-all-done.1.tiles = f32[32,8,128]{2,1,0:T(8,128)S(1)} async-done(((f32[32,8,128]{2,1,0:T(8,128)}), f32[32,8,128]{2,1,0:T(8,128)S(1)}, u32[]{:S(2)}, u32[]{:S(2)}) %all-to-all-start.1) | async-done | bytes 131104 | tf_op jit(solution)/shard_map/all_to_all | solution.py:280
  25.1 0.9 copy-done.3
  26.5 3.0 %collective-permute-start.15 = (f32[64,768]{1,0:T(8,128)S(1)}, f32[64,768]{1,0:T(8,128)S(1)}, u32[]{:S(2)}, u32[]{:S(2)}) collective-permute-start(f32[64,768]{1,0:T(8,128)S(1)} %shard_map.114.w0), channel_id=1, source_target_pairs={{0,2},{1,3},{2,0},{3,1},{4,6},{5,7},{6,4},{7,5},{8,10},{9,11},{10,... | collective-permute-start | bytes 589832 | tf_op jit(solution)/shard_map/ppermute | solution.py:128
  29.9 2.3 %collective-permute-start.17 = (f32[64,768]{1,0:T(8,128)S(1)}, f32[64,768]{1,0:T(8,128)S(1)}, u32[]{:S(2)}, u32[]{:S(2)}) collective-permute-start(f32[64,768]{1,0:T(8,128)S(1)} %shard_map.114.w0), channel_id=1, source_target_pairs={{0,3},{1,0},{2,1},{3,2},{4,7},{5,4},{6,5},{7,6},{8,11},{9,8},{10,9... | collective-permute-start | bytes 589832 | tf_op jit(solution)/shard_map/ppermute | solution.py:128
  32.2 1.3 copy-done
  34.2 2.9 %shard_map.115.x = bf16[640,1024]{1,0:T(8,128)(2,1)S(1)} custom-call(s32[1]{0:T(128)} %bitcast.place, s32[12]{0:T(128)S(1)} %copy-done.5, s32[16]{0:T(128)S(1)} %copy-done.7, f32[20]{0:T(128)S(1)} %copy-done.6, bf16[640,1024]{1,0:T(8,128)(2,1)S(1)} %copy-done, f32[20,640]{1,0:T(8,128)S(1)} %bitcast.9, f32[32,8,128]{2,1,0:T(8,128)S(1)} %all-to-all-done.1.tiles), custom_call_target="tpu_custom_call" | custom-call | tf_op jit(solution)/shard_map/pallas_call | solution.py:166
  37.1 1.2 collective-permute-done.16.w2
  38.3 2.2 %shard_map.116 = (f32[64,640]{1,0:T(8,128)}, f32[32,1152]{1,0:T(8,128)S(1)}, f32[32,1152]{1,0:T(8,128)S(1)}) custom-call(s32[1]{0:T(128)} %bitcast.place, s32[12]{0:T(128)S(1)} %copy-done.5, s32[16]{0:T(128)S(1)} %copy-done.7, f32[20]{0:T(128)S(1)} %copy-done.6, f32[64,768]{1,0:T(8,128)S(1)} %shard_map.114.w0, f32[64,768]{1,0:T(8,128)S(1)} %collective-permute-done.15.w1, ...), custom_call_target="tpu_custom_call" | custom-call | tf_op jit(solution)/shard_map/pallas_call | solution.py:166
  40.5 1.9 %collective-permute-start.18 = (f32[32,1152]{1,0:T(8,128)S(1)}, f32[32,1152]{1,0:T(8,128)S(1)}, u32[]{:S(2)}, u32[]{:S(2)}) collective-permute-start(f32[32,1152]{1,0:T(8,128)S(1)} %get-tuple-element.105), channel_id=1, source_target_pairs={{0,4},{4,0},{1,5},{5,1},{2,6},{6,2},{3,7},{7,3},{8,12},{12,8},{9,1... | collective-permute-start | bytes 442376 | tf_op jit(solution)/shard_map/ppermute | solution.py:124
  42.4 1.0 collective-permute-done.18.got
  43.5 2.7 %collective-permute-start.20 = (f32[8,1152]{1,0:T(8,128)S(1)}, f32[8,1152]{1,0:T(8,128)S(1)}, u32[]{:S(2)}, u32[]{:S(2)}) collective-permute-start(f32[8,1152]{1,0:T(8,128)S(1)} %get-tuple-element.108), channel_id=1, source_target_pairs={{0,24},{8,0},{16,8},{24,16},{1,25},{9,1},{17,9},{25,17},{2,26},{10... | collective-permute-start | bytes 110600 | tf_op jit(solution)/shard_map/ppermute | solution.py:133
  46.2 1.3 collective-permute-done.19.a
  47.5 3.0 %collective-permute-done.21.c = f32[8,1152]{1,0:T(8,128)S(1)} collective-permute-done((f32[8,1152]{1,0:T(8,128)S(1)}, f32[8,1152]{1,0:T(8,128)S(1)}, u32[]{:S(2)}, u32[]{:S(2)}) %collective-permute-start.21) | collective-permute-done | bytes 36896 | tf_op jit(solution)/shard_map/ppermute | solution.py:133
  50.5 12.4 %all_to_all.16.parts = f32[8,8,1152]{2,1,0:T(8,128)S(1)} all-to-all(f32[8,8,1152]{2,1,0:T(8,128)S(1)} %shard_map.118), channel_id=1, replica_groups=mesh['z'=8,'x'=4,'core'=2,'snp'=4] {'z'}, dimensions={0} | all-to-all | bytes 589824 | tf_op jit(solution)/shard_map/all_to_all | solution.py:396
  63.3 2.7 %collective-permute-start.24 = (f32[8,1152]{1,0:T(8,128)S(1)}, f32[8,1152]{1,0:T(8,128)S(1)}, u32[]{:S(2)}, u32[]{:S(2)}) collective-permute-start(f32[8,1152]{1,0:T(8,128)S(1)} %shard_map.119), channel_id=1, source_target_pairs={{0,24},{8,0},{16,8},{24,16},{1,25},{9,1},{17,9},{25,17},{2,26},{10... | collective-permute-start | bytes 110600 | tf_op jit(solution)/shard_map/ppermute | solution.py:133
  65.9 4.3 %collective-permute-start.25 = (f32[8,1152]{1,0:T(8,128)S(1)}, f32[8,1152]{1,0:T(8,128)S(1)}, u32[]{:S(2)}, u32[]{:S(2)}) collective-permute-start(f32[8,1152]{1,0:T(8,128)S(1)} %shard_map.119), channel_id=1, source_target_pairs={{0,4},{4,0},{1,5},{5,1},{2,6},{6,2},{3,7},{7,3},{8,12},{12,8},{9,1... | collective-permute-start | bytes 110600 | tf_op jit(solution)/shard_map/ppermute | solution.py:124
  70.3 2.0 %collective-permute-start.26 = (f32[8,1152]{1,0:T(8,128)S(1)}, f32[8,1152]{1,0:T(8,128)S(1)}, u32[]{:S(2)}, u32[]{:S(2)}) collective-permute-start(f32[8,1152]{1,0:T(8,128)S(1)} %collective-permute-done.22), channel_id=1, source_target_pairs={{0,4},{4,0},{1,5},{5,1},{2,6},{6,2},{3,7},{7,3},{8,12},{12,8},{9,1... | collective-permute-start | bytes 110600 | tf_op jit(solution)/shard_map/ppermute | solution.py:124
  73.8 89.9 %while.28 = (s32[]{:T(128)}, f32[8,1152]{1,0:T(8,128)S(1)}, f32[8,1152]{1,0:T(8,128)S(1)}, f32[8,1152]{1,0:T(8,128)S(1)}, f32[8,1152]{1,0:T(8,128)S(1)}, /*index...) while((s32[]{:T(128)}, f32[8,1152]{1,0:T(8,128)S(1)}, ...), condition=%wide.region_1.0_spmd, body=%wide.region_0.0_spmd.sunk | while | flops 2 | bytes 3670709 | solution.py:513
  73.8 2.9 %eval_jaxpr.6 = (f32[64,1024]{1,0:T(8,128)S(1)}, f32[64,640]{1,0:T(8,128)S(1)}, f32[64,64]{1,0:T(8,128)S(1)}, bf16[64,832]{1,0:T(8,128)(2,1)S(1)}) custom-call(s32[1]{0:T(128)} %get-tuple-element.287.place, f32[8,1152]{1,0:T(8,128)S(1)} %get-tuple-element.263.refs_0_, f32[8,1152]{1,0:T(8,128)S(1)} %get-tuple-element.264.refs_1_, ...), custom_call_target="tpu_custom_call" | custom-call | tf_op jit(solution)/shard_map/while/body/eval_jaxpr/pallas_call | solution.py:166
  76.7 1.9 %collective-permute-start = (bf16[64,832]{1,0:T(8,128)(2,1)S(1)}, bf16[64,832]{1,0:T(8,128)(2,1)S(1)}, u32[]{:S(2)}, u32[]{:S(2)}) collective-permute-start(bf16[64,832]{1,0:T(8,128)(2,1)S(1)} %get-tuple-element.238), channel_id=1, source_target_pairs={{0,2},{1,3},{2,0},{3,1},{4,6},{5,7},{6,4},{7,5},{8,10},{9,11},{10,... | collective-permute-start | bytes 319496 | tf_op jit(solution)/shard_map/while/body/eval_jaxpr/ppermute | solution.py:128
  78.5 1.3 collective-permute-start.1
  79.8 1.4 collective-permute-start.2
  81.2 1.5 collective-permute-done.a
  82.7 2.8 %collective-permute-done.1.b = bf16[64,832]{1,0:T(8,128)(2,1)S(1)} collective-permute-done((bf16[64,832]{1,0:T(8,128)(2,1)S(1)}, bf16[64,832]{1,0:T(8,128)(2,1)S(1)}, u32[]{:S(2)}, u32[]{:S(2)}) %collective-permute-start.1) | collective-permute-done | bytes 106528 | tf_op jit(solution)/shard_map/while/body/eval_jaxpr/ppermute | solution.py:128
  85.5 3.2 %eval_jaxpr.7 = (f32[64,640]{1,0:T(8,128)}, f32[64,64]{1,0:T(8,128)S(1)}, f32[32,1152]{1,0:T(8,128)S(1)}, f32[32,1152]{1,0:T(8,128)S(1)}) custom-call(s32[1]{0:T(128)} %get-tuple-element.287.place, f32[64,640]{1,0:T(8,128)S(1)} %get-tuple-element.236.product, f32[64,64]{1,0:T(8,128)S(1)} %get-tuple-element.237.gram, ...), custom_call_target="tpu_custom_call" | custom-call | tf_op jit(solution)/shard_map/while/body/eval_jaxpr/pallas_call | solution.py:166
  88.7 0.8 collective-permute-start.3
  89.5 1.0 collective-permute-done.3.got
  90.6 1.4 collective-permute-start.4
  92.0 1.4 collective-permute-start.5
  93.4 1.3 collective-permute-start.6
  95.0 1.2 collective-permute-done.5.b
  96.3 10.8 %all_to_all.17.parts = bf16[8,8,1280]{2,1,0:T(8,128)(2,1)S(1)} all-to-all(bf16[8,8,1280]{2,1,0:T(8,128)(2,1)S(1)} %eval_jaxpr.9), channel_id=1, replica_groups=mesh['z'=8,'x'=4,'core'=2,'snp'=4] {'z'}, dimensions={0} | all-to-all | bytes 327680 | tf_op jit(solution)/shard_map/while/body/eval_jaxpr/all_to_all | solution.py:396
  107.2 1.8 %collective-permute-start.7 = (f32[8,1152]{1,0:T(8,128)S(1)}, f32[8,1152]{1,0:T(8,128)S(1)}, u32[]{:S(2)}, u32[]{:S(2)}) collective-permute-start(f32[8,1152]{1,0:T(8,128)S(1)} %eval_jaxpr.10), channel_id=1, source_target_pairs={{0,16},{8,24},{16,0},{24,8},{1,17},{9,25},{17,1},{25,9},{2,18},{10... | collective-permute-start | bytes 110600 | tf_op jit(solution)/shard_map/while/body/eval_jaxpr/ppermute | solution.py:133
  109.0 1.3 collective-permute-start.8
  110.3 1.4 collective-permute-start.9
  111.7 4.0 %collective-permute-start.10 = (f32[8,1152]{1,0:T(8,128)S(1)}, f32[8,1152]{1,0:T(8,128)S(1)}, u32[]{:S(2)}, u32[]{:S(2)}) collective-permute-start(f32[8,1152]{1,0:T(8,128)S(1)} %eval_jaxpr.10), channel_id=1, source_target_pairs={{0,4},{4,0},{1,5},{5,1},{2,6},{6,2},{3,7},{7,3},{8,12},{12,8},{9,1... | collective-permute-start | bytes 110600 | tf_op jit(solution)/shard_map/while/body/eval_jaxpr/ppermute | solution.py:124
  115.8 1.7 %collective-permute-start.12 = (f32[8,1152]{1,0:T(8,128)S(1)}, f32[8,1152]{1,0:T(8,128)S(1)}, u32[]{:S(2)}, u32[]{:S(2)}) collective-permute-start(f32[8,1152]{1,0:T(8,128)S(1)} %collective-permute-done.8), channel_id=1, source_target_pairs={{0,4},{4,0},{1,5},{5,1},{2,6},{6,2},{3,7},{7,3},{8,12},{12,8},{9,1... | collective-permute-start | bytes 110600 | tf_op jit(solution)/shard_map/while/body/eval_jaxpr/ppermute | solution.py:124
  117.9 1.1 eval_jaxpr.11
  119.0 2.9 %eval_jaxpr.6 = (f32[64,1024]{1,0:T(8,128)S(1)}, f32[64,640]{1,0:T(8,128)S(1)}, f32[64,64]{1,0:T(8,128)S(1)}, bf16[64,832]{1,0:T(8,128)(2,1)S(1)}) custom-call(s32[1]{0:T(128)} %get-tuple-element.287.place, f32[8,1152]{1,0:T(8,128)S(1)} %get-tuple-element.263.refs_0_, f32[8,1152]{1,0:T(8,128)S(1)} %get-tuple-element.264.refs_1_, ...), custom_call_target="tpu_custom_call" | custom-call | tf_op jit(solution)/shard_map/while/body/eval_jaxpr/pallas_call | solution.py:166
  121.9 1.8 %collective-permute-start = (bf16[64,832]{1,0:T(8,128)(2,1)S(1)}, bf16[64,832]{1,0:T(8,128)(2,1)S(1)}, u32[]{:S(2)}, u32[]{:S(2)}) collective-permute-start(bf16[64,832]{1,0:T(8,128)(2,1)S(1)} %get-tuple-element.238), channel_id=1, source_target_pairs={{0,2},{1,3},{2,0},{3,1},{4,6},{5,7},{6,4},{7,5},{8,10},{9,11},{10,... | collective-permute-start | bytes 319496 | tf_op jit(solution)/shard_map/while/body/eval_jaxpr/ppermute | solution.py:128
  123.7 1.2 collective-permute-start.1
  124.9 1.4 collective-permute-start.2
  126.3 1.7 %collective-permute-done.a = bf16[64,832]{1,0:T(8,128)(2,1)S(1)} collective-permute-done((bf16[64,832]{1,0:T(8,128)(2,1)S(1)}, bf16[64,832]{1,0:T(8,128)(2,1)S(1)}, u32[]{:S(2)}, u32[]{:S(2)}) %collective-permute-start) | collective-permute-done | bytes 106528 | tf_op jit(solution)/shard_map/while/body/eval_jaxpr/ppermute | solution.py:128
  128.0 2.8 %collective-permute-done.1.b = bf16[64,832]{1,0:T(8,128)(2,1)S(1)} collective-permute-done((bf16[64,832]{1,0:T(8,128)(2,1)S(1)}, bf16[64,832]{1,0:T(8,128)(2,1)S(1)}, u32[]{:S(2)}, u32[]{:S(2)}) %collective-permute-start.1) | collective-permute-done | bytes 106528 | tf_op jit(solution)/shard_map/while/body/eval_jaxpr/ppermute | solution.py:128
  130.9 3.2 %eval_jaxpr.7 = (f32[64,640]{1,0:T(8,128)}, f32[64,64]{1,0:T(8,128)S(1)}, f32[32,1152]{1,0:T(8,128)S(1)}, f32[32,1152]{1,0:T(8,128)S(1)}) custom-call(s32[1]{0:T(128)} %get-tuple-element.287.place, f32[64,640]{1,0:T(8,128)S(1)} %get-tuple-element.236.product, f32[64,64]{1,0:T(8,128)S(1)} %get-tuple-element.237.gram, ...), custom_call_target="tpu_custom_call" | custom-call | tf_op jit(solution)/shard_map/while/body/eval_jaxpr/pallas_call | solution.py:166
  134.7 1.0 collective-permute-done.3.got
  135.7 1.0 collective-permute-start.4
  136.7 2.3 %collective-permute-start.5 = (f32[8,1152]{1,0:T(8,128)S(1)}, f32[8,1152]{1,0:T(8,128)S(1)}, u32[]{:S(2)}, u32[]{:S(2)}) collective-permute-start(f32[8,1152]{1,0:T(8,128)S(1)} %get-tuple-element.243), channel_id=1, source_target_pairs={{0,8},{8,16},{16,24},{24,0},{1,9},{9,17},{17,25},{25,1},{2,10},{10... | collective-permute-start | bytes 110600 | tf_op jit(solution)/shard_map/while/body/eval_jaxpr/ppermute | solution.py:133
  139.3 0.8 collective-permute-done.4.a
  140.1 1.1 collective-permute-done.5.b
  141.2 0.9 collective-permute-done.6.c
  142.2 10.7 %all_to_all.17.parts = bf16[8,8,1280]{2,1,0:T(8,128)(2,1)S(1)} all-to-all(bf16[8,8,1280]{2,1,0:T(8,128)(2,1)S(1)} %eval_jaxpr.9), channel_id=1, replica_groups=mesh['z'=8,'x'=4,'core'=2,'snp'=4] {'z'}, dimensions={0} | all-to-all | bytes 327680 | tf_op jit(solution)/shard_map/while/body/eval_jaxpr/all_to_all | solution.py:396
  153.4 2.0 %collective-permute-start.8 = (f32[8,1152]{1,0:T(8,128)S(1)}, f32[8,1152]{1,0:T(8,128)S(1)}, u32[]{:S(2)}, u32[]{:S(2)}) collective-permute-start(f32[8,1152]{1,0:T(8,128)S(1)} %eval_jaxpr.10), channel_id=1, source_target_pairs={{0,8},{8,16},{16,24},{24,0},{1,9},{9,17},{17,25},{25,1},{2,10},{10... | collective-permute-start | bytes 110600 | tf_op jit(solution)/shard_map/while/body/eval_jaxpr/ppermute | solution.py:133
  156.1 3.7 %collective-permute-start.10 = (f32[8,1152]{1,0:T(8,128)S(1)}, f32[8,1152]{1,0:T(8,128)S(1)}, u32[]{:S(2)}, u32[]{:S(2)}) collective-permute-start(f32[8,1152]{1,0:T(8,128)S(1)} %eval_jaxpr.10), channel_id=1, source_target_pairs={{0,4},{4,0},{1,5},{5,1},{2,6},{6,2},{3,7},{7,3},{8,12},{12,8},{9,1... | collective-permute-start | bytes 110600 | tf_op jit(solution)/shard_map/while/body/eval_jaxpr/ppermute | solution.py:124
  159.9 1.5 collective-permute-start.11
  161.8 0.8 collective-permute-start.13
  162.6 1.1 eval_jaxpr.11
  163.7 3.9 %shard_map.120 = (f32[64,640]{1,0:T(8,128)}, f32[64,1024]{1,0:T(8,128)}) custom-call(s32[1]{0:T(128)} %bitcast.place, f32[8,1152]{1,0:T(8,128)S(1)} %get-tuple-element.111.refs_0_, f32[8,1152]{1,0:T(8,128)S(1)} %get-tuple-element.112.refs_1_, f32[8,1152]{1,0:T(8,128)S(1)} %get-tuple-element.113.refs_2_, f32[8,1152]{1,0:T(8,128)S(1)} %get-tuple-element.114.refs_3_, ...), custom_call_target="tpu_custom_call" | custom-call | tf_op jit(solution)/shard_map/pallas_call | solution.py:166
  (66 shorter events, 7.5 us)
Async XLA Ops:
  0.6 4.4 %collective-permute-start.14 = (f32[16,20]{1,0:T(8,128)}, f32[16,20]{1,0:T(8,128)S(1)}, u32[]{:S(2)}, u32[]{:S(2)}) collective-permute-start(f32[16,20]{1,0:T(8,128)} %mine.1), channel_id=1, source_target_pairs={{0,4},{4,0},{1,5},{5,1},{2,6},{6,2},{3,7},{7,3},{8,12},{12,8},{9,1... | collective-permute-start | bytes 3848 | tf_op jit(solution)/shard_map/ppermute | solution.py:124
  5.0 0.7 copy-start.4
  6.4 18.7 %all-to-all-start.1 = ((f32[32,8,128]{2,1,0:T(8,128)}), f32[32,8,128]{2,1,0:T(8,128)S(1)}, u32[]{:S(2)}, u32[]{:S(2)}) async-start(f32[32,8,128]{2,1,0:T(8,128)} %shard_map.113), calls=%async_computation.1 | async-start | bytes 262144 | tf_op jit(solution)/shard_map/all_to_all | solution.py:280
  15.7 9.3 %copy-start.1 = (bf16[1024,64]{0,1:T(8,128)(2,1)S(1)}, bf16[1024,64]{0,1:T(8,128)(2,1)}, u32[]{:S(2)}) copy-start(bf16[1024,64]{0,1:T(8,128)(2,1)} %param.16) | copy-start | bytes 393220
  15.8 16.5 %copy-start.2 = (f32[640,20]{0,1:T(8,128)S(1)}, f32[640,20]{0,1:T(8,128)}, u32[]{:S(2)}) copy-start(f32[640,20]{0,1:T(8,128)} %param.13) | copy-start | bytes 153604
  15.8 16.5 %copy-start.5 = (s32[12]{0:T(128)S(1)}, s32[12]{0:T(128)}, u32[]{:S(2)}) copy-start(s32[12]{0:T(128)} %sizes.3) | copy-start | bytes 148
  15.8 16.4 %copy-start.6 = (f32[20]{0:T(128)S(1)}, f32[20]{0:T(128)}, u32[]{:S(2)}) copy-start(f32[20]{0:T(128)} %scale.3) | copy-start | bytes 244
  25.1 0.9 copy-start.3
  26.5 10.6 %collective-permute-start.15 = (f32[64,768]{1,0:T(8,128)S(1)}, f32[64,768]{1,0:T(8,128)S(1)}, u32[]{:S(2)}, u32[]{:S(2)}) collective-permute-start(f32[64,768]{1,0:T(8,128)S(1)} %shard_map.114.w0), channel_id=1, source_target_pairs={{0,2},{1,3},{2,0},{3,1},{4,6},{5,7},{6,4},{7,5},{8,10},{9,11},{10,... | collective-permute-start | bytes 589832 | tf_op jit(solution)/shard_map/ppermute | solution.py:128
  29.5 8.8 %collective-permute-start.16 = (f32[64,768]{1,0:T(8,128)S(1)}, f32[64,768]{1,0:T(8,128)S(1)}, u32[]{:S(2)}, u32[]{:S(2)}) collective-permute-start(f32[64,768]{1,0:T(8,128)S(1)} %shard_map.114.w0), channel_id=1, source_target_pairs={{0,1},{1,2},{2,3},{3,0},{4,5},{5,6},{6,7},{7,4},{8,9},{9,10},{10,1... | collective-permute-start | bytes 589832 | tf_op jit(solution)/shard_map/ppermute | solution.py:128
  29.9 8.4 %collective-permute-start.17 = (f32[64,768]{1,0:T(8,128)S(1)}, f32[64,768]{1,0:T(8,128)S(1)}, u32[]{:S(2)}, u32[]{:S(2)}) collective-permute-start(f32[64,768]{1,0:T(8,128)S(1)} %shard_map.114.w0), channel_id=1, source_target_pairs={{0,3},{1,0},{2,1},{3,2},{4,7},{5,4},{6,5},{7,6},{8,11},{9,8},{10,9... | collective-permute-start | bytes 589832 | tf_op jit(solution)/shard_map/ppermute | solution.py:128
  32.2 1.3 copy-start
  33.5 0.7 copy-start.7
  40.5 2.9 %collective-permute-start.18 = (f32[32,1152]{1,0:T(8,128)S(1)}, f32[32,1152]{1,0:T(8,128)S(1)}, u32[]{:S(2)}, u32[]{:S(2)}) collective-permute-start(f32[32,1152]{1,0:T(8,128)S(1)} %get-tuple-element.105), channel_id=1, source_target_pairs={{0,4},{4,0},{1,5},{5,1},{2,6},{6,2},{3,7},{7,3},{8,12},{12,8},{9,1... | collective-permute-start | bytes 442376 | tf_op jit(solution)/shard_map/ppermute | solution.py:124
  43.4 4.1 %collective-permute-start.19 = (f32[8,1152]{1,0:T(8,128)S(1)}, f32[8,1152]{1,0:T(8,128)S(1)}, u32[]{:S(2)}, u32[]{:S(2)}) collective-permute-start(f32[8,1152]{1,0:T(8,128)S(1)} %get-tuple-element.107), channel_id=1, source_target_pairs={{0,8},{8,16},{16,24},{24,0},{1,9},{9,17},{17,25},{25,1},{2,10},{10... | collective-permute-start | bytes 110600 | tf_op jit(solution)/shard_map/ppermute | solution.py:133
  43.5 4.0 %collective-permute-start.20 = (f32[8,1152]{1,0:T(8,128)S(1)}, f32[8,1152]{1,0:T(8,128)S(1)}, u32[]{:S(2)}, u32[]{:S(2)}) collective-permute-start(f32[8,1152]{1,0:T(8,128)S(1)} %get-tuple-element.108), channel_id=1, source_target_pairs={{0,24},{8,0},{16,8},{24,16},{1,25},{9,1},{17,9},{25,17},{2,26},{10... | collective-permute-start | bytes 110600 | tf_op jit(solution)/shard_map/ppermute | solution.py:133
  46.2 4.3 %collective-permute-start.21 = (f32[8,1152]{1,0:T(8,128)S(1)}, f32[8,1152]{1,0:T(8,128)S(1)}, u32[]{:S(2)}, u32[]{:S(2)}) collective-permute-start(f32[8,1152]{1,0:T(8,128)S(1)} %get-tuple-element.109), channel_id=1, source_target_pairs={{0,16},{8,24},{16,0},{24,8},{1,17},{9,25},{17,1},{25,9},{2,18},{10... | collective-permute-start | bytes 110600 | tf_op jit(solution)/shard_map/ppermute | solution.py:133
  62.9 7.3 %collective-permute-start.22 = (f32[8,1152]{1,0:T(8,128)S(1)}, f32[8,1152]{1,0:T(8,128)S(1)}, u32[]{:S(2)}, u32[]{:S(2)}) collective-permute-start(f32[8,1152]{1,0:T(8,128)S(1)} %shard_map.119), channel_id=1, source_target_pairs={{0,16},{8,24},{16,0},{24,8},{1,17},{9,25},{17,1},{25,9},{2,18},{10... | collective-permute-start | bytes 110600 | tf_op jit(solution)/shard_map/ppermute | solution.py:133
  63.0 9.3 %collective-permute-start.23 = (f32[8,1152]{1,0:T(8,128)S(1)}, f32[8,1152]{1,0:T(8,128)S(1)}, u32[]{:S(2)}, u32[]{:S(2)}) collective-permute-start(f32[8,1152]{1,0:T(8,128)S(1)} %shard_map.119), channel_id=1, source_target_pairs={{0,8},{8,16},{16,24},{24,0},{1,9},{9,17},{17,25},{25,1},{2,10},{10... | collective-permute-start | bytes 110600 | tf_op jit(solution)/shard_map/ppermute | solution.py:133
  63.3 9.3 %collective-permute-start.24 = (f32[8,1152]{1,0:T(8,128)S(1)}, f32[8,1152]{1,0:T(8,128)S(1)}, u32[]{:S(2)}, u32[]{:S(2)}) collective-permute-start(f32[8,1152]{1,0:T(8,128)S(1)} %shard_map.119), channel_id=1, source_target_pairs={{0,24},{8,0},{16,8},{24,16},{1,25},{9,1},{17,9},{25,17},{2,26},{10... | collective-permute-start | bytes 110600 | tf_op jit(solution)/shard_map/ppermute | solution.py:133
  65.9 6.9 %collective-permute-start.25 = (f32[8,1152]{1,0:T(8,128)S(1)}, f32[8,1152]{1,0:T(8,128)S(1)}, u32[]{:S(2)}, u32[]{:S(2)}) collective-permute-start(f32[8,1152]{1,0:T(8,128)S(1)} %shard_map.119), channel_id=1, source_target_pairs={{0,4},{4,0},{1,5},{5,1},{2,6},{6,2},{3,7},{7,3},{8,12},{12,8},{9,1... | collective-permute-start | bytes 110600 | tf_op jit(solution)/shard_map/ppermute | solution.py:124
  70.3 2.9 %collective-permute-start.26 = (f32[8,1152]{1,0:T(8,128)S(1)}, f32[8,1152]{1,0:T(8,128)S(1)}, u32[]{:S(2)}, u32[]{:S(2)}) collective-permute-start(f32[8,1152]{1,0:T(8,128)S(1)} %collective-permute-done.22), channel_id=1, source_target_pairs={{0,4},{4,0},{1,5},{5,1},{2,6},{6,2},{3,7},{7,3},{8,12},{12,8},{9,1... | collective-permute-start | bytes 110600 | tf_op jit(solution)/shard_map/ppermute | solution.py:124
  72.3 1.2 collective-permute-start.27
  72.6 1.2 collective-permute-start.28
  76.7 6.1 %collective-permute-start = (bf16[64,832]{1,0:T(8,128)(2,1)S(1)}, bf16[64,832]{1,0:T(8,128)(2,1)S(1)}, u32[]{:S(2)}, u32[]{:S(2)}) collective-permute-start(bf16[64,832]{1,0:T(8,128)(2,1)S(1)} %get-tuple-element.238), channel_id=1, source_target_pairs={{0,2},{1,3},{2,0},{3,1},{4,6},{5,7},{6,4},{7,5},{8,10},{9,11},{10,... | collective-permute-start | bytes 319496 | tf_op jit(solution)/shard_map/while/body/eval_jaxpr/ppermute | solution.py:128
  78.5 7.0 %collective-permute-start.1 = (bf16[64,832]{1,0:T(8,128)(2,1)S(1)}, bf16[64,832]{1,0:T(8,128)(2,1)S(1)}, u32[]{:S(2)}, u32[]{:S(2)}) collective-permute-start(bf16[64,832]{1,0:T(8,128)(2,1)S(1)} %get-tuple-element.238), channel_id=1, source_target_pairs={{0,1},{1,2},{2,3},{3,0},{4,5},{5,6},{6,7},{7,4},{8,9},{9,10},{10,1... | collective-permute-start | bytes 319496 | tf_op jit(solution)/shard_map/while/body/eval_jaxpr/ppermute | solution.py:128
  79.8 5.7 %collective-permute-start.2 = (bf16[64,832]{1,0:T(8,128)(2,1)S(1)}, bf16[64,832]{1,0:T(8,128)(2,1)S(1)}, u32[]{:S(2)}, u32[]{:S(2)}) collective-permute-start(bf16[64,832]{1,0:T(8,128)(2,1)S(1)} %get-tuple-element.238), channel_id=1, source_target_pairs={{0,3},{1,0},{2,1},{3,2},{4,7},{5,4},{6,5},{7,6},{8,11},{9,8},{10,9... | collective-permute-start | bytes 319496 | tf_op jit(solution)/shard_map/while/body/eval_jaxpr/ppermute | solution.py:128
  88.7 1.8 %collective-permute-start.3 = (f32[32,1152]{1,0:T(8,128)S(1)}, f32[32,1152]{1,0:T(8,128)S(1)}, u32[]{:S(2)}, u32[]{:S(2)}) collective-permute-start(f32[32,1152]{1,0:T(8,128)S(1)} %get-tuple-element.240), channel_id=1, source_target_pairs={{0,4},{4,0},{1,5},{5,1},{2,6},{6,2},{3,7},{7,3},{8,12},{12,8},{9,1... | collective-permute-start | bytes 442376 | tf_op jit(solution)/shard_map/while/body/eval_jaxpr/ppermute | solution.py:124
  90.6 4.4 %collective-permute-start.4 = (f32[8,1152]{1,0:T(8,128)S(1)}, f32[8,1152]{1,0:T(8,128)S(1)}, u32[]{:S(2)}, u32[]{:S(2)}) collective-permute-start(f32[8,1152]{1,0:T(8,128)S(1)} %get-tuple-element.242), channel_id=1, source_target_pairs={{0,16},{8,24},{16,0},{24,8},{1,17},{9,25},{17,1},{25,9},{2,18},{10... | collective-permute-start | bytes 110600 | tf_op jit(solution)/shard_map/while/body/eval_jaxpr/ppermute | solution.py:133
  92.0 4.2 %collective-permute-start.5 = (f32[8,1152]{1,0:T(8,128)S(1)}, f32[8,1152]{1,0:T(8,128)S(1)}, u32[]{:S(2)}, u32[]{:S(2)}) collective-permute-start(f32[8,1152]{1,0:T(8,128)S(1)} %get-tuple-element.243), channel_id=1, source_target_pairs={{0,8},{8,16},{16,24},{24,0},{1,9},{9,17},{17,25},{25,1},{2,10},{10... | collective-permute-start | bytes 110600 | tf_op jit(solution)/shard_map/while/body/eval_jaxpr/ppermute | solution.py:133
  93.4 2.8 %collective-permute-start.6 = (f32[8,1152]{1,0:T(8,128)S(1)}, f32[8,1152]{1,0:T(8,128)S(1)}, u32[]{:S(2)}, u32[]{:S(2)}) collective-permute-start(f32[8,1152]{1,0:T(8,128)S(1)} %get-tuple-element.244), channel_id=1, source_target_pairs={{0,24},{8,0},{16,8},{24,16},{1,25},{9,1},{17,9},{25,17},{2,26},{10... | collective-permute-start | bytes 110600 | tf_op jit(solution)/shard_map/while/body/eval_jaxpr/ppermute | solution.py:133
  107.2 8.4 %collective-permute-start.7 = (f32[8,1152]{1,0:T(8,128)S(1)}, f32[8,1152]{1,0:T(8,128)S(1)}, u32[]{:S(2)}, u32[]{:S(2)}) collective-permute-start(f32[8,1152]{1,0:T(8,128)S(1)} %eval_jaxpr.10), channel_id=1, source_target_pairs={{0,16},{8,24},{16,0},{24,8},{1,17},{9,25},{17,1},{25,9},{2,18},{10... | collective-permute-start | bytes 110600 | tf_op jit(solution)/shard_map/while/body/eval_jaxpr/ppermute | solution.py:133
  109.0 6.8 %collective-permute-start.8 = (f32[8,1152]{1,0:T(8,128)S(1)}, f32[8,1152]{1,0:T(8,128)S(1)}, u32[]{:S(2)}, u32[]{:S(2)}) collective-permute-start(f32[8,1152]{1,0:T(8,128)S(1)} %eval_jaxpr.10), channel_id=1, source_target_pairs={{0,8},{8,16},{16,24},{24,0},{1,9},{9,17},{17,25},{25,1},{2,10},{10... | collective-permute-start | bytes 110600 | tf_op jit(solution)/shard_map/while/body/eval_jaxpr/ppermute | solution.py:133
  110.3 7.3 %collective-permute-start.9 = (f32[8,1152]{1,0:T(8,128)S(1)}, f32[8,1152]{1,0:T(8,128)S(1)}, u32[]{:S(2)}, u32[]{:S(2)}) collective-permute-start(f32[8,1152]{1,0:T(8,128)S(1)} %eval_jaxpr.10), channel_id=1, source_target_pairs={{0,24},{8,0},{16,8},{24,16},{1,25},{9,1},{17,9},{25,17},{2,26},{10... | collective-permute-start | bytes 110600 | tf_op jit(solution)/shard_map/while/body/eval_jaxpr/ppermute | solution.py:133
  111.7 7.3 %collective-permute-start.10 = (f32[8,1152]{1,0:T(8,128)S(1)}, f32[8,1152]{1,0:T(8,128)S(1)}, u32[]{:S(2)}, u32[]{:S(2)}) collective-permute-start(f32[8,1152]{1,0:T(8,128)S(1)} %eval_jaxpr.10), channel_id=1, source_target_pairs={{0,4},{4,0},{1,5},{5,1},{2,6},{6,2},{3,7},{7,3},{8,12},{12,8},{9,1... | collective-permute-start | bytes 110600 | tf_op jit(solution)/shard_map/while/body/eval_jaxpr/ppermute | solution.py:124
  115.6 3.4 %collective-permute-start.11 = (f32[8,1152]{1,0:T(8,128)S(1)}, f32[8,1152]{1,0:T(8,128)S(1)}, u32[]{:S(2)}, u32[]{:S(2)}) collective-permute-start(f32[8,1152]{1,0:T(8,128)S(1)} %collective-permute-done.7), channel_id=1, source_target_pairs={{0,4},{4,0},{1,5},{5,1},{2,6},{6,2},{3,7},{7,3},{8,12},{12,8},{9,1... | collective-permute-start | bytes 110600 | tf_op jit(solution)/shard_map/while/body/eval_jaxpr/ppermute | solution.py:124
  115.8 3.2 %collective-permute-start.12 = (f32[8,1152]{1,0:T(8,128)S(1)}, f32[8,1152]{1,0:T(8,128)S(1)}, u32[]{:S(2)}, u32[]{:S(2)}) collective-permute-start(f32[8,1152]{1,0:T(8,128)S(1)} %collective-permute-done.8), channel_id=1, source_target_pairs={{0,4},{4,0},{1,5},{5,1},{2,6},{6,2},{3,7},{7,3},{8,12},{12,8},{9,1... | collective-permute-start | bytes 110600 | tf_op jit(solution)/shard_map/while/body/eval_jaxpr/ppermute | solution.py:124
  117.6 1.4 collective-permute-start.13
  121.9 6.2 %collective-permute-start = (bf16[64,832]{1,0:T(8,128)(2,1)S(1)}, bf16[64,832]{1,0:T(8,128)(2,1)S(1)}, u32[]{:S(2)}, u32[]{:S(2)}) collective-permute-start(bf16[64,832]{1,0:T(8,128)(2,1)S(1)} %get-tuple-element.238), channel_id=1, source_target_pairs={{0,2},{1,3},{2,0},{3,1},{4,6},{5,7},{6,4},{7,5},{8,10},{9,11},{10,... | collective-permute-start | bytes 319496 | tf_op jit(solution)/shard_map/while/body/eval_jaxpr/ppermute | solution.py:128
  123.7 7.2 %collective-permute-start.1 = (bf16[64,832]{1,0:T(8,128)(2,1)S(1)}, bf16[64,832]{1,0:T(8,128)(2,1)S(1)}, u32[]{:S(2)}, u32[]{:S(2)}) collective-permute-start(bf16[64,832]{1,0:T(8,128)(2,1)S(1)} %get-tuple-element.238), channel_id=1, source_target_pairs={{0,1},{1,2},{2,3},{3,0},{4,5},{5,6},{6,7},{7,4},{8,9},{9,10},{10,1... | collective-permute-start | bytes 319496 | tf_op jit(solution)/shard_map/while/body/eval_jaxpr/ppermute | solution.py:128
  124.9 5.9 %collective-permute-start.2 = (bf16[64,832]{1,0:T(8,128)(2,1)S(1)}, bf16[64,832]{1,0:T(8,128)(2,1)S(1)}, u32[]{:S(2)}, u32[]{:S(2)}) collective-permute-start(bf16[64,832]{1,0:T(8,128)(2,1)S(1)} %get-tuple-element.238), channel_id=1, source_target_pairs={{0,3},{1,0},{2,1},{3,2},{4,7},{5,4},{6,5},{7,6},{8,11},{9,8},{10,9... | collective-permute-start | bytes 319496 | tf_op jit(solution)/shard_map/while/body/eval_jaxpr/ppermute | solution.py:128
  134.1 1.6 collective-permute-start.3
  135.7 4.4 %collective-permute-start.4 = (f32[8,1152]{1,0:T(8,128)S(1)}, f32[8,1152]{1,0:T(8,128)S(1)}, u32[]{:S(2)}, u32[]{:S(2)}) collective-permute-start(f32[8,1152]{1,0:T(8,128)S(1)} %get-tuple-element.242), channel_id=1, source_target_pairs={{0,16},{8,24},{16,0},{24,8},{1,17},{9,25},{17,1},{25,9},{2,18},{10... | collective-permute-start | bytes 110600 | tf_op jit(solution)/shard_map/while/body/eval_jaxpr/ppermute | solution.py:133
  136.7 4.6 %collective-permute-start.5 = (f32[8,1152]{1,0:T(8,128)S(1)}, f32[8,1152]{1,0:T(8,128)S(1)}, u32[]{:S(2)}, u32[]{:S(2)}) collective-permute-start(f32[8,1152]{1,0:T(8,128)S(1)} %get-tuple-element.243), channel_id=1, source_target_pairs={{0,8},{8,16},{16,24},{24,0},{1,9},{9,17},{17,25},{25,1},{2,10},{10... | collective-permute-start | bytes 110600 | tf_op jit(solution)/shard_map/while/body/eval_jaxpr/ppermute | solution.py:133
  139.0 3.1 %collective-permute-start.6 = (f32[8,1152]{1,0:T(8,128)S(1)}, f32[8,1152]{1,0:T(8,128)S(1)}, u32[]{:S(2)}, u32[]{:S(2)}) collective-permute-start(f32[8,1152]{1,0:T(8,128)S(1)} %get-tuple-element.244), channel_id=1, source_target_pairs={{0,24},{8,0},{16,8},{24,16},{1,25},{9,1},{17,9},{25,17},{2,26},{10... | collective-permute-start | bytes 110600 | tf_op jit(solution)/shard_map/while/body/eval_jaxpr/ppermute | solution.py:133
  153.0 6.9 %collective-permute-start.7 = (f32[8,1152]{1,0:T(8,128)S(1)}, f32[8,1152]{1,0:T(8,128)S(1)}, u32[]{:S(2)}, u32[]{:S(2)}) collective-permute-start(f32[8,1152]{1,0:T(8,128)S(1)} %eval_jaxpr.10), channel_id=1, source_target_pairs={{0,16},{8,24},{16,0},{24,8},{1,17},{9,25},{17,1},{25,9},{2,18},{10... | collective-permute-start | bytes 110600 | tf_op jit(solution)/shard_map/while/body/eval_jaxpr/ppermute | solution.py:133
  153.4 8.0 %collective-permute-start.8 = (f32[8,1152]{1,0:T(8,128)S(1)}, f32[8,1152]{1,0:T(8,128)S(1)}, u32[]{:S(2)}, u32[]{:S(2)}) collective-permute-start(f32[8,1152]{1,0:T(8,128)S(1)} %eval_jaxpr.10), channel_id=1, source_target_pairs={{0,8},{8,16},{16,24},{24,0},{1,9},{9,17},{17,25},{25,1},{2,10},{10... | collective-permute-start | bytes 110600 | tf_op jit(solution)/shard_map/while/body/eval_jaxpr/ppermute | solution.py:133
  155.4 6.4 %collective-permute-start.9 = (f32[8,1152]{1,0:T(8,128)S(1)}, f32[8,1152]{1,0:T(8,128)S(1)}, u32[]{:S(2)}, u32[]{:S(2)}) collective-permute-start(f32[8,1152]{1,0:T(8,128)S(1)} %eval_jaxpr.10), channel_id=1, source_target_pairs={{0,24},{8,0},{16,8},{24,16},{1,25},{9,1},{17,9},{25,17},{2,26},{10... | collective-permute-start | bytes 110600 | tf_op jit(solution)/shard_map/while/body/eval_jaxpr/ppermute | solution.py:133
  156.1 7.5 %collective-permute-start.10 = (f32[8,1152]{1,0:T(8,128)S(1)}, f32[8,1152]{1,0:T(8,128)S(1)}, u32[]{:S(2)}, u32[]{:S(2)}) collective-permute-start(f32[8,1152]{1,0:T(8,128)S(1)} %eval_jaxpr.10), channel_id=1, source_target_pairs={{0,4},{4,0},{1,5},{5,1},{2,6},{6,2},{3,7},{7,3},{8,12},{12,8},{9,1... | collective-permute-start | bytes 110600 | tf_op jit(solution)/shard_map/while/body/eval_jaxpr/ppermute | solution.py:124
  159.9 3.8 %collective-permute-start.11 = (f32[8,1152]{1,0:T(8,128)S(1)}, f32[8,1152]{1,0:T(8,128)S(1)}, u32[]{:S(2)}, u32[]{:S(2)}) collective-permute-start(f32[8,1152]{1,0:T(8,128)S(1)} %collective-permute-done.7), channel_id=1, source_target_pairs={{0,4},{4,0},{1,5},{5,1},{2,6},{6,2},{3,7},{7,3},{8,12},{12,8},{9,1... | collective-permute-start | bytes 110600 | tf_op jit(solution)/shard_map/while/body/eval_jaxpr/ppermute | solution.py:124
  161.4 2.3 %collective-permute-start.12 = (f32[8,1152]{1,0:T(8,128)S(1)}, f32[8,1152]{1,0:T(8,128)S(1)}, u32[]{:S(2)}, u32[]{:S(2)}) collective-permute-start(f32[8,1152]{1,0:T(8,128)S(1)} %collective-permute-done.8), channel_id=1, source_target_pairs={{0,4},{4,0},{1,5},{5,1},{2,6},{6,2},{3,7},{7,3},{8,12},{12,8},{9,1... | collective-permute-start | bytes 110600 | tf_op jit(solution)/shard_map/while/body/eval_jaxpr/ppermute | solution.py:124
  161.8 1.9 %collective-permute-start.13 = (f32[8,1152]{1,0:T(8,128)S(1)}, f32[8,1152]{1,0:T(8,128)S(1)}, u32[]{:S(2)}, u32[]{:S(2)}) collective-permute-start(f32[8,1152]{1,0:T(8,128)S(1)} %collective-permute-done.9), channel_id=1, source_target_pairs={{0,4},{4,0},{1,5},{5,1},{2,6},{6,2},{3,7},{7,3},{8,12},{12,8},{9,1... | collective-permute-start | bytes 110600 | tf_op jit(solution)/shard_map/while/body/eval_jaxpr/ppermute | solution.py:124

commit v5 on v4

--- a/solution.py
+++ b/solution.py
@@ -254,7 +254,7 @@
                 pltpu.VMEM((width, col_width), BF16),
                 pltpu.SemaphoreType.DMA((5 + row_count // chunk,)),
             ],
-            compiler_params=pltpu.CompilerParams(vmem_limit_bytes=63 * 1024 * 1024),
+            compiler_params=pltpu.CompilerParams(vmem_limit_bytes=48 * 1024 * 1024),
         )(
             place,
             batch_sizes,
@@ -465,11 +465,10 @@
                 other,
             )
 
-        def columns_kernel(place, factor, raw, columns):
-            columns[...] = exact_dot(factor[...], raw[...], 1, 0)
-
         def last_kernel(place, *refs):
-            tiles, (samples, basis, projection, whole) = refs[: 2 * ring], refs[2 * ring :]
+            tiles, rest = refs[: 2 * ring], refs[2 * ring :]
+            samples, upper, raw, basis, projection, snp_basis, whole = rest
+            snp_basis[...] = exact_dot(upper[...], raw[...], 1, 0)
             columns, gram = read_sum(place, tiles, whole)
             factor = inverse_factor(gram / sample_count, True)
             basis[...] = exact_dot(factor, samples[...], 1, 0)
@@ -507,20 +506,26 @@
                 *snp_others(wire),
                 matrix,
             )
-            columns = call_with_place(columns_kernel, columns_shape, factor, raw)
-            return samp_sum(mine, other, BF16), samples, columns
-
-        tiles, samples, columns = lax.fori_loop(
+            return samp_sum(mine, other, BF16), samples, factor, raw
+
+        tiles, samples, factor, raw = lax.fori_loop(
             0,
             ITERS,
             sweep,
-            (samp_sum(mine, other, F32), samples, jnp.zeros(columns_shape.shape, F32)),
-        )
-        basis, projection = call_with_place(
+            (
+                samp_sum(mine, other, F32),
+                samples,
+                jnp.zeros((width, width), F32),
+                jnp.zeros(columns_shape.shape, F32),
+            ),
+        )
+        basis, projection, columns = call_with_place(
             last_kernel,
-            (samples_shape, columns_shape),
+            (samples_shape, columns_shape, columns_shape),
             *tiles,
             samples,
+            factor,
+            raw,
             scratch=whole_scratch,
         )
         return (basis.T, projection.T, columns.T)

time: 168 us -> 169 us (level)
  Pallas kernels: 28.3 us -> 25.3 us
  local copies, waits for them, and re-layouts: 3.61 us -> 6 us
  blocking collectives: 33.8 us -> 35.6 us
    all_to_all x1, waiting for transfers between devices: 6.08 us -> 1.66 us  [on_device(): lax.all_to_all(call_with_place(pack_kernel, shape_of((chips, SUB, LANES))...]
    unnamed x16 -> x22, local copies, waits for them, and re-layouts: 3.61 us -> 6 us
    pallas_call x20 -> x18, Pallas kernels: 25.1 us -> 23 us  [call_with_place(): pl.pallas_call(body, out_shape=outs, in_specs=specs, scratch_shapes=scrat...]
    ppermute x16, waiting for transfers between devices: 5.06 us -> 6.98 us  [swap(): return lax.ppermute(value, 'core', [(0, 1), (1, 0)])]
    ppermute x9, waiting for transfers between devices: 10 us -> 11.8 us  [snp_others(): lax.ppermute(value, 'snp', [(i, (i + k) % snp) for i in range(snp)])]
    all_to_all x3, blocking collectives: 33.8 us -> 35.6 us  [samp_sum(): lax.all_to_all(spread, 'z', 0, 0)]
  transfers between devices with their start and end apart: 44 -> 44, of which waited for: 21 -> 23; matrix products, arithmetic and copies ran while one was open for 0% -> 0% of each run, Pallas kernels for 5% -> 3%
where the time goes in v5:
time: 169 us
  starting transfers between devices  71.9 us (43%)
  blocking collectives  35.6 us (21%)
  waiting for transfers between devices  29.3 us (17%)
  Pallas kernels  25.3 us (15%)
  local copies, waits for them, and re-layouts  6 us (4%)
    all_to_all x3, blocking collectives, samp_sum(): lax.all_to_all(spread, 'z', 0, 0)  35.6 us
    ppermute x16, starting transfers between devices, swap(): return lax.ppermute(value, 'core', [(0, 1), (1, 0)])  26.2 us
    pallas_call x18, Pallas kernels, call_with_place(): pl.pallas_call(body, out_shape=outs, in_specs=specs, scratch_shapes=scrat...  23 us
    ppermute x18, starting transfers between devices, x_shift(): return lax.ppermute(value, 'x', [(i, (i + k) % ring) for i in range(ring)])  21.6 us
    ppermute x9, starting transfers between devices, snp_others(): lax.ppermute(value, 'snp', [(i, (i + k) % snp) for i in range(snp)])  14.8 us
    ppermute x9, waiting for transfers between devices, snp_others(): lax.ppermute(value, 'snp', [(i, (i + k) % snp) for i in range(snp)])  11.8 us
    all_to_all x1, starting transfers between devices, on_device(): lax.all_to_all(call_with_place(pack_kernel, shape_of((chips, SUB, LANES))...  9.3 us
    ppermute x18, waiting for transfers between devices, x_shift(): return lax.ppermute(value, 'x', [(i, (i + k) % ring) for i in range(ring)])  8.85 us
  transfers between devices with their start and end apart: 44, of which 23 were waited for; matrix products, arithmetic and copies ran while one was open for 0% of the time, Pallas kernels for 3%

profile of v5, /device:TPU:1, one launch (start us, length us, event | category | flops | bytes accessed | tf_op | source)
XLA Modules:
  0.0 168.9 jit_solution(13746933750135039701)
XLA Ops:
  0.6 3.3 %collective-permute-start.14 = (f32[16,20]{1,0:T(8,128)}, f32[16,20]{1,0:T(8,128)S(1)}, u32[]{:S(2)}, u32[]{:S(2)}) collective-permute-start(f32[16,20]{1,0:T(8,128)} %mine.1), channel_id=1, source_target_pairs={{0,4},{4,0},{1,5},{5,1},{2,6},{6,2},{3,7},{7,3},{8,12},{12,8},{9,1... | collective-permute-start | bytes 3848 | tf_op jit(solution)/shard_map/ppermute | solution.py:124
  4.0 1.0 collective-permute-done.14.other
  5.0 0.7 copy-done.4
  5.7 0.7 shard_map.113
  6.4 9.3 %all-to-all-start.1 = ((f32[32,8,128]{2,1,0:T(8,128)}), f32[32,8,128]{2,1,0:T(8,128)S(1)}, u32[]{:S(2)}, u32[]{:S(2)}) async-start(f32[32,8,128]{2,1,0:T(8,128)} %shard_map.113), calls=%async_computation.1 | async-start | bytes 262144 | tf_op jit(solution)/shard_map/all_to_all | solution.py:280
  15.8 1.7 %copy-done = s32[640,1024]{1,0:T(8,128)S(1)} copy-done((s32[640,1024]{1,0:T(8,128)S(1)}, s32[640,1024]{1,0:T(8,128)}, u32[]{:S(2)}) %copy-start) | copy-done | bytes 2621464
  17.5 0.9 copy-done.1
  21.1 2.4 %shard_map.112 = (bf16[640,1024]{1,0:T(8,128)(2,1)S(1)}, f32[64,640]{1,0:T(8,128)S(1)}, s32[16]{0:T(128)S(1)}) custom-call(s32[1]{0:T(128)} %bitcast.place, s32[12]{0:T(128)S(1)} %copy-done.5, s32[48]{0:T(128)S(1)} %copy-done.9, s32[48]{0:T(128)S(1)} %copy-done.10, s32[640,1024]{1,0:T(8,128)S(1)} %copy-done, f32[1,1024]{1,0:T(1,128)S(1)} %bitcast.11, ...), custom_call_target="tpu_custom_call" | custom-call | tf_op jit(solution)/shard_map/pallas_call | solution.py:239
  23.4 1.7 all-to-all-done.1.tiles
  25.6 3.0 %collective-permute-start.15 = (f32[64,768]{1,0:T(8,128)S(1)}, f32[64,768]{1,0:T(8,128)S(1)}, u32[]{:S(2)}, u32[]{:S(2)}) collective-permute-start(f32[64,768]{1,0:T(8,128)S(1)} %shard_map.114.w0), channel_id=1, source_target_pairs={{0,2},{1,3},{2,0},{3,1},{4,6},{5,7},{6,4},{7,5},{8,10},{9,11},{10,... | collective-permute-start | bytes 589832 | tf_op jit(solution)/shard_map/ppermute | solution.py:128
  29.0 2.3 %collective-permute-start.17 = (f32[64,768]{1,0:T(8,128)S(1)}, f32[64,768]{1,0:T(8,128)S(1)}, u32[]{:S(2)}, u32[]{:S(2)}) collective-permute-start(f32[64,768]{1,0:T(8,128)S(1)} %shard_map.114.w0), channel_id=1, source_target_pairs={{0,3},{1,0},{2,1},{3,2},{4,7},{5,4},{6,5},{7,6},{8,11},{9,8},{10,9... | collective-permute-start | bytes 589832 | tf_op jit(solution)/shard_map/ppermute | solution.py:128
  31.3 2.9 %shard_map.115.x = bf16[640,1024]{1,0:T(8,128)(2,1)S(1)} custom-call(s32[1]{0:T(128)} %bitcast.place, s32[12]{0:T(128)S(1)} %copy-done.6, s32[16]{0:T(128)S(1)} %get-tuple-element.107.bits, f32[20]{0:T(128)S(1)} %copy-done.8, bf16[640,1024]{1,0:T(8,128)(2,1)S(1)} %get-tuple-element.109.obs, f32[20,640]{1,0:T(8,128)S(1)} %bitcast.9, ...), custom_call_target="tpu_custom_call" | custom-call | tf_op jit(solution)/shard_map/pallas_call | solution.py:166
  34.2 3.2 %collective-permute-done.16.w2 = f32[64,768]{1,0:T(8,128)S(1)} collective-permute-done((f32[64,768]{1,0:T(8,128)S(1)}, f32[64,768]{1,0:T(8,128)S(1)}, u32[]{:S(2)}, u32[]{:S(2)}) %collective-permute-start.16) | collective-permute-done | bytes 196640 | tf_op jit(solution)/shard_map/ppermute | solution.py:128
  37.4 2.2 %shard_map.116 = (f32[64,640]{1,0:T(8,128)}, f32[32,1152]{1,0:T(8,128)S(1)}, f32[32,1152]{1,0:T(8,128)S(1)}) custom-call(s32[1]{0:T(128)} %bitcast.place, s32[12]{0:T(128)S(1)} %copy-done.6, s32[16]{0:T(128)S(1)} %get-tuple-element.107.bits, f32[20]{0:T(128)S(1)} %copy-done.8, f32[64,768]{1,0:T(8,128)S(1)} %shard_map.114.w0, ...), custom_call_target="tpu_custom_call" | custom-call | tf_op jit(solution)/shard_map/pallas_call | solution.py:166
  39.6 1.9 %collective-permute-start.18 = (f32[32,1152]{1,0:T(8,128)S(1)}, f32[32,1152]{1,0:T(8,128)S(1)}, u32[]{:S(2)}, u32[]{:S(2)}) collective-permute-start(f32[32,1152]{1,0:T(8,128)S(1)} %get-tuple-element.111), channel_id=1, source_target_pairs={{0,4},{4,0},{1,5},{5,1},{2,6},{6,2},{3,7},{7,3},{8,12},{12,8},{9,1... | collective-permute-start | bytes 442376 | tf_op jit(solution)/shard_map/ppermute | solution.py:124
  41.5 1.0 collective-permute-done.18.got
  42.6 2.7 %collective-permute-start.20 = (f32[8,1152]{1,0:T(8,128)S(1)}, f32[8,1152]{1,0:T(8,128)S(1)}, u32[]{:S(2)}, u32[]{:S(2)}) collective-permute-start(f32[8,1152]{1,0:T(8,128)S(1)} %get-tuple-element.114), channel_id=1, source_target_pairs={{0,24},{8,0},{16,8},{24,16},{1,25},{9,1},{17,9},{25,17},{2,26},{10... | collective-permute-start | bytes 110600 | tf_op jit(solution)/shard_map/ppermute | solution.py:133
  45.3 1.3 collective-permute-done.19.a
  46.6 3.0 %collective-permute-done.21.c = f32[8,1152]{1,0:T(8,128)S(1)} collective-permute-done((f32[8,1152]{1,0:T(8,128)S(1)}, f32[8,1152]{1,0:T(8,128)S(1)}, u32[]{:S(2)}, u32[]{:S(2)}) %collective-permute-start.21) | collective-permute-done | bytes 36896 | tf_op jit(solution)/shard_map/ppermute | solution.py:133
  49.6 14.2 %all_to_all.16.parts = f32[8,8,1152]{2,1,0:T(8,128)S(1)} all-to-all(f32[8,8,1152]{2,1,0:T(8,128)S(1)} %shard_map.118), channel_id=1, replica_groups=mesh['z'=8,'x'=4,'core'=2,'snp'=4] {'z'}, dimensions={0} | all-to-all | bytes 589824 | tf_op jit(solution)/shard_map/all_to_all | solution.py:396
  63.8 1.6 collective-permute-start.22
  65.7 2.4 %collective-permute-start.24 = (f32[8,1152]{1,0:T(8,128)S(1)}, f32[8,1152]{1,0:T(8,128)S(1)}, u32[]{:S(2)}, u32[]{:S(2)}) collective-permute-start(f32[8,1152]{1,0:T(8,128)S(1)} %shard_map.119), channel_id=1, source_target_pairs={{0,24},{8,0},{16,8},{24,16},{1,25},{9,1},{17,9},{25,17},{2,26},{10... | collective-permute-start | bytes 110600 | tf_op jit(solution)/shard_map/ppermute | solution.py:133
  68.1 4.6 %collective-permute-start.25 = (f32[8,1152]{1,0:T(8,128)S(1)}, f32[8,1152]{1,0:T(8,128)S(1)}, u32[]{:S(2)}, u32[]{:S(2)}) collective-permute-start(f32[8,1152]{1,0:T(8,128)S(1)} %shard_map.119), channel_id=1, source_target_pairs={{0,4},{4,0},{1,5},{5,1},{2,6},{6,2},{3,7},{7,3},{8,12},{12,8},{9,1... | collective-permute-start | bytes 110600 | tf_op jit(solution)/shard_map/ppermute | solution.py:124
  73.1 1.5 collective-permute-start.27
  74.6 0.8 collective-permute-done.27
  75.8 89.0 %while.30 = (s32[]{:T(128)}, f32[8,1152]{1,0:T(8,128)S(1)}, f32[8,1152]{1,0:T(8,128)S(1)}, f32[8,1152]{1,0:T(8,128)S(1)}, f32[8,1152]{1,0:T(8,128)S(1)}, /*index...) while((s32[]{:T(128)}, f32[8,1152]{1,0:T(8,128)S(1)}, ...), condition=%wide.region_1.0_spmd, body=%wide.region_0.0_spmd.sunk | while | flops 2 | bytes 3670717 | solution.py:511
  75.8 2.9 %eval_jaxpr.5 = (f32[64,1024]{1,0:T(8,128)}, f32[64,640]{1,0:T(8,128)S(1)}, f32[64,64]{1,0:T(8,128)S(1)}, bf16[64,832]{1,0:T(8,128)(2,1)S(1)}) custom-call(s32[1]{0:T(128)} %get-tuple-element.304.place, f32[8,1152]{1,0:T(8,128)S(1)} %get-tuple-element.278.refs_0_, f32[8,1152]{1,0:T(8,128)S(1)} %get-tuple-element.279.refs_1_, ...), custom_call_target="tpu_custom_call" | custom-call | tf_op jit(solution)/shard_map/while/body/eval_jaxpr/pallas_call | solution.py:166
  78.7 1.9 %collective-permute-start = (bf16[64,832]{1,0:T(8,128)(2,1)S(1)}, bf16[64,832]{1,0:T(8,128)(2,1)S(1)}, u32[]{:S(2)}, u32[]{:S(2)}) collective-permute-start(bf16[64,832]{1,0:T(8,128)(2,1)S(1)} %get-tuple-element.252), channel_id=1, source_target_pairs={{0,2},{1,3},{2,0},{3,1},{4,6},{5,7},{6,4},{7,5},{8,10},{9,11},{10,... | collective-permute-start | bytes 319496 | tf_op jit(solution)/shard_map/while/body/eval_jaxpr/ppermute | solution.py:128
  80.5 1.2 collective-permute-start.1
  81.7 1.5 collective-permute-start.2
  83.2 1.6 collective-permute-done.a
  84.8 2.8 %collective-permute-done.1.b = bf16[64,832]{1,0:T(8,128)(2,1)S(1)} collective-permute-done((bf16[64,832]{1,0:T(8,128)(2,1)S(1)}, bf16[64,832]{1,0:T(8,128)(2,1)S(1)}, u32[]{:S(2)}, u32[]{:S(2)}) %collective-permute-start.1) | collective-permute-done | bytes 106528 | tf_op jit(solution)/shard_map/while/body/eval_jaxpr/ppermute | solution.py:128
  87.6 3.1 %eval_jaxpr.6 = (f32[64,640]{1,0:T(8,128)}, f32[64,64]{1,0:T(8,128)}, f32[32,1152]{1,0:T(8,128)S(1)}, f32[32,1152]{1,0:T(8,128)S(1)}) custom-call(s32[1]{0:T(128)} %get-tuple-element.304.place, f32[64,640]{1,0:T(8,128)S(1)} %get-tuple-element.250.product, f32[64,64]{1,0:T(8,128)S(1)} %get-tuple-element.251.gram, bf16[64,832]{1,0:T(8,128)(2,1)S(1)} %collective-permute-done.a, ...), custom_call_target="tpu_custom_call" | custom-call | tf_op jit(solution)/shard_map/while/body/eval_jaxpr/pallas_call | solution.py:166
  91.3 1.0 collective-permute-done.3.got
  92.4 1.2 collective-permute-start.4
  93.6 2.1 %collective-permute-start.5 = (f32[8,1152]{1,0:T(8,128)S(1)}, f32[8,1152]{1,0:T(8,128)S(1)}, u32[]{:S(2)}, u32[]{:S(2)}) collective-permute-start(f32[8,1152]{1,0:T(8,128)S(1)} %get-tuple-element.257), channel_id=1, source_target_pairs={{0,8},{8,16},{16,24},{24,0},{1,9},{9,17},{17,25},{25,1},{2,10},{10... | collective-permute-start | bytes 110600 | tf_op jit(solution)/shard_map/while/body/eval_jaxpr/ppermute | solution.py:133
  96.8 1.4 collective-permute-done.5.b
  98.8 10.7 %all_to_all.17.parts = bf16[8,8,1280]{2,1,0:T(8,128)(2,1)S(1)} all-to-all(bf16[8,8,1280]{2,1,0:T(8,128)(2,1)S(1)} %eval_jaxpr.8), channel_id=1, replica_groups=mesh['z'=8,'x'=4,'core'=2,'snp'=4] {'z'}, dimensions={0} | all-to-all | bytes 327680 | tf_op jit(solution)/shard_map/while/body/eval_jaxpr/all_to_all | solution.py:396
  110.1 2.1 %collective-permute-start.8 = (f32[8,1152]{1,0:T(8,128)S(1)}, f32[8,1152]{1,0:T(8,128)S(1)}, u32[]{:S(2)}, u32[]{:S(2)}) collective-permute-start(f32[8,1152]{1,0:T(8,128)S(1)} %eval_jaxpr.9), channel_id=1, source_target_pairs={{0,8},{8,16},{16,24},{24,0},{1,9},{9,17},{17,25},{25,1},{2,10},{10... | collective-permute-start | bytes 110600 | tf_op jit(solution)/shard_map/while/body/eval_jaxpr/ppermute | solution.py:133
  112.8 3.7 %collective-permute-start.10 = (f32[8,1152]{1,0:T(8,128)S(1)}, f32[8,1152]{1,0:T(8,128)S(1)}, u32[]{:S(2)}, u32[]{:S(2)}) collective-permute-start(f32[8,1152]{1,0:T(8,128)S(1)} %eval_jaxpr.9), channel_id=1, source_target_pairs={{0,4},{4,0},{1,5},{5,1},{2,6},{6,2},{3,7},{7,3},{8,12},{12,8},{9,1... | collective-permute-start | bytes 110600 | tf_op jit(solution)/shard_map/while/body/eval_jaxpr/ppermute | solution.py:124
  116.5 1.5 collective-permute-start.11
  118.4 1.0 collective-permute-start.13
  119.5 0.9 collective-permute-done.13
  120.3 2.9 %eval_jaxpr.5 = (f32[64,1024]{1,0:T(8,128)}, f32[64,640]{1,0:T(8,128)S(1)}, f32[64,64]{1,0:T(8,128)S(1)}, bf16[64,832]{1,0:T(8,128)(2,1)S(1)}) custom-call(s32[1]{0:T(128)} %get-tuple-element.304.place, f32[8,1152]{1,0:T(8,128)S(1)} %get-tuple-element.278.refs_0_, f32[8,1152]{1,0:T(8,128)S(1)} %get-tuple-element.279.refs_1_, ...), custom_call_target="tpu_custom_call" | custom-call | tf_op jit(solution)/shard_map/while/body/eval_jaxpr/pallas_call | solution.py:166
  123.2 1.9 %collective-permute-start = (bf16[64,832]{1,0:T(8,128)(2,1)S(1)}, bf16[64,832]{1,0:T(8,128)(2,1)S(1)}, u32[]{:S(2)}, u32[]{:S(2)}) collective-permute-start(bf16[64,832]{1,0:T(8,128)(2,1)S(1)} %get-tuple-element.252), channel_id=1, source_target_pairs={{0,2},{1,3},{2,0},{3,1},{4,6},{5,7},{6,4},{7,5},{8,10},{9,11},{10,... | collective-permute-start | bytes 319496 | tf_op jit(solution)/shard_map/while/body/eval_jaxpr/ppermute | solution.py:128
  125.1 1.2 collective-permute-start.1
  126.3 1.4 collective-permute-start.2
  127.8 1.4 collective-permute-done.a
  129.2 2.8 %collective-permute-done.1.b = bf16[64,832]{1,0:T(8,128)(2,1)S(1)} collective-permute-done((bf16[64,832]{1,0:T(8,128)(2,1)S(1)}, bf16[64,832]{1,0:T(8,128)(2,1)S(1)}, u32[]{:S(2)}, u32[]{:S(2)}) %collective-permute-start.1) | collective-permute-done | bytes 106528 | tf_op jit(solution)/shard_map/while/body/eval_jaxpr/ppermute | solution.py:128
  132.0 3.1 %eval_jaxpr.6 = (f32[64,640]{1,0:T(8,128)}, f32[64,64]{1,0:T(8,128)}, f32[32,1152]{1,0:T(8,128)S(1)}, f32[32,1152]{1,0:T(8,128)S(1)}) custom-call(s32[1]{0:T(128)} %get-tuple-element.304.place, f32[64,640]{1,0:T(8,128)S(1)} %get-tuple-element.250.product, f32[64,64]{1,0:T(8,128)S(1)} %get-tuple-element.251.gram, bf16[64,832]{1,0:T(8,128)(2,1)S(1)} %collective-permute-done.a, ...), custom_call_target="tpu_custom_call" | custom-call | tf_op jit(solution)/shard_map/while/body/eval_jaxpr/pallas_call | solution.py:166
  135.1 0.9 collective-permute-start.3
  135.9 1.0 collective-permute-done.3.got
  137.0 1.0 collective-permute-start.4
  138.0 1.6 collective-permute-start.5
  139.6 1.1 collective-permute-start.6
  140.6 0.7 collective-permute-done.4.a
  141.4 1.1 collective-permute-done.5.b
  142.7 10.7 %all_to_all.17.parts = bf16[8,8,1280]{2,1,0:T(8,128)(2,1)S(1)} all-to-all(bf16[8,8,1280]{2,1,0:T(8,128)(2,1)S(1)} %eval_jaxpr.8), channel_id=1, replica_groups=mesh['z'=8,'x'=4,'core'=2,'snp'=4] {'z'}, dimensions={0} | all-to-all | bytes 327680 | tf_op jit(solution)/shard_map/while/body/eval_jaxpr/all_to_all | solution.py:396
  153.6 1.3 collective-permute-start.7
  154.9 1.3 collective-permute-start.8
  156.2 1.4 collective-permute-start.9
  157.6 3.7 %collective-permute-start.10 = (f32[8,1152]{1,0:T(8,128)S(1)}, f32[8,1152]{1,0:T(8,128)S(1)}, u32[]{:S(2)}, u32[]{:S(2)}) collective-permute-start(f32[8,1152]{1,0:T(8,128)S(1)} %eval_jaxpr.9), channel_id=1, source_target_pairs={{0,4},{4,0},{1,5},{5,1},{2,6},{6,2},{3,7},{7,3},{8,12},{12,8},{9,1... | collective-permute-start | bytes 110600 | tf_op jit(solution)/shard_map/while/body/eval_jaxpr/ppermute | solution.py:124
  161.9 1.3 collective-permute-start.12
  164.7 4.2 %shard_map.120 = (f32[64,640]{1,0:T(8,128)}, f32[64,1024]{1,0:T(8,128)}, f32[64,1024]{1,0:T(8,128)}) custom-call(s32[1]{0:T(128)} %bitcast.place, f32[8,1152]{1,0:T(8,128)S(1)} %get-tuple-element.117.refs_0_, f32[8,1152]{1,0:T(8,128)S(1)} %get-tuple-element.118.refs_1_, f32[8,1152]{1,0:T(8,128)S(1)} %get-tuple-element.119.refs_2_, ...), custom_call_target="tpu_custom_call" | custom-call | tf_op jit(solution)/shard_map/pallas_call | solution.py:166
  (71 shorter events, 11.3 us)
Async XLA Ops:
  0.6 4.4 %collective-permute-start.14 = (f32[16,20]{1,0:T(8,128)}, f32[16,20]{1,0:T(8,128)S(1)}, u32[]{:S(2)}, u32[]{:S(2)}) collective-permute-start(f32[16,20]{1,0:T(8,128)} %mine.1), channel_id=1, source_target_pairs={{0,4},{4,0},{1,5},{5,1},{2,6},{6,2},{3,7},{7,3},{8,12},{12,8},{9,1... | collective-permute-start | bytes 3848 | tf_op jit(solution)/shard_map/ppermute | solution.py:124
  5.0 0.7 copy-start.4
  6.4 18.7 %all-to-all-start.1 = ((f32[32,8,128]{2,1,0:T(8,128)}), f32[32,8,128]{2,1,0:T(8,128)S(1)}, u32[]{:S(2)}, u32[]{:S(2)}) async-start(f32[32,8,128]{2,1,0:T(8,128)} %shard_map.113), calls=%async_computation.1 | async-start | bytes 262144 | tf_op jit(solution)/shard_map/all_to_all | solution.py:280
  15.7 1.7 %copy-start = (s32[640,1024]{1,0:T(8,128)S(1)}, s32[640,1024]{1,0:T(8,128)}, u32[]{:S(2)}) copy-start(s32[640,1024]{1,0:T(8,128)} %geno_in.1) | copy-start | bytes 7864324
  17.5 0.9 copy-start.1
  18.4 0.7 copy-start.5
  19.0 0.7 copy-start.7
  19.7 0.7 copy-start.9
  20.4 0.7 copy-start.10
  21.0 4.0 %copy-start.2 = (bf16[1024,64]{0,1:T(8,128)(2,1)S(1)}, bf16[1024,64]{0,1:T(8,128)(2,1)}, u32[]{:S(2)}) copy-start(bf16[1024,64]{0,1:T(8,128)(2,1)} %param.16) | copy-start | bytes 393220
  21.0 10.3 %copy-start.3 = (f32[640,20]{0,1:T(8,128)S(1)}, f32[640,20]{0,1:T(8,128)}, u32[]{:S(2)}) copy-start(f32[640,20]{0,1:T(8,128)} %param.13) | copy-start | bytes 153604
  21.0 10.3 %copy-start.6 = (s32[12]{0:T(128)S(1)}, s32[12]{0:T(128)}, u32[]{:S(2)}) copy-start(s32[12]{0:T(128)} %sizes.3) | copy-start | bytes 148
  21.0 10.3 %copy-start.8 = (f32[20]{0:T(128)S(1)}, f32[20]{0:T(128)}, u32[]{:S(2)}) copy-start(f32[20]{0:T(128)} %scale.3) | copy-start | bytes 244
  25.6 8.6 %collective-permute-start.15 = (f32[64,768]{1,0:T(8,128)S(1)}, f32[64,768]{1,0:T(8,128)S(1)}, u32[]{:S(2)}, u32[]{:S(2)}) collective-permute-start(f32[64,768]{1,0:T(8,128)S(1)} %shard_map.114.w0), channel_id=1, source_target_pairs={{0,2},{1,3},{2,0},{3,1},{4,6},{5,7},{6,4},{7,5},{8,10},{9,11},{10,... | collective-permute-start | bytes 589832 | tf_op jit(solution)/shard_map/ppermute | solution.py:128
  28.6 8.8 %collective-permute-start.16 = (f32[64,768]{1,0:T(8,128)S(1)}, f32[64,768]{1,0:T(8,128)S(1)}, u32[]{:S(2)}, u32[]{:S(2)}) collective-permute-start(f32[64,768]{1,0:T(8,128)S(1)} %shard_map.114.w0), channel_id=1, source_target_pairs={{0,1},{1,2},{2,3},{3,0},{4,5},{5,6},{6,7},{7,4},{8,9},{9,10},{10,1... | collective-permute-start | bytes 589832 | tf_op jit(solution)/shard_map/ppermute | solution.py:128
  29.0 8.4 %collective-permute-start.17 = (f32[64,768]{1,0:T(8,128)S(1)}, f32[64,768]{1,0:T(8,128)S(1)}, u32[]{:S(2)}, u32[]{:S(2)}) collective-permute-start(f32[64,768]{1,0:T(8,128)S(1)} %shard_map.114.w0), channel_id=1, source_target_pairs={{0,3},{1,0},{2,1},{3,2},{4,7},{5,4},{6,5},{7,6},{8,11},{9,8},{10,9... | collective-permute-start | bytes 589832 | tf_op jit(solution)/shard_map/ppermute | solution.py:128
  39.6 2.9 %collective-permute-start.18 = (f32[32,1152]{1,0:T(8,128)S(1)}, f32[32,1152]{1,0:T(8,128)S(1)}, u32[]{:S(2)}, u32[]{:S(2)}) collective-permute-start(f32[32,1152]{1,0:T(8,128)S(1)} %get-tuple-element.111), channel_id=1, source_target_pairs={{0,4},{4,0},{1,5},{5,1},{2,6},{6,2},{3,7},{7,3},{8,12},{12,8},{9,1... | collective-permute-start | bytes 442376 | tf_op jit(solution)/shard_map/ppermute | solution.py:124
  42.5 4.1 %collective-permute-start.19 = (f32[8,1152]{1,0:T(8,128)S(1)}, f32[8,1152]{1,0:T(8,128)S(1)}, u32[]{:S(2)}, u32[]{:S(2)}) collective-permute-start(f32[8,1152]{1,0:T(8,128)S(1)} %get-tuple-element.113), channel_id=1, source_target_pairs={{0,8},{8,16},{16,24},{24,0},{1,9},{9,17},{17,25},{25,1},{2,10},{10... | collective-permute-start | bytes 110600 | tf_op jit(solution)/shard_map/ppermute | solution.py:133
  42.6 4.0 %collective-permute-start.20 = (f32[8,1152]{1,0:T(8,128)S(1)}, f32[8,1152]{1,0:T(8,128)S(1)}, u32[]{:S(2)}, u32[]{:S(2)}) collective-permute-start(f32[8,1152]{1,0:T(8,128)S(1)} %get-tuple-element.114), channel_id=1, source_target_pairs={{0,24},{8,0},{16,8},{24,16},{1,25},{9,1},{17,9},{25,17},{2,26},{10... | collective-permute-start | bytes 110600 | tf_op jit(solution)/shard_map/ppermute | solution.py:133
  45.3 4.3 %collective-permute-start.21 = (f32[8,1152]{1,0:T(8,128)S(1)}, f32[8,1152]{1,0:T(8,128)S(1)}, u32[]{:S(2)}, u32[]{:S(2)}) collective-permute-start(f32[8,1152]{1,0:T(8,128)S(1)} %get-tuple-element.115), channel_id=1, source_target_pairs={{0,16},{8,24},{16,0},{24,8},{1,17},{9,25},{17,1},{25,9},{2,18},{10... | collective-permute-start | bytes 110600 | tf_op jit(solution)/shard_map/ppermute | solution.py:133
  63.8 8.8 %collective-permute-start.22 = (f32[8,1152]{1,0:T(8,128)S(1)}, f32[8,1152]{1,0:T(8,128)S(1)}, u32[]{:S(2)}, u32[]{:S(2)}) collective-permute-start(f32[8,1152]{1,0:T(8,128)S(1)} %shard_map.119), channel_id=1, source_target_pairs={{0,16},{8,24},{16,0},{24,8},{1,17},{9,25},{17,1},{25,9},{2,18},{10... | collective-permute-start | bytes 110600 | tf_op jit(solution)/shard_map/ppermute | solution.py:133
  65.4 7.7 %collective-permute-start.23 = (f32[8,1152]{1,0:T(8,128)S(1)}, f32[8,1152]{1,0:T(8,128)S(1)}, u32[]{:S(2)}, u32[]{:S(2)}) collective-permute-start(f32[8,1152]{1,0:T(8,128)S(1)} %shard_map.119), channel_id=1, source_target_pairs={{0,8},{8,16},{16,24},{24,0},{1,9},{9,17},{17,25},{25,1},{2,10},{10... | collective-permute-start | bytes 110600 | tf_op jit(solution)/shard_map/ppermute | solution.py:133
  65.7 8.9 %collective-permute-start.24 = (f32[8,1152]{1,0:T(8,128)S(1)}, f32[8,1152]{1,0:T(8,128)S(1)}, u32[]{:S(2)}, u32[]{:S(2)}) collective-permute-start(f32[8,1152]{1,0:T(8,128)S(1)} %shard_map.119), channel_id=1, source_target_pairs={{0,24},{8,0},{16,8},{24,16},{1,25},{9,1},{17,9},{25,17},{2,26},{10... | collective-permute-start | bytes 110600 | tf_op jit(solution)/shard_map/ppermute | solution.py:133
  68.1 6.5 %collective-permute-start.25 = (f32[8,1152]{1,0:T(8,128)S(1)}, f32[8,1152]{1,0:T(8,128)S(1)}, u32[]{:S(2)}, u32[]{:S(2)}) collective-permute-start(f32[8,1152]{1,0:T(8,128)S(1)} %shard_map.119), channel_id=1, source_target_pairs={{0,4},{4,0},{1,5},{5,1},{2,6},{6,2},{3,7},{7,3},{8,12},{12,8},{9,1... | collective-permute-start | bytes 110600 | tf_op jit(solution)/shard_map/ppermute | solution.py:124
  72.6 2.0 %collective-permute-start.26 = (f32[8,1152]{1,0:T(8,128)S(1)}, f32[8,1152]{1,0:T(8,128)S(1)}, u32[]{:S(2)}, u32[]{:S(2)}) collective-permute-start(f32[8,1152]{1,0:T(8,128)S(1)} %collective-permute-done.22), channel_id=1, source_target_pairs={{0,4},{4,0},{1,5},{5,1},{2,6},{6,2},{3,7},{7,3},{8,12},{12,8},{9,1... | collective-permute-start | bytes 110600 | tf_op jit(solution)/shard_map/ppermute | solution.py:124
  73.1 2.3 %collective-permute-start.27 = (f32[8,1152]{1,0:T(8,128)S(1)}, f32[8,1152]{1,0:T(8,128)S(1)}, u32[]{:S(2)}, u32[]{:S(2)}) collective-permute-start(f32[8,1152]{1,0:T(8,128)S(1)} %collective-permute-done.23), channel_id=1, source_target_pairs={{0,4},{4,0},{1,5},{5,1},{2,6},{6,2},{3,7},{7,3},{8,12},{12,8},{9,1... | collective-permute-start | bytes 110600 | tf_op jit(solution)/shard_map/ppermute | solution.py:124
  74.6 1.2 collective-permute-start.28
  78.7 6.2 %collective-permute-start = (bf16[64,832]{1,0:T(8,128)(2,1)S(1)}, bf16[64,832]{1,0:T(8,128)(2,1)S(1)}, u32[]{:S(2)}, u32[]{:S(2)}) collective-permute-start(bf16[64,832]{1,0:T(8,128)(2,1)S(1)} %get-tuple-element.252), channel_id=1, source_target_pairs={{0,2},{1,3},{2,0},{3,1},{4,6},{5,7},{6,4},{7,5},{8,10},{9,11},{10,... | collective-permute-start | bytes 319496 | tf_op jit(solution)/shard_map/while/body/eval_jaxpr/ppermute | solution.py:128
  80.5 7.1 %collective-permute-start.1 = (bf16[64,832]{1,0:T(8,128)(2,1)S(1)}, bf16[64,832]{1,0:T(8,128)(2,1)S(1)}, u32[]{:S(2)}, u32[]{:S(2)}) collective-permute-start(bf16[64,832]{1,0:T(8,128)(2,1)S(1)} %get-tuple-element.252), channel_id=1, source_target_pairs={{0,1},{1,2},{2,3},{3,0},{4,5},{5,6},{6,7},{7,4},{8,9},{9,10},{10,1... | collective-permute-start | bytes 319496 | tf_op jit(solution)/shard_map/while/body/eval_jaxpr/ppermute | solution.py:128
  81.7 5.9 %collective-permute-start.2 = (bf16[64,832]{1,0:T(8,128)(2,1)S(1)}, bf16[64,832]{1,0:T(8,128)(2,1)S(1)}, u32[]{:S(2)}, u32[]{:S(2)}) collective-permute-start(bf16[64,832]{1,0:T(8,128)(2,1)S(1)} %get-tuple-element.252), channel_id=1, source_target_pairs={{0,3},{1,0},{2,1},{3,2},{4,7},{5,4},{6,5},{7,6},{8,11},{9,8},{10,9... | collective-permute-start | bytes 319496 | tf_op jit(solution)/shard_map/while/body/eval_jaxpr/ppermute | solution.py:128
  90.7 1.7 collective-permute-start.3
  92.4 4.4 %collective-permute-start.4 = (f32[8,1152]{1,0:T(8,128)S(1)}, f32[8,1152]{1,0:T(8,128)S(1)}, u32[]{:S(2)}, u32[]{:S(2)}) collective-permute-start(f32[8,1152]{1,0:T(8,128)S(1)} %get-tuple-element.256), channel_id=1, source_target_pairs={{0,16},{8,24},{16,0},{24,8},{1,17},{9,25},{17,1},{25,9},{2,18},{10... | collective-permute-start | bytes 110600 | tf_op jit(solution)/shard_map/while/body/eval_jaxpr/ppermute | solution.py:133
  93.6 4.6 %collective-permute-start.5 = (f32[8,1152]{1,0:T(8,128)S(1)}, f32[8,1152]{1,0:T(8,128)S(1)}, u32[]{:S(2)}, u32[]{:S(2)}) collective-permute-start(f32[8,1152]{1,0:T(8,128)S(1)} %get-tuple-element.257), channel_id=1, source_target_pairs={{0,8},{8,16},{16,24},{24,0},{1,9},{9,17},{17,25},{25,1},{2,10},{10... | collective-permute-start | bytes 110600 | tf_op jit(solution)/shard_map/while/body/eval_jaxpr/ppermute | solution.py:133
  95.6 3.1 %collective-permute-start.6 = (f32[8,1152]{1,0:T(8,128)S(1)}, f32[8,1152]{1,0:T(8,128)S(1)}, u32[]{:S(2)}, u32[]{:S(2)}) collective-permute-start(f32[8,1152]{1,0:T(8,128)S(1)} %get-tuple-element.258), channel_id=1, source_target_pairs={{0,24},{8,0},{16,8},{24,16},{1,25},{9,1},{17,9},{25,17},{2,26},{10... | collective-permute-start | bytes 110600 | tf_op jit(solution)/shard_map/while/body/eval_jaxpr/ppermute | solution.py:133
  109.7 6.8 %collective-permute-start.7 = (f32[8,1152]{1,0:T(8,128)S(1)}, f32[8,1152]{1,0:T(8,128)S(1)}, u32[]{:S(2)}, u32[]{:S(2)}) collective-permute-start(f32[8,1152]{1,0:T(8,128)S(1)} %eval_jaxpr.9), channel_id=1, source_target_pairs={{0,16},{8,24},{16,0},{24,8},{1,17},{9,25},{17,1},{25,9},{2,18},{10... | collective-permute-start | bytes 110600 | tf_op jit(solution)/shard_map/while/body/eval_jaxpr/ppermute | solution.py:133
  110.1 8.0 %collective-permute-start.8 = (f32[8,1152]{1,0:T(8,128)S(1)}, f32[8,1152]{1,0:T(8,128)S(1)}, u32[]{:S(2)}, u32[]{:S(2)}) collective-permute-start(f32[8,1152]{1,0:T(8,128)S(1)} %eval_jaxpr.9), channel_id=1, source_target_pairs={{0,8},{8,16},{16,24},{24,0},{1,9},{9,17},{17,25},{25,1},{2,10},{10... | collective-permute-start | bytes 110600 | tf_op jit(solution)/shard_map/while/body/eval_jaxpr/ppermute | solution.py:133
  112.2 6.3 %collective-permute-start.9 = (f32[8,1152]{1,0:T(8,128)S(1)}, f32[8,1152]{1,0:T(8,128)S(1)}, u32[]{:S(2)}, u32[]{:S(2)}) collective-permute-start(f32[8,1152]{1,0:T(8,128)S(1)} %eval_jaxpr.9), channel_id=1, source_target_pairs={{0,24},{8,0},{16,8},{24,16},{1,25},{9,1},{17,9},{25,17},{2,26},{10... | collective-permute-start | bytes 110600 | tf_op jit(solution)/shard_map/while/body/eval_jaxpr/ppermute | solution.py:133
  112.8 6.7 %collective-permute-start.10 = (f32[8,1152]{1,0:T(8,128)S(1)}, f32[8,1152]{1,0:T(8,128)S(1)}, u32[]{:S(2)}, u32[]{:S(2)}) collective-permute-start(f32[8,1152]{1,0:T(8,128)S(1)} %eval_jaxpr.9), channel_id=1, source_target_pairs={{0,4},{4,0},{1,5},{5,1},{2,6},{6,2},{3,7},{7,3},{8,12},{12,8},{9,1... | collective-permute-start | bytes 110600 | tf_op jit(solution)/shard_map/while/body/eval_jaxpr/ppermute | solution.py:124
  116.5 3.0 %collective-permute-start.11 = (f32[8,1152]{1,0:T(8,128)S(1)}, f32[8,1152]{1,0:T(8,128)S(1)}, u32[]{:S(2)}, u32[]{:S(2)}) collective-permute-start(f32[8,1152]{1,0:T(8,128)S(1)} %collective-permute-done.7), channel_id=1, source_target_pairs={{0,4},{4,0},{1,5},{5,1},{2,6},{6,2},{3,7},{7,3},{8,12},{12,8},{9,1... | collective-permute-start | bytes 110600 | tf_op jit(solution)/shard_map/while/body/eval_jaxpr/ppermute | solution.py:124
  118.0 1.5 collective-permute-start.12
  118.4 1.9 %collective-permute-start.13 = (f32[8,1152]{1,0:T(8,128)S(1)}, f32[8,1152]{1,0:T(8,128)S(1)}, u32[]{:S(2)}, u32[]{:S(2)}) collective-permute-start(f32[8,1152]{1,0:T(8,128)S(1)} %collective-permute-done.9), channel_id=1, source_target_pairs={{0,4},{4,0},{1,5},{5,1},{2,6},{6,2},{3,7},{7,3},{8,12},{12,8},{9,1... | collective-permute-start | bytes 110600 | tf_op jit(solution)/shard_map/while/body/eval_jaxpr/ppermute | solution.py:124
  123.2 6.0 %collective-permute-start = (bf16[64,832]{1,0:T(8,128)(2,1)S(1)}, bf16[64,832]{1,0:T(8,128)(2,1)S(1)}, u32[]{:S(2)}, u32[]{:S(2)}) collective-permute-start(bf16[64,832]{1,0:T(8,128)(2,1)S(1)} %get-tuple-element.252), channel_id=1, source_target_pairs={{0,2},{1,3},{2,0},{3,1},{4,6},{5,7},{6,4},{7,5},{8,10},{9,11},{10,... | collective-permute-start | bytes 319496 | tf_op jit(solution)/shard_map/while/body/eval_jaxpr/ppermute | solution.py:128
  125.1 6.9 %collective-permute-start.1 = (bf16[64,832]{1,0:T(8,128)(2,1)S(1)}, bf16[64,832]{1,0:T(8,128)(2,1)S(1)}, u32[]{:S(2)}, u32[]{:S(2)}) collective-permute-start(bf16[64,832]{1,0:T(8,128)(2,1)S(1)} %get-tuple-element.252), channel_id=1, source_target_pairs={{0,1},{1,2},{2,3},{3,0},{4,5},{5,6},{6,7},{7,4},{8,9},{9,10},{10,1... | collective-permute-start | bytes 319496 | tf_op jit(solution)/shard_map/while/body/eval_jaxpr/ppermute | solution.py:128
  126.3 5.7 %collective-permute-start.2 = (bf16[64,832]{1,0:T(8,128)(2,1)S(1)}, bf16[64,832]{1,0:T(8,128)(2,1)S(1)}, u32[]{:S(2)}, u32[]{:S(2)}) collective-permute-start(bf16[64,832]{1,0:T(8,128)(2,1)S(1)} %get-tuple-element.252), channel_id=1, source_target_pairs={{0,3},{1,0},{2,1},{3,2},{4,7},{5,4},{6,5},{7,6},{8,11},{9,8},{10,9... | collective-permute-start | bytes 319496 | tf_op jit(solution)/shard_map/while/body/eval_jaxpr/ppermute | solution.py:128
  135.1 1.9 %collective-permute-start.3 = (f32[32,1152]{1,0:T(8,128)S(1)}, f32[32,1152]{1,0:T(8,128)S(1)}, u32[]{:S(2)}, u32[]{:S(2)}) collective-permute-start(f32[32,1152]{1,0:T(8,128)S(1)} %get-tuple-element.254), channel_id=1, source_target_pairs={{0,4},{4,0},{1,5},{5,1},{2,6},{6,2},{3,7},{7,3},{8,12},{12,8},{9,1... | collective-permute-start | bytes 442376 | tf_op jit(solution)/shard_map/while/body/eval_jaxpr/ppermute | solution.py:124
  137.0 4.4 %collective-permute-start.4 = (f32[8,1152]{1,0:T(8,128)S(1)}, f32[8,1152]{1,0:T(8,128)S(1)}, u32[]{:S(2)}, u32[]{:S(2)}) collective-permute-start(f32[8,1152]{1,0:T(8,128)S(1)} %get-tuple-element.256), channel_id=1, source_target_pairs={{0,16},{8,24},{16,0},{24,8},{1,17},{9,25},{17,1},{25,9},{2,18},{10... | collective-permute-start | bytes 110600 | tf_op jit(solution)/shard_map/while/body/eval_jaxpr/ppermute | solution.py:133
  138.0 4.5 %collective-permute-start.5 = (f32[8,1152]{1,0:T(8,128)S(1)}, f32[8,1152]{1,0:T(8,128)S(1)}, u32[]{:S(2)}, u32[]{:S(2)}) collective-permute-start(f32[8,1152]{1,0:T(8,128)S(1)} %get-tuple-element.257), channel_id=1, source_target_pairs={{0,8},{8,16},{16,24},{24,0},{1,9},{9,17},{17,25},{25,1},{2,10},{10... | collective-permute-start | bytes 110600 | tf_op jit(solution)/shard_map/while/body/eval_jaxpr/ppermute | solution.py:133
  139.6 3.1 %collective-permute-start.6 = (f32[8,1152]{1,0:T(8,128)S(1)}, f32[8,1152]{1,0:T(8,128)S(1)}, u32[]{:S(2)}, u32[]{:S(2)}) collective-permute-start(f32[8,1152]{1,0:T(8,128)S(1)} %get-tuple-element.258), channel_id=1, source_target_pairs={{0,24},{8,0},{16,8},{24,16},{1,25},{9,1},{17,9},{25,17},{2,26},{10... | collective-permute-start | bytes 110600 | tf_op jit(solution)/shard_map/while/body/eval_jaxpr/ppermute | solution.py:133
  153.6 7.8 %collective-permute-start.7 = (f32[8,1152]{1,0:T(8,128)S(1)}, f32[8,1152]{1,0:T(8,128)S(1)}, u32[]{:S(2)}, u32[]{:S(2)}) collective-permute-start(f32[8,1152]{1,0:T(8,128)S(1)} %eval_jaxpr.9), channel_id=1, source_target_pairs={{0,16},{8,24},{16,0},{24,8},{1,17},{9,25},{17,1},{25,9},{2,18},{10... | collective-permute-start | bytes 110600 | tf_op jit(solution)/shard_map/while/body/eval_jaxpr/ppermute | solution.py:133
  154.9 7.0 %collective-permute-start.8 = (f32[8,1152]{1,0:T(8,128)S(1)}, f32[8,1152]{1,0:T(8,128)S(1)}, u32[]{:S(2)}, u32[]{:S(2)}) collective-permute-start(f32[8,1152]{1,0:T(8,128)S(1)} %eval_jaxpr.9), channel_id=1, source_target_pairs={{0,8},{8,16},{16,24},{24,0},{1,9},{9,17},{17,25},{25,1},{2,10},{10... | collective-permute-start | bytes 110600 | tf_op jit(solution)/shard_map/while/body/eval_jaxpr/ppermute | solution.py:133
  156.2 7.1 %collective-permute-start.9 = (f32[8,1152]{1,0:T(8,128)S(1)}, f32[8,1152]{1,0:T(8,128)S(1)}, u32[]{:S(2)}, u32[]{:S(2)}) collective-permute-start(f32[8,1152]{1,0:T(8,128)S(1)} %eval_jaxpr.9), channel_id=1, source_target_pairs={{0,24},{8,0},{16,8},{24,16},{1,25},{9,1},{17,9},{25,17},{2,26},{10... | collective-permute-start | bytes 110600 | tf_op jit(solution)/shard_map/while/body/eval_jaxpr/ppermute | solution.py:133
  157.6 6.3 %collective-permute-start.10 = (f32[8,1152]{1,0:T(8,128)S(1)}, f32[8,1152]{1,0:T(8,128)S(1)}, u32[]{:S(2)}, u32[]{:S(2)}) collective-permute-start(f32[8,1152]{1,0:T(8,128)S(1)} %eval_jaxpr.9), channel_id=1, source_target_pairs={{0,4},{4,0},{1,5},{5,1},{2,6},{6,2},{3,7},{7,3},{8,12},{12,8},{9,1... | collective-permute-start | bytes 110600 | tf_op jit(solution)/shard_map/while/body/eval_jaxpr/ppermute | solution.py:124
  161.3 2.5 %collective-permute-start.11 = (f32[8,1152]{1,0:T(8,128)S(1)}, f32[8,1152]{1,0:T(8,128)S(1)}, u32[]{:S(2)}, u32[]{:S(2)}) collective-permute-start(f32[8,1152]{1,0:T(8,128)S(1)} %collective-permute-done.7), channel_id=1, source_target_pairs={{0,4},{4,0},{1,5},{5,1},{2,6},{6,2},{3,7},{7,3},{8,12},{12,8},{9,1... | collective-permute-start | bytes 110600 | tf_op jit(solution)/shard_map/while/body/eval_jaxpr/ppermute | solution.py:124
  161.9 2.2 %collective-permute-start.12 = (f32[8,1152]{1,0:T(8,128)S(1)}, f32[8,1152]{1,0:T(8,128)S(1)}, u32[]{:S(2)}, u32[]{:S(2)}) collective-permute-start(f32[8,1152]{1,0:T(8,128)S(1)} %collective-permute-done.8), channel_id=1, source_target_pairs={{0,4},{4,0},{1,5},{5,1},{2,6},{6,2},{3,7},{7,3},{8,12},{12,8},{9,1... | collective-permute-start | bytes 110600 | tf_op jit(solution)/shard_map/while/body/eval_jaxpr/ppermute | solution.py:124
  163.3 1.5 collective-permute-start.13

commit v6 on v5

--- a/solution.py
+++ b/solution.py
@@ -158,7 +158,7 @@
         def x_of(place):
             return place[0] // (snp * 2) % ring
 
-        def call_with_place(body, outs, *operands, scalars=(), scratch=()):
+        def call_with_place(body, outs, *operands, scalars=(), scratch=(), out_specs=None):
             smem = pl.BlockSpec(memory_space=pltpu.SMEM)
             specs = [smem] * (1 + len(scalars)) + [
                 pl.BlockSpec(memory_space=pltpu.VMEM) for _ in operands
@@ -168,6 +168,7 @@
                 out_shape=outs,
                 in_specs=specs,
                 scratch_shapes=scratch,
+                **({} if out_specs is None else {"out_specs": out_specs}),
                 compiler_params=pltpu.CompilerParams(vmem_limit_bytes=48 * 1024 * 1024),
             )(place, *scalars, *operands)
 
@@ -467,12 +468,22 @@
 
         def last_kernel(place, *refs):
             tiles, rest = refs[: 2 * ring], refs[2 * ring :]
-            samples, upper, raw, basis, projection, snp_basis, whole = rest
-            snp_basis[...] = exact_dot(upper[...], raw[...], 1, 0)
+            samples, upper, raw, *outs = rest[:6]
+            whole, *holds, sems = rest[6:]
+            copies = [
+                pltpu.make_async_copy(hold, out, sems.at[n])
+                for n, (hold, out) in enumerate(zip(holds, outs))
+            ]
+            holds[2][...] = exact_dot(upper[...], raw[...], 1, 0)
+            copies[2].start()
             columns, gram = read_sum(place, tiles, whole)
             factor = inverse_factor(gram / sample_count, True)
-            basis[...] = exact_dot(factor, samples[...], 1, 0)
-            projection[...] = exact_dot(factor / math.sqrt(sample_count), columns, 1, 0)
+            holds[1][...] = exact_dot(factor / math.sqrt(sample_count), columns, 1, 0)
+            copies[1].start()
+            holds[0][...] = exact_dot(factor, samples[...], 1, 0)
+            copies[0].start()
+            for copy in copies:
+                copy.wait()
 
         samples_shape = shape_of((width, row_count))
         columns_shape = shape_of((width, col_width))
@@ -526,7 +537,14 @@
             samples,
             factor,
             raw,
-            scratch=whole_scratch,
+            scratch=[
+                *whole_scratch,
+                pltpu.VMEM((width, row_count), F32),
+                pltpu.VMEM((width, col_width), F32),
+                pltpu.VMEM((width, col_width), F32),
+                pltpu.SemaphoreType.DMA((3,)),
+            ],
+            out_specs=(pl.BlockSpec(memory_space=pltpu.HBM),) * 3,
         )
         return (basis.T, projection.T, columns.T)
 

time: 169 us -> 169 us (level)
  no operation moved by 1% of the time
where the time goes in v6:
time: 169 us
  starting transfers between devices  71.9 us (43%)
  blocking collectives  35.6 us (21%)
  waiting for transfers between devices  29.3 us (17%)
  Pallas kernels  25.2 us (15%)
  local copies, waits for them, and re-layouts  6 us (4%)
    all_to_all x3, blocking collectives, samp_sum(): lax.all_to_all(spread, 'z', 0, 0)  35.6 us
    ppermute x16, starting transfers between devices, swap(): return lax.ppermute(value, 'core', [(0, 1), (1, 0)])  26.2 us
    pallas_call x18, Pallas kernels, call_with_place(): pl.pallas_call(body, out_shape=outs, in_specs=specs, scratch_shapes=scrat...  22.9 us
    ppermute x18, starting transfers between devices, x_shift(): return lax.ppermute(value, 'x', [(i, (i + k) % ring) for i in range(ring)])  21.6 us
    ppermute x9, starting transfers between devices, snp_others(): lax.ppermute(value, 'snp', [(i, (i + k) % snp) for i in range(snp)])  14.8 us
    ppermute x9, waiting for transfers between devices, snp_others(): lax.ppermute(value, 'snp', [(i, (i + k) % snp) for i in range(snp)])  11.8 us
    all_to_all x1, starting transfers between devices, on_device(): lax.all_to_all(call_with_place(pack_kernel, shape_of((chips, SUB, LANES))...  9.3 us
    ppermute x18, waiting for transfers between devices, x_shift(): return lax.ppermute(value, 'x', [(i, (i + k) % ring) for i in range(ring)])  8.85 us
  transfers between devices with their start and end apart: 44, of which 23 were waited for; matrix products, arithmetic and copies ran while one was open for 0% of the time, Pallas kernels for 3%

profile of v6, /device:TPU:1, one launch (start us, length us, event | category | flops | bytes accessed | tf_op | source)
XLA Modules:
  0.0 169.0 jit_solution(4820697220388835569)
XLA Ops:
  0.6 3.3 %collective-permute-start.14 = (f32[16,20]{1,0:T(8,128)}, f32[16,20]{1,0:T(8,128)S(1)}, u32[]{:S(2)}, u32[]{:S(2)}) collective-permute-start(f32[16,20]{1,0:T(8,128)} %mine.1), channel_id=1, source_target_pairs={{0,4},{4,0},{1,5},{5,1},{2,6},{6,2},{3,7},{7,3},{8,12},{12,8},{9,1... | collective-permute-start | bytes 3848 | tf_op jit(solution)/shard_map/ppermute | solution.py:124
  4.0 1.0 collective-permute-done.14.other
  5.0 0.7 copy-done.4
  5.7 0.7 shard_map.113
  6.4 9.3 %all-to-all-start.1 = ((f32[32,8,128]{2,1,0:T(8,128)}), f32[32,8,128]{2,1,0:T(8,128)S(1)}, u32[]{:S(2)}, u32[]{:S(2)}) async-start(f32[32,8,128]{2,1,0:T(8,128)} %shard_map.113), calls=%async_computation.1 | async-start | bytes 262144 | tf_op jit(solution)/shard_map/all_to_all | solution.py:281
  15.8 1.7 %copy-done = s32[640,1024]{1,0:T(8,128)S(1)} copy-done((s32[640,1024]{1,0:T(8,128)S(1)}, s32[640,1024]{1,0:T(8,128)}, u32[]{:S(2)}) %copy-start) | copy-done | bytes 2621464
  17.5 0.9 copy-done.1
  21.1 2.4 %shard_map.112 = (bf16[640,1024]{1,0:T(8,128)(2,1)S(1)}, f32[64,640]{1,0:T(8,128)S(1)}, s32[16]{0:T(128)S(1)}) custom-call(s32[1]{0:T(128)} %bitcast.place, s32[12]{0:T(128)S(1)} %copy-done.5, s32[48]{0:T(128)S(1)} %copy-done.9, s32[48]{0:T(128)S(1)} %copy-done.10, s32[640,1024]{1,0:T(8,128)S(1)} %copy-done, f32[1,1024]{1,0:T(1,128)S(1)} %bitcast.11, ...), custom_call_target="tpu_custom_call" | custom-call | tf_op jit(solution)/shard_map/pallas_call | solution.py:240
  23.4 1.7 all-to-all-done.1.tiles
  25.6 3.0 %collective-permute-start.15 = (f32[64,768]{1,0:T(8,128)S(1)}, f32[64,768]{1,0:T(8,128)S(1)}, u32[]{:S(2)}, u32[]{:S(2)}) collective-permute-start(f32[64,768]{1,0:T(8,128)S(1)} %shard_map.114.w0), channel_id=1, source_target_pairs={{0,2},{1,3},{2,0},{3,1},{4,6},{5,7},{6,4},{7,5},{8,10},{9,11},{10,... | collective-permute-start | bytes 589832 | tf_op jit(solution)/shard_map/ppermute | solution.py:128
  29.0 2.3 %collective-permute-start.17 = (f32[64,768]{1,0:T(8,128)S(1)}, f32[64,768]{1,0:T(8,128)S(1)}, u32[]{:S(2)}, u32[]{:S(2)}) collective-permute-start(f32[64,768]{1,0:T(8,128)S(1)} %shard_map.114.w0), channel_id=1, source_target_pairs={{0,3},{1,0},{2,1},{3,2},{4,7},{5,4},{6,5},{7,6},{8,11},{9,8},{10,9... | collective-permute-start | bytes 589832 | tf_op jit(solution)/shard_map/ppermute | solution.py:128
  31.3 2.9 %shard_map.115.x = bf16[640,1024]{1,0:T(8,128)(2,1)S(1)} custom-call(s32[1]{0:T(128)} %bitcast.place, s32[12]{0:T(128)S(1)} %copy-done.6, s32[16]{0:T(128)S(1)} %get-tuple-element.107.bits, f32[20]{0:T(128)S(1)} %copy-done.8, bf16[640,1024]{1,0:T(8,128)(2,1)S(1)} %get-tuple-element.109.obs, f32[20,640]{1,0:T(8,128)S(1)} %bitcast.9, ...), custom_call_target="tpu_custom_call" | custom-call | tf_op jit(solution)/shard_map/pallas_call | solution.py:166
  34.2 3.2 %collective-permute-done.16.w2 = f32[64,768]{1,0:T(8,128)S(1)} collective-permute-done((f32[64,768]{1,0:T(8,128)S(1)}, f32[64,768]{1,0:T(8,128)S(1)}, u32[]{:S(2)}, u32[]{:S(2)}) %collective-permute-start.16) | collective-permute-done | bytes 196640 | tf_op jit(solution)/shard_map/ppermute | solution.py:128
  37.4 2.2 %shard_map.116 = (f32[64,640]{1,0:T(8,128)}, f32[32,1152]{1,0:T(8,128)S(1)}, f32[32,1152]{1,0:T(8,128)S(1)}) custom-call(s32[1]{0:T(128)} %bitcast.place, s32[12]{0:T(128)S(1)} %copy-done.6, s32[16]{0:T(128)S(1)} %get-tuple-element.107.bits, f32[20]{0:T(128)S(1)} %copy-done.8, f32[64,768]{1,0:T(8,128)S(1)} %shard_map.114.w0, ...), custom_call_target="tpu_custom_call" | custom-call | tf_op jit(solution)/shard_map/pallas_call | solution.py:166
  39.6 1.9 %collective-permute-start.18 = (f32[32,1152]{1,0:T(8,128)S(1)}, f32[32,1152]{1,0:T(8,128)S(1)}, u32[]{:S(2)}, u32[]{:S(2)}) collective-permute-start(f32[32,1152]{1,0:T(8,128)S(1)} %get-tuple-element.111), channel_id=1, source_target_pairs={{0,4},{4,0},{1,5},{5,1},{2,6},{6,2},{3,7},{7,3},{8,12},{12,8},{9,1... | collective-permute-start | bytes 442376 | tf_op jit(solution)/shard_map/ppermute | solution.py:124
  41.5 1.0 collective-permute-done.18.got
  42.6 2.7 %collective-permute-start.20 = (f32[8,1152]{1,0:T(8,128)S(1)}, f32[8,1152]{1,0:T(8,128)S(1)}, u32[]{:S(2)}, u32[]{:S(2)}) collective-permute-start(f32[8,1152]{1,0:T(8,128)S(1)} %get-tuple-element.114), channel_id=1, source_target_pairs={{0,24},{8,0},{16,8},{24,16},{1,25},{9,1},{17,9},{25,17},{2,26},{10... | collective-permute-start | bytes 110600 | tf_op jit(solution)/shard_map/ppermute | solution.py:133
  45.3 1.3 collective-permute-done.19.a
  46.6 3.0 %collective-permute-done.21.c = f32[8,1152]{1,0:T(8,128)S(1)} collective-permute-done((f32[8,1152]{1,0:T(8,128)S(1)}, f32[8,1152]{1,0:T(8,128)S(1)}, u32[]{:S(2)}, u32[]{:S(2)}) %collective-permute-start.21) | collective-permute-done | bytes 36896 | tf_op jit(solution)/shard_map/ppermute | solution.py:133
  49.6 14.2 %all_to_all.16.parts = f32[8,8,1152]{2,1,0:T(8,128)S(1)} all-to-all(f32[8,8,1152]{2,1,0:T(8,128)S(1)} %shard_map.118), channel_id=1, replica_groups=mesh['z'=8,'x'=4,'core'=2,'snp'=4] {'z'}, dimensions={0} | all-to-all | bytes 589824 | tf_op jit(solution)/shard_map/all_to_all | solution.py:397
  63.8 1.6 collective-permute-start.22
  65.7 2.4 %collective-permute-start.24 = (f32[8,1152]{1,0:T(8,128)S(1)}, f32[8,1152]{1,0:T(8,128)S(1)}, u32[]{:S(2)}, u32[]{:S(2)}) collective-permute-start(f32[8,1152]{1,0:T(8,128)S(1)} %shard_map.119), channel_id=1, source_target_pairs={{0,24},{8,0},{16,8},{24,16},{1,25},{9,1},{17,9},{25,17},{2,26},{10... | collective-permute-start | bytes 110600 | tf_op jit(solution)/shard_map/ppermute | solution.py:133
  68.1 4.6 %collective-permute-start.25 = (f32[8,1152]{1,0:T(8,128)S(1)}, f32[8,1152]{1,0:T(8,128)S(1)}, u32[]{:S(2)}, u32[]{:S(2)}) collective-permute-start(f32[8,1152]{1,0:T(8,128)S(1)} %shard_map.119), channel_id=1, source_target_pairs={{0,4},{4,0},{1,5},{5,1},{2,6},{6,2},{3,7},{7,3},{8,12},{12,8},{9,1... | collective-permute-start | bytes 110600 | tf_op jit(solution)/shard_map/ppermute | solution.py:124
  73.1 1.5 collective-permute-start.27
  74.6 0.8 collective-permute-done.27
  75.8 89.0 %while.30 = (s32[]{:T(128)}, f32[8,1152]{1,0:T(8,128)S(1)}, f32[8,1152]{1,0:T(8,128)S(1)}, f32[8,1152]{1,0:T(8,128)S(1)}, f32[8,1152]{1,0:T(8,128)S(1)}, /*index...) while((s32[]{:T(128)}, f32[8,1152]{1,0:T(8,128)S(1)}, ...), condition=%wide.region_1.0_spmd, body=%wide.region_0.0_spmd.sunk | while | flops 2 | bytes 3670717 | solution.py:522
  75.8 2.9 %eval_jaxpr.5 = (f32[64,1024]{1,0:T(8,128)}, f32[64,640]{1,0:T(8,128)S(1)}, f32[64,64]{1,0:T(8,128)S(1)}, bf16[64,832]{1,0:T(8,128)(2,1)S(1)}) custom-call(s32[1]{0:T(128)} %get-tuple-element.304.place, f32[8,1152]{1,0:T(8,128)S(1)} %get-tuple-element.278.refs_0_, f32[8,1152]{1,0:T(8,128)S(1)} %get-tuple-element.279.refs_1_, ...), custom_call_target="tpu_custom_call" | custom-call | tf_op jit(solution)/shard_map/while/body/eval_jaxpr/pallas_call | solution.py:166
  78.7 1.9 %collective-permute-start = (bf16[64,832]{1,0:T(8,128)(2,1)S(1)}, bf16[64,832]{1,0:T(8,128)(2,1)S(1)}, u32[]{:S(2)}, u32[]{:S(2)}) collective-permute-start(bf16[64,832]{1,0:T(8,128)(2,1)S(1)} %get-tuple-element.252), channel_id=1, source_target_pairs={{0,2},{1,3},{2,0},{3,1},{4,6},{5,7},{6,4},{7,5},{8,10},{9,11},{10,... | collective-permute-start | bytes 319496 | tf_op jit(solution)/shard_map/while/body/eval_jaxpr/ppermute | solution.py:128
  80.5 1.2 collective-permute-start.1
  81.7 1.5 collective-permute-start.2
  83.2 1.6 collective-permute-done.a
  84.8 2.8 %collective-permute-done.1.b = bf16[64,832]{1,0:T(8,128)(2,1)S(1)} collective-permute-done((bf16[64,832]{1,0:T(8,128)(2,1)S(1)}, bf16[64,832]{1,0:T(8,128)(2,1)S(1)}, u32[]{:S(2)}, u32[]{:S(2)}) %collective-permute-start.1) | collective-permute-done | bytes 106528 | tf_op jit(solution)/shard_map/while/body/eval_jaxpr/ppermute | solution.py:128
  87.6 3.1 %eval_jaxpr.6 = (f32[64,640]{1,0:T(8,128)}, f32[64,64]{1,0:T(8,128)}, f32[32,1152]{1,0:T(8,128)S(1)}, f32[32,1152]{1,0:T(8,128)S(1)}) custom-call(s32[1]{0:T(128)} %get-tuple-element.304.place, f32[64,640]{1,0:T(8,128)S(1)} %get-tuple-element.250.product, f32[64,64]{1,0:T(8,128)S(1)} %get-tuple-element.251.gram, bf16[64,832]{1,0:T(8,128)(2,1)S(1)} %collective-permute-done.a, ...), custom_call_target="tpu_custom_call" | custom-call | tf_op jit(solution)/shard_map/while/body/eval_jaxpr/pallas_call | solution.py:166
  91.3 1.0 collective-permute-done.3.got
  92.4 1.2 collective-permute-start.4
  93.6 2.1 %collective-permute-start.5 = (f32[8,1152]{1,0:T(8,128)S(1)}, f32[8,1152]{1,0:T(8,128)S(1)}, u32[]{:S(2)}, u32[]{:S(2)}) collective-permute-start(f32[8,1152]{1,0:T(8,128)S(1)} %get-tuple-element.257), channel_id=1, source_target_pairs={{0,8},{8,16},{16,24},{24,0},{1,9},{9,17},{17,25},{25,1},{2,10},{10... | collective-permute-start | bytes 110600 | tf_op jit(solution)/shard_map/while/body/eval_jaxpr/ppermute | solution.py:133
  96.8 1.4 collective-permute-done.5.b
  98.8 10.7 %all_to_all.17.parts = bf16[8,8,1280]{2,1,0:T(8,128)(2,1)S(1)} all-to-all(bf16[8,8,1280]{2,1,0:T(8,128)(2,1)S(1)} %eval_jaxpr.8), channel_id=1, replica_groups=mesh['z'=8,'x'=4,'core'=2,'snp'=4] {'z'}, dimensions={0} | all-to-all | bytes 327680 | tf_op jit(solution)/shard_map/while/body/eval_jaxpr/all_to_all | solution.py:397
  110.1 2.1 %collective-permute-start.8 = (f32[8,1152]{1,0:T(8,128)S(1)}, f32[8,1152]{1,0:T(8,128)S(1)}, u32[]{:S(2)}, u32[]{:S(2)}) collective-permute-start(f32[8,1152]{1,0:T(8,128)S(1)} %eval_jaxpr.9), channel_id=1, source_target_pairs={{0,8},{8,16},{16,24},{24,0},{1,9},{9,17},{17,25},{25,1},{2,10},{10... | collective-permute-start | bytes 110600 | tf_op jit(solution)/shard_map/while/body/eval_jaxpr/ppermute | solution.py:133
  112.8 3.7 %collective-permute-start.10 = (f32[8,1152]{1,0:T(8,128)S(1)}, f32[8,1152]{1,0:T(8,128)S(1)}, u32[]{:S(2)}, u32[]{:S(2)}) collective-permute-start(f32[8,1152]{1,0:T(8,128)S(1)} %eval_jaxpr.9), channel_id=1, source_target_pairs={{0,4},{4,0},{1,5},{5,1},{2,6},{6,2},{3,7},{7,3},{8,12},{12,8},{9,1... | collective-permute-start | bytes 110600 | tf_op jit(solution)/shard_map/while/body/eval_jaxpr/ppermute | solution.py:124
  116.5 1.5 collective-permute-start.11
  118.4 1.0 collective-permute-start.13
  119.5 0.9 collective-permute-done.13
  120.3 2.9 %eval_jaxpr.5 = (f32[64,1024]{1,0:T(8,128)}, f32[64,640]{1,0:T(8,128)S(1)}, f32[64,64]{1,0:T(8,128)S(1)}, bf16[64,832]{1,0:T(8,128)(2,1)S(1)}) custom-call(s32[1]{0:T(128)} %get-tuple-element.304.place, f32[8,1152]{1,0:T(8,128)S(1)} %get-tuple-element.278.refs_0_, f32[8,1152]{1,0:T(8,128)S(1)} %get-tuple-element.279.refs_1_, ...), custom_call_target="tpu_custom_call" | custom-call | tf_op jit(solution)/shard_map/while/body/eval_jaxpr/pallas_call | solution.py:166
  123.2 1.9 %collective-permute-start = (bf16[64,832]{1,0:T(8,128)(2,1)S(1)}, bf16[64,832]{1,0:T(8,128)(2,1)S(1)}, u32[]{:S(2)}, u32[]{:S(2)}) collective-permute-start(bf16[64,832]{1,0:T(8,128)(2,1)S(1)} %get-tuple-element.252), channel_id=1, source_target_pairs={{0,2},{1,3},{2,0},{3,1},{4,6},{5,7},{6,4},{7,5},{8,10},{9,11},{10,... | collective-permute-start | bytes 319496 | tf_op jit(solution)/shard_map/while/body/eval_jaxpr/ppermute | solution.py:128
  125.1 1.2 collective-permute-start.1
  126.3 1.4 collective-permute-start.2
  127.8 1.4 collective-permute-done.a
  129.2 2.8 %collective-permute-done.1.b = bf16[64,832]{1,0:T(8,128)(2,1)S(1)} collective-permute-done((bf16[64,832]{1,0:T(8,128)(2,1)S(1)}, bf16[64,832]{1,0:T(8,128)(2,1)S(1)}, u32[]{:S(2)}, u32[]{:S(2)}) %collective-permute-start.1) | collective-permute-done | bytes 106528 | tf_op jit(solution)/shard_map/while/body/eval_jaxpr/ppermute | solution.py:128
  132.0 3.1 %eval_jaxpr.6 = (f32[64,640]{1,0:T(8,128)}, f32[64,64]{1,0:T(8,128)}, f32[32,1152]{1,0:T(8,128)S(1)}, f32[32,1152]{1,0:T(8,128)S(1)}) custom-call(s32[1]{0:T(128)} %get-tuple-element.304.place, f32[64,640]{1,0:T(8,128)S(1)} %get-tuple-element.250.product, f32[64,64]{1,0:T(8,128)S(1)} %get-tuple-element.251.gram, bf16[64,832]{1,0:T(8,128)(2,1)S(1)} %collective-permute-done.a, ...), custom_call_target="tpu_custom_call" | custom-call | tf_op jit(solution)/shard_map/while/body/eval_jaxpr/pallas_call | solution.py:166
  135.1 0.9 collective-permute-start.3
  135.9 1.0 collective-permute-done.3.got
  137.0 1.0 collective-permute-start.4
  138.0 1.6 collective-permute-start.5
  139.6 1.1 collective-permute-start.6
  140.6 0.7 collective-permute-done.4.a
  141.4 1.1 collective-permute-done.5.b
  142.7 10.7 %all_to_all.17.parts = bf16[8,8,1280]{2,1,0:T(8,128)(2,1)S(1)} all-to-all(bf16[8,8,1280]{2,1,0:T(8,128)(2,1)S(1)} %eval_jaxpr.8), channel_id=1, replica_groups=mesh['z'=8,'x'=4,'core'=2,'snp'=4] {'z'}, dimensions={0} | all-to-all | bytes 327680 | tf_op jit(solution)/shard_map/while/body/eval_jaxpr/all_to_all | solution.py:397
  153.6 1.3 collective-permute-start.7
  154.9 1.3 collective-permute-start.8
  156.2 1.4 collective-permute-start.9
  157.6 3.7 %collective-permute-start.10 = (f32[8,1152]{1,0:T(8,128)S(1)}, f32[8,1152]{1,0:T(8,128)S(1)}, u32[]{:S(2)}, u32[]{:S(2)}) collective-permute-start(f32[8,1152]{1,0:T(8,128)S(1)} %eval_jaxpr.9), channel_id=1, source_target_pairs={{0,4},{4,0},{1,5},{5,1},{2,6},{6,2},{3,7},{7,3},{8,12},{12,8},{9,1... | collective-permute-start | bytes 110600 | tf_op jit(solution)/shard_map/while/body/eval_jaxpr/ppermute | solution.py:124
  161.9 1.3 collective-permute-start.12
  164.7 4.1 %shard_map.120 = (f32[64,640]{1,0:T(8,128)}, f32[64,1024]{1,0:T(8,128)}, f32[64,1024]{1,0:T(8,128)}) custom-call(s32[1]{0:T(128)} %bitcast.place, f32[8,1152]{1,0:T(8,128)S(1)} %get-tuple-element.117.refs_0_, f32[8,1152]{1,0:T(8,128)S(1)} %get-tuple-element.118.refs_1_, f32[8,1152]{1,0:T(8,128)S(1)} %get-tuple-element.119.refs_2_, ...), custom_call_target="tpu_custom_call" | custom-call | tf_op jit(solution)/shard_map/pallas_call | solution.py:166
  (71 shorter events, 11.3 us)
Async XLA Ops:
  0.6 4.4 %collective-permute-start.14 = (f32[16,20]{1,0:T(8,128)}, f32[16,20]{1,0:T(8,128)S(1)}, u32[]{:S(2)}, u32[]{:S(2)}) collective-permute-start(f32[16,20]{1,0:T(8,128)} %mine.1), channel_id=1, source_target_pairs={{0,4},{4,0},{1,5},{5,1},{2,6},{6,2},{3,7},{7,3},{8,12},{12,8},{9,1... | collective-permute-start | bytes 3848 | tf_op jit(solution)/shard_map/ppermute | solution.py:124
  5.0 0.7 copy-start.4
  6.4 18.7 %all-to-all-start.1 = ((f32[32,8,128]{2,1,0:T(8,128)}), f32[32,8,128]{2,1,0:T(8,128)S(1)}, u32[]{:S(2)}, u32[]{:S(2)}) async-start(f32[32,8,128]{2,1,0:T(8,128)} %shard_map.113), calls=%async_computation.1 | async-start | bytes 262144 | tf_op jit(solution)/shard_map/all_to_all | solution.py:281
  15.7 1.7 %copy-start = (s32[640,1024]{1,0:T(8,128)S(1)}, s32[640,1024]{1,0:T(8,128)}, u32[]{:S(2)}) copy-start(s32[640,1024]{1,0:T(8,128)} %geno_in.1) | copy-start | bytes 7864324
  17.5 0.9 copy-start.1
  18.4 0.7 copy-start.5
  19.0 0.7 copy-start.7
  19.7 0.7 copy-start.9
  20.4 0.7 copy-start.10
  21.0 4.0 %copy-start.2 = (bf16[1024,64]{0,1:T(8,128)(2,1)S(1)}, bf16[1024,64]{0,1:T(8,128)(2,1)}, u32[]{:S(2)}) copy-start(bf16[1024,64]{0,1:T(8,128)(2,1)} %param.16) | copy-start | bytes 393220
  21.0 10.3 %copy-start.3 = (f32[640,20]{0,1:T(8,128)S(1)}, f32[640,20]{0,1:T(8,128)}, u32[]{:S(2)}) copy-start(f32[640,20]{0,1:T(8,128)} %param.13) | copy-start | bytes 153604
  21.0 10.3 %copy-start.6 = (s32[12]{0:T(128)S(1)}, s32[12]{0:T(128)}, u32[]{:S(2)}) copy-start(s32[12]{0:T(128)} %sizes.3) | copy-start | bytes 148
  21.0 10.3 %copy-start.8 = (f32[20]{0:T(128)S(1)}, f32[20]{0:T(128)}, u32[]{:S(2)}) copy-start(f32[20]{0:T(128)} %scale.3) | copy-start | bytes 244
  25.6 8.6 %collective-permute-start.15 = (f32[64,768]{1,0:T(8,128)S(1)}, f32[64,768]{1,0:T(8,128)S(1)}, u32[]{:S(2)}, u32[]{:S(2)}) collective-permute-start(f32[64,768]{1,0:T(8,128)S(1)} %shard_map.114.w0), channel_id=1, source_target_pairs={{0,2},{1,3},{2,0},{3,1},{4,6},{5,7},{6,4},{7,5},{8,10},{9,11},{10,... | collective-permute-start | bytes 589832 | tf_op jit(solution)/shard_map/ppermute | solution.py:128
  28.6 8.8 %collective-permute-start.16 = (f32[64,768]{1,0:T(8,128)S(1)}, f32[64,768]{1,0:T(8,128)S(1)}, u32[]{:S(2)}, u32[]{:S(2)}) collective-permute-start(f32[64,768]{1,0:T(8,128)S(1)} %shard_map.114.w0), channel_id=1, source_target_pairs={{0,1},{1,2},{2,3},{3,0},{4,5},{5,6},{6,7},{7,4},{8,9},{9,10},{10,1... | collective-permute-start | bytes 589832 | tf_op jit(solution)/shard_map/ppermute | solution.py:128
  29.0 8.4 %collective-permute-start.17 = (f32[64,768]{1,0:T(8,128)S(1)}, f32[64,768]{1,0:T(8,128)S(1)}, u32[]{:S(2)}, u32[]{:S(2)}) collective-permute-start(f32[64,768]{1,0:T(8,128)S(1)} %shard_map.114.w0), channel_id=1, source_target_pairs={{0,3},{1,0},{2,1},{3,2},{4,7},{5,4},{6,5},{7,6},{8,11},{9,8},{10,9... | collective-permute-start | bytes 589832 | tf_op jit(solution)/shard_map/ppermute | solution.py:128
  39.6 2.9 %collective-permute-start.18 = (f32[32,1152]{1,0:T(8,128)S(1)}, f32[32,1152]{1,0:T(8,128)S(1)}, u32[]{:S(2)}, u32[]{:S(2)}) collective-permute-start(f32[32,1152]{1,0:T(8,128)S(1)} %get-tuple-element.111), channel_id=1, source_target_pairs={{0,4},{4,0},{1,5},{5,1},{2,6},{6,2},{3,7},{7,3},{8,12},{12,8},{9,1... | collective-permute-start | bytes 442376 | tf_op jit(solution)/shard_map/ppermute | solution.py:124
  42.5 4.1 %collective-permute-start.19 = (f32[8,1152]{1,0:T(8,128)S(1)}, f32[8,1152]{1,0:T(8,128)S(1)}, u32[]{:S(2)}, u32[]{:S(2)}) collective-permute-start(f32[8,1152]{1,0:T(8,128)S(1)} %get-tuple-element.113), channel_id=1, source_target_pairs={{0,8},{8,16},{16,24},{24,0},{1,9},{9,17},{17,25},{25,1},{2,10},{10... | collective-permute-start | bytes 110600 | tf_op jit(solution)/shard_map/ppermute | solution.py:133
  42.6 4.0 %collective-permute-start.20 = (f32[8,1152]{1,0:T(8,128)S(1)}, f32[8,1152]{1,0:T(8,128)S(1)}, u32[]{:S(2)}, u32[]{:S(2)}) collective-permute-start(f32[8,1152]{1,0:T(8,128)S(1)} %get-tuple-element.114), channel_id=1, source_target_pairs={{0,24},{8,0},{16,8},{24,16},{1,25},{9,1},{17,9},{25,17},{2,26},{10... | collective-permute-start | bytes 110600 | tf_op jit(solution)/shard_map/ppermute | solution.py:133
  45.3 4.3 %collective-permute-start.21 = (f32[8,1152]{1,0:T(8,128)S(1)}, f32[8,1152]{1,0:T(8,128)S(1)}, u32[]{:S(2)}, u32[]{:S(2)}) collective-permute-start(f32[8,1152]{1,0:T(8,128)S(1)} %get-tuple-element.115), channel_id=1, source_target_pairs={{0,16},{8,24},{16,0},{24,8},{1,17},{9,25},{17,1},{25,9},{2,18},{10... | collective-permute-start | bytes 110600 | tf_op jit(solution)/shard_map/ppermute | solution.py:133
  63.8 8.8 %collective-permute-start.22 = (f32[8,1152]{1,0:T(8,128)S(1)}, f32[8,1152]{1,0:T(8,128)S(1)}, u32[]{:S(2)}, u32[]{:S(2)}) collective-permute-start(f32[8,1152]{1,0:T(8,128)S(1)} %shard_map.119), channel_id=1, source_target_pairs={{0,16},{8,24},{16,0},{24,8},{1,17},{9,25},{17,1},{25,9},{2,18},{10... | collective-permute-start | bytes 110600 | tf_op jit(solution)/shard_map/ppermute | solution.py:133
  65.4 7.7 %collective-permute-start.23 = (f32[8,1152]{1,0:T(8,128)S(1)}, f32[8,1152]{1,0:T(8,128)S(1)}, u32[]{:S(2)}, u32[]{:S(2)}) collective-permute-start(f32[8,1152]{1,0:T(8,128)S(1)} %shard_map.119), channel_id=1, source_target_pairs={{0,8},{8,16},{16,24},{24,0},{1,9},{9,17},{17,25},{25,1},{2,10},{10... | collective-permute-start | bytes 110600 | tf_op jit(solution)/shard_map/ppermute | solution.py:133
  65.7 8.9 %collective-permute-start.24 = (f32[8,1152]{1,0:T(8,128)S(1)}, f32[8,1152]{1,0:T(8,128)S(1)}, u32[]{:S(2)}, u32[]{:S(2)}) collective-permute-start(f32[8,1152]{1,0:T(8,128)S(1)} %shard_map.119), channel_id=1, source_target_pairs={{0,24},{8,0},{16,8},{24,16},{1,25},{9,1},{17,9},{25,17},{2,26},{10... | collective-permute-start | bytes 110600 | tf_op jit(solution)/shard_map/ppermute | solution.py:133
  68.1 6.5 %collective-permute-start.25 = (f32[8,1152]{1,0:T(8,128)S(1)}, f32[8,1152]{1,0:T(8,128)S(1)}, u32[]{:S(2)}, u32[]{:S(2)}) collective-permute-start(f32[8,1152]{1,0:T(8,128)S(1)} %shard_map.119), channel_id=1, source_target_pairs={{0,4},{4,0},{1,5},{5,1},{2,6},{6,2},{3,7},{7,3},{8,12},{12,8},{9,1... | collective-permute-start | bytes 110600 | tf_op jit(solution)/shard_map/ppermute | solution.py:124
  72.6 2.0 %collective-permute-start.26 = (f32[8,1152]{1,0:T(8,128)S(1)}, f32[8,1152]{1,0:T(8,128)S(1)}, u32[]{:S(2)}, u32[]{:S(2)}) collective-permute-start(f32[8,1152]{1,0:T(8,128)S(1)} %collective-permute-done.22), channel_id=1, source_target_pairs={{0,4},{4,0},{1,5},{5,1},{2,6},{6,2},{3,7},{7,3},{8,12},{12,8},{9,1... | collective-permute-start | bytes 110600 | tf_op jit(solution)/shard_map/ppermute | solution.py:124
  73.1 2.3 %collective-permute-start.27 = (f32[8,1152]{1,0:T(8,128)S(1)}, f32[8,1152]{1,0:T(8,128)S(1)}, u32[]{:S(2)}, u32[]{:S(2)}) collective-permute-start(f32[8,1152]{1,0:T(8,128)S(1)} %collective-permute-done.23), channel_id=1, source_target_pairs={{0,4},{4,0},{1,5},{5,1},{2,6},{6,2},{3,7},{7,3},{8,12},{12,8},{9,1... | collective-permute-start | bytes 110600 | tf_op jit(solution)/shard_map/ppermute | solution.py:124
  74.6 1.2 collective-permute-start.28
  78.7 6.2 %collective-permute-start = (bf16[64,832]{1,0:T(8,128)(2,1)S(1)}, bf16[64,832]{1,0:T(8,128)(2,1)S(1)}, u32[]{:S(2)}, u32[]{:S(2)}) collective-permute-start(bf16[64,832]{1,0:T(8,128)(2,1)S(1)} %get-tuple-element.252), channel_id=1, source_target_pairs={{0,2},{1,3},{2,0},{3,1},{4,6},{5,7},{6,4},{7,5},{8,10},{9,11},{10,... | collective-permute-start | bytes 319496 | tf_op jit(solution)/shard_map/while/body/eval_jaxpr/ppermute | solution.py:128
  80.5 7.1 %collective-permute-start.1 = (bf16[64,832]{1,0:T(8,128)(2,1)S(1)}, bf16[64,832]{1,0:T(8,128)(2,1)S(1)}, u32[]{:S(2)}, u32[]{:S(2)}) collective-permute-start(bf16[64,832]{1,0:T(8,128)(2,1)S(1)} %get-tuple-element.252), channel_id=1, source_target_pairs={{0,1},{1,2},{2,3},{3,0},{4,5},{5,6},{6,7},{7,4},{8,9},{9,10},{10,1... | collective-permute-start | bytes 319496 | tf_op jit(solution)/shard_map/while/body/eval_jaxpr/ppermute | solution.py:128
  81.7 5.9 %collective-permute-start.2 = (bf16[64,832]{1,0:T(8,128)(2,1)S(1)}, bf16[64,832]{1,0:T(8,128)(2,1)S(1)}, u32[]{:S(2)}, u32[]{:S(2)}) collective-permute-start(bf16[64,832]{1,0:T(8,128)(2,1)S(1)} %get-tuple-element.252), channel_id=1, source_target_pairs={{0,3},{1,0},{2,1},{3,2},{4,7},{5,4},{6,5},{7,6},{8,11},{9,8},{10,9... | collective-permute-start | bytes 319496 | tf_op jit(solution)/shard_map/while/body/eval_jaxpr/ppermute | solution.py:128
  90.7 1.7 collective-permute-start.3
  92.4 4.4 %collective-permute-start.4 = (f32[8,1152]{1,0:T(8,128)S(1)}, f32[8,1152]{1,0:T(8,128)S(1)}, u32[]{:S(2)}, u32[]{:S(2)}) collective-permute-start(f32[8,1152]{1,0:T(8,128)S(1)} %get-tuple-element.256), channel_id=1, source_target_pairs={{0,16},{8,24},{16,0},{24,8},{1,17},{9,25},{17,1},{25,9},{2,18},{10... | collective-permute-start | bytes 110600 | tf_op jit(solution)/shard_map/while/body/eval_jaxpr/ppermute | solution.py:133
  93.6 4.6 %collective-permute-start.5 = (f32[8,1152]{1,0:T(8,128)S(1)}, f32[8,1152]{1,0:T(8,128)S(1)}, u32[]{:S(2)}, u32[]{:S(2)}) collective-permute-start(f32[8,1152]{1,0:T(8,128)S(1)} %get-tuple-element.257), channel_id=1, source_target_pairs={{0,8},{8,16},{16,24},{24,0},{1,9},{9,17},{17,25},{25,1},{2,10},{10... | collective-permute-start | bytes 110600 | tf_op jit(solution)/shard_map/while/body/eval_jaxpr/ppermute | solution.py:133
  95.6 3.1 %collective-permute-start.6 = (f32[8,1152]{1,0:T(8,128)S(1)}, f32[8,1152]{1,0:T(8,128)S(1)}, u32[]{:S(2)}, u32[]{:S(2)}) collective-permute-start(f32[8,1152]{1,0:T(8,128)S(1)} %get-tuple-element.258), channel_id=1, source_target_pairs={{0,24},{8,0},{16,8},{24,16},{1,25},{9,1},{17,9},{25,17},{2,26},{10... | collective-permute-start | bytes 110600 | tf_op jit(solution)/shard_map/while/body/eval_jaxpr/ppermute | solution.py:133
  109.7 6.8 %collective-permute-start.7 = (f32[8,1152]{1,0:T(8,128)S(1)}, f32[8,1152]{1,0:T(8,128)S(1)}, u32[]{:S(2)}, u32[]{:S(2)}) collective-permute-start(f32[8,1152]{1,0:T(8,128)S(1)} %eval_jaxpr.9), channel_id=1, source_target_pairs={{0,16},{8,24},{16,0},{24,8},{1,17},{9,25},{17,1},{25,9},{2,18},{10... | collective-permute-start | bytes 110600 | tf_op jit(solution)/shard_map/while/body/eval_jaxpr/ppermute | solution.py:133
  110.1 8.0 %collective-permute-start.8 = (f32[8,1152]{1,0:T(8,128)S(1)}, f32[8,1152]{1,0:T(8,128)S(1)}, u32[]{:S(2)}, u32[]{:S(2)}) collective-permute-start(f32[8,1152]{1,0:T(8,128)S(1)} %eval_jaxpr.9), channel_id=1, source_target_pairs={{0,8},{8,16},{16,24},{24,0},{1,9},{9,17},{17,25},{25,1},{2,10},{10... | collective-permute-start | bytes 110600 | tf_op jit(solution)/shard_map/while/body/eval_jaxpr/ppermute | solution.py:133
  112.2 6.3 %collective-permute-start.9 = (f32[8,1152]{1,0:T(8,128)S(1)}, f32[8,1152]{1,0:T(8,128)S(1)}, u32[]{:S(2)}, u32[]{:S(2)}) collective-permute-start(f32[8,1152]{1,0:T(8,128)S(1)} %eval_jaxpr.9), channel_id=1, source_target_pairs={{0,24},{8,0},{16,8},{24,16},{1,25},{9,1},{17,9},{25,17},{2,26},{10... | collective-permute-start | bytes 110600 | tf_op jit(solution)/shard_map/while/body/eval_jaxpr/ppermute | solution.py:133
  112.8 6.7 %collective-permute-start.10 = (f32[8,1152]{1,0:T(8,128)S(1)}, f32[8,1152]{1,0:T(8,128)S(1)}, u32[]{:S(2)}, u32[]{:S(2)}) collective-permute-start(f32[8,1152]{1,0:T(8,128)S(1)} %eval_jaxpr.9), channel_id=1, source_target_pairs={{0,4},{4,0},{1,5},{5,1},{2,6},{6,2},{3,7},{7,3},{8,12},{12,8},{9,1... | collective-permute-start | bytes 110600 | tf_op jit(solution)/shard_map/while/body/eval_jaxpr/ppermute | solution.py:124
  116.5 3.0 %collective-permute-start.11 = (f32[8,1152]{1,0:T(8,128)S(1)}, f32[8,1152]{1,0:T(8,128)S(1)}, u32[]{:S(2)}, u32[]{:S(2)}) collective-permute-start(f32[8,1152]{1,0:T(8,128)S(1)} %collective-permute-done.7), channel_id=1, source_target_pairs={{0,4},{4,0},{1,5},{5,1},{2,6},{6,2},{3,7},{7,3},{8,12},{12,8},{9,1... | collective-permute-start | bytes 110600 | tf_op jit(solution)/shard_map/while/body/eval_jaxpr/ppermute | solution.py:124
  118.0 1.5 collective-permute-start.12
  118.4 1.9 %collective-permute-start.13 = (f32[8,1152]{1,0:T(8,128)S(1)}, f32[8,1152]{1,0:T(8,128)S(1)}, u32[]{:S(2)}, u32[]{:S(2)}) collective-permute-start(f32[8,1152]{1,0:T(8,128)S(1)} %collective-permute-done.9), channel_id=1, source_target_pairs={{0,4},{4,0},{1,5},{5,1},{2,6},{6,2},{3,7},{7,3},{8,12},{12,8},{9,1... | collective-permute-start | bytes 110600 | tf_op jit(solution)/shard_map/while/body/eval_jaxpr/ppermute | solution.py:124
  123.2 6.0 %collective-permute-start = (bf16[64,832]{1,0:T(8,128)(2,1)S(1)}, bf16[64,832]{1,0:T(8,128)(2,1)S(1)}, u32[]{:S(2)}, u32[]{:S(2)}) collective-permute-start(bf16[64,832]{1,0:T(8,128)(2,1)S(1)} %get-tuple-element.252), channel_id=1, source_target_pairs={{0,2},{1,3},{2,0},{3,1},{4,6},{5,7},{6,4},{7,5},{8,10},{9,11},{10,... | collective-permute-start | bytes 319496 | tf_op jit(solution)/shard_map/while/body/eval_jaxpr/ppermute | solution.py:128
  125.1 6.9 %collective-permute-start.1 = (bf16[64,832]{1,0:T(8,128)(2,1)S(1)}, bf16[64,832]{1,0:T(8,128)(2,1)S(1)}, u32[]{:S(2)}, u32[]{:S(2)}) collective-permute-start(bf16[64,832]{1,0:T(8,128)(2,1)S(1)} %get-tuple-element.252), channel_id=1, source_target_pairs={{0,1},{1,2},{2,3},{3,0},{4,5},{5,6},{6,7},{7,4},{8,9},{9,10},{10,1... | collective-permute-start | bytes 319496 | tf_op jit(solution)/shard_map/while/body/eval_jaxpr/ppermute | solution.py:128
  126.3 5.7 %collective-permute-start.2 = (bf16[64,832]{1,0:T(8,128)(2,1)S(1)}, bf16[64,832]{1,0:T(8,128)(2,1)S(1)}, u32[]{:S(2)}, u32[]{:S(2)}) collective-permute-start(bf16[64,832]{1,0:T(8,128)(2,1)S(1)} %get-tuple-element.252), channel_id=1, source_target_pairs={{0,3},{1,0},{2,1},{3,2},{4,7},{5,4},{6,5},{7,6},{8,11},{9,8},{10,9... | collective-permute-start | bytes 319496 | tf_op jit(solution)/shard_map/while/body/eval_jaxpr/ppermute | solution.py:128
  135.1 1.9 %collective-permute-start.3 = (f32[32,1152]{1,0:T(8,128)S(1)}, f32[32,1152]{1,0:T(8,128)S(1)}, u32[]{:S(2)}, u32[]{:S(2)}) collective-permute-start(f32[32,1152]{1,0:T(8,128)S(1)} %get-tuple-element.254), channel_id=1, source_target_pairs={{0,4},{4,0},{1,5},{5,1},{2,6},{6,2},{3,7},{7,3},{8,12},{12,8},{9,1... | collective-permute-start | bytes 442376 | tf_op jit(solution)/shard_map/while/body/eval_jaxpr/ppermute | solution.py:124
  137.0 4.4 %collective-permute-start.4 = (f32[8,1152]{1,0:T(8,128)S(1)}, f32[8,1152]{1,0:T(8,128)S(1)}, u32[]{:S(2)}, u32[]{:S(2)}) collective-permute-start(f32[8,1152]{1,0:T(8,128)S(1)} %get-tuple-element.256), channel_id=1, source_target_pairs={{0,16},{8,24},{16,0},{24,8},{1,17},{9,25},{17,1},{25,9},{2,18},{10... | collective-permute-start | bytes 110600 | tf_op jit(solution)/shard_map/while/body/eval_jaxpr/ppermute | solution.py:133
  138.0 4.5 %collective-permute-start.5 = (f32[8,1152]{1,0:T(8,128)S(1)}, f32[8,1152]{1,0:T(8,128)S(1)}, u32[]{:S(2)}, u32[]{:S(2)}) collective-permute-start(f32[8,1152]{1,0:T(8,128)S(1)} %get-tuple-element.257), channel_id=1, source_target_pairs={{0,8},{8,16},{16,24},{24,0},{1,9},{9,17},{17,25},{25,1},{2,10},{10... | collective-permute-start | bytes 110600 | tf_op jit(solution)/shard_map/while/body/eval_jaxpr/ppermute | solution.py:133
  139.6 3.1 %collective-permute-start.6 = (f32[8,1152]{1,0:T(8,128)S(1)}, f32[8,1152]{1,0:T(8,128)S(1)}, u32[]{:S(2)}, u32[]{:S(2)}) collective-permute-start(f32[8,1152]{1,0:T(8,128)S(1)} %get-tuple-element.258), channel_id=1, source_target_pairs={{0,24},{8,0},{16,8},{24,16},{1,25},{9,1},{17,9},{25,17},{2,26},{10... | collective-permute-start | bytes 110600 | tf_op jit(solution)/shard_map/while/body/eval_jaxpr/ppermute | solution.py:133
  153.6 7.8 %collective-permute-start.7 = (f32[8,1152]{1,0:T(8,128)S(1)}, f32[8,1152]{1,0:T(8,128)S(1)}, u32[]{:S(2)}, u32[]{:S(2)}) collective-permute-start(f32[8,1152]{1,0:T(8,128)S(1)} %eval_jaxpr.9), channel_id=1, source_target_pairs={{0,16},{8,24},{16,0},{24,8},{1,17},{9,25},{17,1},{25,9},{2,18},{10... | collective-permute-start | bytes 110600 | tf_op jit(solution)/shard_map/while/body/eval_jaxpr/ppermute | solution.py:133
  154.9 7.0 %collective-permute-start.8 = (f32[8,1152]{1,0:T(8,128)S(1)}, f32[8,1152]{1,0:T(8,128)S(1)}, u32[]{:S(2)}, u32[]{:S(2)}) collective-permute-start(f32[8,1152]{1,0:T(8,128)S(1)} %eval_jaxpr.9), channel_id=1, source_target_pairs={{0,8},{8,16},{16,24},{24,0},{1,9},{9,17},{17,25},{25,1},{2,10},{10... | collective-permute-start | bytes 110600 | tf_op jit(solution)/shard_map/while/body/eval_jaxpr/ppermute | solution.py:133
  156.2 7.1 %collective-permute-start.9 = (f32[8,1152]{1,0:T(8,128)S(1)}, f32[8,1152]{1,0:T(8,128)S(1)}, u32[]{:S(2)}, u32[]{:S(2)}) collective-permute-start(f32[8,1152]{1,0:T(8,128)S(1)} %eval_jaxpr.9), channel_id=1, source_target_pairs={{0,24},{8,0},{16,8},{24,16},{1,25},{9,1},{17,9},{25,17},{2,26},{10... | collective-permute-start | bytes 110600 | tf_op jit(solution)/shard_map/while/body/eval_jaxpr/ppermute | solution.py:133
  157.6 6.3 %collective-permute-start.10 = (f32[8,1152]{1,0:T(8,128)S(1)}, f32[8,1152]{1,0:T(8,128)S(1)}, u32[]{:S(2)}, u32[]{:S(2)}) collective-permute-start(f32[8,1152]{1,0:T(8,128)S(1)} %eval_jaxpr.9), channel_id=1, source_target_pairs={{0,4},{4,0},{1,5},{5,1},{2,6},{6,2},{3,7},{7,3},{8,12},{12,8},{9,1... | collective-permute-start | bytes 110600 | tf_op jit(solution)/shard_map/while/body/eval_jaxpr/ppermute | solution.py:124
  161.3 2.5 %collective-permute-start.11 = (f32[8,1152]{1,0:T(8,128)S(1)}, f32[8,1152]{1,0:T(8,128)S(1)}, u32[]{:S(2)}, u32[]{:S(2)}) collective-permute-start(f32[8,1152]{1,0:T(8,128)S(1)} %collective-permute-done.7), channel_id=1, source_target_pairs={{0,4},{4,0},{1,5},{5,1},{2,6},{6,2},{3,7},{7,3},{8,12},{12,8},{9,1... | collective-permute-start | bytes 110600 | tf_op jit(solution)/shard_map/while/body/eval_jaxpr/ppermute | solution.py:124
  161.9 2.2 %collective-permute-start.12 = (f32[8,1152]{1,0:T(8,128)S(1)}, f32[8,1152]{1,0:T(8,128)S(1)}, u32[]{:S(2)}, u32[]{:S(2)}) collective-permute-start(f32[8,1152]{1,0:T(8,128)S(1)} %collective-permute-done.8), channel_id=1, source_target_pairs={{0,4},{4,0},{1,5},{5,1},{2,6},{6,2},{3,7},{7,3},{8,12},{12,8},{9,1... | collective-permute-start | bytes 110600 | tf_op jit(solution)/shard_map/while/body/eval_jaxpr/ppermute | solution.py:124
  163.3 1.5 collective-permute-start.13
